TPU v7x, 32 devices: a whole 2x2x4 slice. The times are simulated.
32 devices in a mesh: tm: 2 (over x), height: 16 (over z, y, core).
Axes of the slice: x: 2, y: 2, z: 4, core: 2. Of those that a mesh axis runs over, the one named last changes fastest.
Arguments:
- pixels: bfloat16 [4, 3, 128, 1024], P('tm', None, 'height'), may hold values from -6 to 6
- conv_weight: bfloat16 [3, 3, 3, 48, 128], replicated, may hold values from -0.15625 to 0.15625
- conv_bias: float32 [128], replicated, may hold values from -3 to 3
- down_weight: bfloat16 [2, 2, 128, 256], replicated, may hold values from -0.25 to 0.25
- down_bias: float32 [256], replicated, may hold values from -3 to 3
- cotangent: bfloat16 [4, 16, 128, 256], P('tm', 'height'), may hold values from -6 to 6
Outputs:
- features: bfloat16 [4, 16, 128, 256], P('tm', 'height')
- grad_conv: float32 [3, 3, 3, 48, 128], replicated
- grad_conv_bias: float32 [128], replicated
- grad_down: float32 [2, 2, 128, 256], replicated
- grad_down_bias: float32 [256], replicated
- grad_pixels: float32 [4, 3, 128, 1024], P('tm', None, 'height')
All inputs are finite; a program needn't handle non-finite values.
Results may differ from a plain program's by a relative error of at most 0.012.
Values may be sent and summed in bfloat16 or wider, within the bound.
No kernel may reach another device: no remote copies, remote signals or barrier semaphores. Data moves between devices by JAX's collectives and lax.ppermute only.
A program may use at most 64 MiB of HBM per device.

v0:
```python
import math

import jax
import jax.numpy as jnp
import numpy as np
from jax import lax
from jax.sharding import PartitionSpec as P

haar_matrix = (
    np.kron(np.array([[1.0, 1.0], [1.0, -1.0]]), np.array([[1.0, 1.0], [1.0, -1.0]])) * 0.5
)


def extended_2(shard, sides, width):
    for axis, dim in sides:
        size, length = (lax.axis_size(axis), shard.shape[dim])
        up = [(i, (i + 1) % size) for i in range(size - 1)]
        down = [(j, i) for i, j in up]
        last = lax.slice_in_dim(shard, length - width, length, axis=dim)
        first = lax.slice_in_dim(shard, 0, width, axis=dim)
        before = lax.ppermute(last, axis, up)
        after = lax.ppermute(first, axis, down)
        shard = jnp.concatenate([before, shard, after], axis=dim)
    return shard


def passed_along(value, axis, steps):
    count = lax.axis_size(axis)
    first, last = (max(0, -steps), min(count, count - steps))
    return lax.ppermute(value, axis, [(source, source + steps) for source in range(first, last)])


def analyse(pixels):
    frame_count, colors, height_px, width_px = pixels.shape
    table = jnp.asarray(haar_matrix, jnp.float32)
    blocks = pixels.astype(jnp.float32).reshape(
        frame_count, colors, height_px // 4, 4, width_px // 4, 4
    )
    result = jnp.einsum("fkrucv,iu,jv->fkijrc", blocks, table, table)
    return result.reshape(frame_count, colors * 16, height_px // 4, width_px // 4)


def synthesise(dcoeffs):
    frame_count, channels, height_cells, width_cells = dcoeffs.shape
    table = jnp.asarray(haar_matrix, jnp.float32)
    parts = dcoeffs.reshape(frame_count, channels // 16, 4, 4, height_cells, width_cells)
    result = jnp.einsum("fkijrc,iu,jv->fkrucv", parts, table, table)
    return result.reshape(frame_count, channels // 16, height_cells * 4, width_cells * 4)


def all_taps():
    return [
        (tap_time, tap_row, tap_col)
        for tap_time in range(3)
        for tap_row in range(3)
        for tap_col in range(3)
    ]


def local(pixels, conv_weight, conv_bias, down_weight, down_bias, cotangent):
    frame_count = pixels.shape[0]
    height_cells = pixels.shape[2] // 4
    width_cells = pixels.shape[3] // 4
    channels = conv_weight.shape[3]
    outer = conv_weight.shape[4]
    coeffs = analyse(pixels).astype(jnp.bfloat16)
    tall = extended_2(coeffs, (("height", 2),), 1)
    earlier = passed_along(tall, "tm", 1)
    extended = jnp.pad(jnp.concatenate([earlier, tall], axis=0), ((0, 0), (0, 0), (0, 0), (1, 1)))
    pre = jnp.zeros((frame_count, height_cells, width_cells, outer), jnp.float32) + conv_bias
    for tap_time, tap_row, tap_col in all_taps():
        window = extended[
            tap_time : tap_time + frame_count,
            :,
            tap_row : tap_row + height_cells,
            tap_col : tap_col + width_cells,
        ]
        pre = pre + jnp.einsum(
            "fkrc,ko->frco",
            window,
            conv_weight[tap_time, tap_row, tap_col],
            preferred_element_type=jnp.float32,
        )
    act = jax.nn.silu(pre).astype(jnp.bfloat16)
    grouped = act.reshape(frame_count, height_cells // 2, 2, width_cells // 2, 2, outer)
    features = (
        jnp.einsum("fqupvk,uvko->fqpo", grouped, down_weight, preferred_element_type=jnp.float32)
        + down_bias
    ).astype(jnp.bfloat16)
    dact = jnp.einsum(
        "fqpo,uvko->fqupvk", cotangent, down_weight, preferred_element_type=jnp.float32
    )
    dact = dact.reshape(frame_count, height_cells, width_cells, outer)
    sig = jax.nn.sigmoid(pre)
    slope = (dact * sig * (1.0 + pre * (1.0 - sig))).astype(jnp.bfloat16)
    local_down = jnp.einsum(
        "fqupvk,fqpo->uvko", grouped, cotangent, preferred_element_type=jnp.float32
    )
    local_down_bias = jnp.sum(cotangent.astype(jnp.float32), axis=(0, 1, 2))
    pieces = []
    for tap_time, tap_row, tap_col in all_taps():
        window = extended[
            tap_time : tap_time + frame_count,
            :,
            tap_row : tap_row + height_cells,
            tap_col : tap_col + width_cells,
        ]
        pieces.append(
            jnp.einsum("fkrc,frco->ko", window, slope, preferred_element_type=jnp.float32)
        )
    local_conv = jnp.stack(pieces).reshape(3, 3, 3, channels, outer)
    local_conv_bias = jnp.sum(slope.astype(jnp.float32), axis=(0, 1, 2))
    summed = lax.psum((local_conv, local_conv_bias, local_down, local_down_bias), ("tm", "height"))
    count = frame_count * lax.axis_size("tm") * height_cells * lax.axis_size("height") * width_cells
    scale = 1.0 / math.sqrt(count)
    grad_conv = scale * summed[0]
    grad_conv_bias = scale * summed[1]
    grad_down = scale * summed[2]
    grad_down_bias = scale * summed[3]
    slope_tall = extended_2(slope, (("height", 1),), 1)
    following = passed_along(slope_tall, "tm", -1)
    later = jnp.pad(
        jnp.concatenate([slope_tall, following], axis=0), ((0, 0), (0, 0), (1, 1), (0, 0))
    )
    dcoeffs = jnp.zeros((frame_count, channels, height_cells, width_cells), jnp.float32)
    for tap_time, tap_row, tap_col in all_taps():
        window = later[
            2 - tap_time : 2 - tap_time + frame_count,
            2 - tap_row : 2 - tap_row + height_cells,
            2 - tap_col : 2 - tap_col + width_cells,
        ]
        dcoeffs = dcoeffs + jnp.einsum(
            "frco,ko->fkrc",
            window,
            conv_weight[tap_time, tap_row, tap_col],
            preferred_element_type=jnp.float32,
        )
    grad_pixels = synthesise(dcoeffs)
    return (features, grad_conv, grad_conv_bias, grad_down, grad_down_bias, grad_pixels)


def solution(mesh):
    return jax.shard_map(
        local,
        mesh=mesh,
        in_specs=(P("tm", None, "height", None), P(), P(), P(), P(), P("tm", "height", None, None)),
        out_specs=(
            P("tm", "height", None, None),
            P(),
            P(),
            P(),
            P(),
            P("tm", None, "height", None),
        ),
        check_vma=False,
    )
```

profile of v0, /device:TPU:0, one launch (start us, length us, event | category | flops | bytes accessed | tf_op | source)
XLA Modules:
  0.0 221.6 jit_solution(14600014938950224252)
XLA Ops:
  7.2 8.5 %reshape.49 = bf16[2,3,2,4,256,4]{5,4,3,2,1,0:T(8,128)(2,1)} reshape(bf16[2,3,8,1024]{3,2,1,0:T(8,128)(2,1)} %param.8) | data formatting | bytes 196608 | tf_op jit(solution)/shard_map/reshape | solution.py:36
  15.7 3.3 %copy.34 = bf16[2,3,2,4,256,4]{4,3,5,2,1,0:T(4,128)(2,1)S(1)} copy(bf16[2,3,2,4,256,4]{5,4,3,2,1,0:T(8,128)(2,1)} %reshape.49) | data formatting | bytes 196608 | tf_op jit(solution)/shard_map/reshape | solution.py:36
  19.7 2.4 %collective-permute-start = (bf16[2,48,1,256]{3,1,2,0:T(8,128)(2,1)S(1)}, bf16[2,48,1,256]{3,1,2,0:T(8,128)(2,1)S(1)}, u32[]{:S(2)}, u32[]{:S(2)}) collective-permute-start(bf16[2,48,1,256]{3,1,2,0:T(8,128)(2,1)S(1)} %copy.115), channel_id=1, source_target_pairs={{0,1},{1,2},{2,3},{3,4},{4,5},{5,6},{6,7},{7,8},{8,9},{9,10},{10,1... | collective-permute-start | bytes 147464 | tf_op jit(solution)/shard_map/ppermute | solution.py:21
  22.1 1.3 collective-permute-start.1
  23.5 3.9 %collective-permute-done.1 = bf16[2,48,1,256]{3,1,2,0:T(8,128)(2,1)S(1)} collective-permute-done((bf16[2,48,1,256]{3,1,2,0:T(8,128)(2,1)S(1)}, bf16[2,48,1,256]{3,1,2,0:T(8,128)(2,1)S(1)}, u32[]{:S(2)}, u32[]{:S(2)}) %collective-permute-start.1) | collective-permute-done | bytes 49184 | tf_op jit(solution)/shard_map/ppermute | solution.py:22
  27.4 3.4 %collective-permute-start.2 = (bf16[2,48,4,256]{3,1,2,0:T(8,128)(2,1)S(1)}, bf16[2,48,4,256]{3,1,2,0:T(8,128)(2,1)S(1)}, u32[]{:S(2)}, u32[]{:S(2)}) collective-permute-start(bf16[2,48,4,256]{3,1,2,0:T(8,128)(2,1)S(1)} %get-tuple-element.33), channel_id=1, source_target_pairs={{0,16},{1,17},{2,18},{3,19},{4,20},{5,21},{6,22},{7,23},{8,24},{9,... | collective-permute-start | bytes 589832 | tf_op jit(solution)/shard_map/ppermute | solution.py:30
  31.1 0.4 copy.27
  31.5 2.7 %collective-permute-done.2 = bf16[2,48,4,256]{3,1,2,0:T(8,128)(2,1)S(1)} collective-permute-done((bf16[2,48,4,256]{3,1,2,0:T(8,128)(2,1)S(1)}, bf16[2,48,4,256]{3,1,2,0:T(8,128)(2,1)S(1)}, u32[]{:S(2)}, u32[]{:S(2)}) %collective-permute-start.2) | collective-permute-done | bytes 196640 | tf_op jit(solution)/shard_map/ppermute | solution.py:30
  42.0 0.3 convolution_add_fusion.9
  42.4 0.3 convolution_add_fusion.8
  42.7 0.5 convert_reduce_fusion
  43.7 3.8 %collective-permute-start.3 = (bf16[2,1,256,128]{3,2,1,0:T(8,128)(2,1)S(1)}, bf16[2,1,256,128]{3,2,1,0:T(8,128)(2,1)S(1)}, u32[]{:S(2)}, u32[]{:S(2)}) collective-permute-start(bf16[2,1,256,128]{3,2,1,0:T(8,128)(2,1)S(1)} %get-tuple-element.25), channel_id=1, source_target_pairs={{0,1},{1,2},{2,3},{3,4},{4,5},{5,6},{6,7},{7,8},{8,9},{9,10},{10,1... | collective-permute-start | bytes 393224 | tf_op jit(solution)/shard_map/ppermute | solution.py:21
  47.5 1.3 collective-permute-start.4
  54.4 1.1 convolution_bitcast_fusion
  55.5 45.2 %all-reduce.2 = (f32[128]{0:T(128)S(1)}, f32[256]{0:T(256)S(1)}) all-reduce(f32[128]{0:T(128)S(1)} %get-tuple-element.22, f32[256]{0:T(256)S(1)} %convert_reduce_fusion.1), channel_id=1, replica_groups=mesh['tm'=2,'height'=16] {'tm','height'}, use_global_device_ids=true, to_apply=%region_2.3 | all-reduce | flops 384 | bytes 3072 | tf_op jit(solution)/shard_map/psum | solution.py:113
  100.7 0.6 broadcast_multiply_fusion.2
  101.3 0.5 broadcast_multiply_fusion.3
  101.9 1.5 collective-permute-start.5
  103.3 0.9 fusion.36
  104.2 89.1 %all-reduce.6.cloned.1.call-done = (f32[3,3,3,48,128]{4,3,2,1,0:T(8,128)}, f32[2,2,128,256]{3,2,1,0:T(8,128)}) async-done(((f32[3,3,3,48,128]{4,3,2,1,0:T(8,128)}, f32[2,2,128,256]{3,2,1,0:T(8,128)}), (f32[3,3,3,48,128]{4,3,2,1,0:T(8,128)}, f32[2,2,128,256]{3,2,1,0:T(8,128)})) %all-reduce.6.cloned.1.call-update) | async-done | bytes 1187856 | tf_op jit(solution)/shard_map/psum | solution.py:113
  193.3 1.9 broadcast_multiply_fusion.1
  195.2 2.0 broadcast_multiply_fusion
  203.5 4.0 %copy.31 = f32[2,3,2,4,256,4]{5,4,3,2,1,0:T(8,128)} copy(f32[2,3,2,4,256,4]{4,5,2,1,0,3:T(4,128)S(1)} %convolution_bitcast_fusion.5) | data formatting | bytes 393216 | tf_op jit(solution)/shard_map/fkijrc,iu,jv->fkrucv/transpose | solution.py:47
  207.5 7.3 %reshape.55 = f32[2,3,8,1024]{3,2,1,0:T(8,128)} reshape(f32[2,3,2,4,256,4]{5,4,3,2,1,0:T(8,128)} %copy.31) | data formatting | bytes 393216 | tf_op jit(solution)/shard_map/reshape | solution.py:48
  (116 shorter events, 20.5 us)
Async XLA Ops:
  7.2 23.6 %copy-start = (bf16[2,2,128,256]{3,2,1,0:T(8,128)(2,1)S(1)}, bf16[2,2,128,256]{3,2,1,0:T(8,128)(2,1)}, u32[]{:S(2)}) copy-start(bf16[2,2,128,256]{3,2,1,0:T(8,128)(2,1)} %param.11) | copy-start | bytes 786436
  7.2 186.2 %all-reduce.6.cloned.1.call-start = ((), (), s32[]{:S(2)}) async-start(), calls=%async_computation | async-start | bytes 2375680 | tf_op jit(solution)/shard_map/psum | solution.py:113
  15.7 3.3 %copy-start.4 = (bf16[4,4,1,1,1,1]{1,0,5,4,3,2:T(4,128)(2,1)S(1)}, bf16[4,4,1,1,1,1]{1,0,5,4,3,2:T(4,128)(2,1)}, u32[]{:S(2)}) copy-start(bf16[4,4,1,1,1,1]{1,0,5,4,3,2:T(4,128)(2,1)} %constant.321) | copy-start | bytes 100
  15.7 15.0 %copy-start.1 = (bf16[2,1,128,256]{3,2,1,0:T(8,128)(2,1)S(1)}, bf16[2,1,128,256]{3,2,1,0:T(8,128)(2,1)}, u32[]{:S(2)}) copy-start(bf16[2,1,128,256]{3,2,1,0:T(8,128)(2,1)} %param.13) | copy-start | bytes 393220
  19.5 14.8 %copy-start.2 = (bf16[3,3,3,48,128]{4,3,2,1,0:T(8,128)(2,1)S(1)}, bf16[3,3,3,48,128]{4,3,2,1,0:T(8,128)(2,1)}, u32[]{:S(2)}) copy-start(bf16[3,3,3,48,128]{4,3,2,1,0:T(8,128)(2,1)} %param.9) | copy-start | bytes 995332
  19.7 3.7 %collective-permute-start = (bf16[2,48,1,256]{3,1,2,0:T(8,128)(2,1)S(1)}, bf16[2,48,1,256]{3,1,2,0:T(8,128)(2,1)S(1)}, u32[]{:S(2)}, u32[]{:S(2)}) collective-permute-start(bf16[2,48,1,256]{3,1,2,0:T(8,128)(2,1)S(1)} %copy.115), channel_id=1, source_target_pairs={{0,1},{1,2},{2,3},{3,4},{4,5},{5,6},{6,7},{7,8},{8,9},{9,10},{10,1... | collective-permute-start | bytes 147464 | tf_op jit(solution)/shard_map/ppermute | solution.py:21
  22.1 5.2 %collective-permute-start.1 = (bf16[2,48,1,256]{3,1,2,0:T(8,128)(2,1)S(1)}, bf16[2,48,1,256]{3,1,2,0:T(8,128)(2,1)S(1)}, u32[]{:S(2)}, u32[]{:S(2)}) collective-permute-start(bf16[2,48,1,256]{3,1,2,0:T(8,128)(2,1)S(1)} %copy.116), channel_id=1, source_target_pairs={{1,0},{2,1},{3,2},{4,3},{5,4},{6,5},{7,6},{8,7},{9,8},{10,9},{11,1... | collective-permute-start | bytes 147464 | tf_op jit(solution)/shard_map/ppermute | solution.py:22
  27.4 6.9 %collective-permute-start.2 = (bf16[2,48,4,256]{3,1,2,0:T(8,128)(2,1)S(1)}, bf16[2,48,4,256]{3,1,2,0:T(8,128)(2,1)S(1)}, u32[]{:S(2)}, u32[]{:S(2)}) collective-permute-start(bf16[2,48,4,256]{3,1,2,0:T(8,128)(2,1)S(1)} %get-tuple-element.33), channel_id=1, source_target_pairs={{0,16},{1,17},{2,18},{3,19},{4,20},{5,21},{6,22},{7,23},{8,24},{9,... | collective-permute-start | bytes 589832 | tf_op jit(solution)/shard_map/ppermute | solution.py:30
  37.8 1.8 copy-start.5
  43.7 58.1 %collective-permute-start.3 = (bf16[2,1,256,128]{3,2,1,0:T(8,128)(2,1)S(1)}, bf16[2,1,256,128]{3,2,1,0:T(8,128)(2,1)S(1)}, u32[]{:S(2)}, u32[]{:S(2)}) collective-permute-start(bf16[2,1,256,128]{3,2,1,0:T(8,128)(2,1)S(1)} %get-tuple-element.25), channel_id=1, source_target_pairs={{0,1},{1,2},{2,3},{3,4},{4,5},{5,6},{6,7},{7,8},{8,9},{9,10},{10,1... | collective-permute-start | bytes 393224 | tf_op jit(solution)/shard_map/ppermute | solution.py:21
  47.5 54.3 %collective-permute-start.4 = (bf16[2,1,256,128]{3,2,1,0:T(8,128)(2,1)S(1)}, bf16[2,1,256,128]{3,2,1,0:T(8,128)(2,1)S(1)}, u32[]{:S(2)}, u32[]{:S(2)}) collective-permute-start(bf16[2,1,256,128]{3,2,1,0:T(8,128)(2,1)S(1)} %get-tuple-element.26), channel_id=1, source_target_pairs={{1,0},{2,1},{3,2},{4,3},{5,4},{6,5},{7,6},{8,7},{9,8},{10,9},{11,1... | collective-permute-start | bytes 393224 | tf_op jit(solution)/shard_map/ppermute | solution.py:22
  54.0 49.3 %copy-start.6 = (f32[256]{0:T(256)S(1)}, f32[256]{0:T(256)}, u32[]{:S(2)}) copy-start(f32[256]{0:T(256)} %param.12) | copy-start | bytes 3076
  54.4 1.1 copy-start.3
  101.9 95.4 %collective-permute-start.5 = (bf16[2,4,256,128]{3,2,1,0:T(8,128)(2,1)S(1)}, bf16[2,4,256,128]{3,2,1,0:T(8,128)(2,1)S(1)}, u32[]{:S(2)}, u32[]{:S(2)}) collective-permute-start(bf16[2,4,256,128]{3,2,1,0:T(8,128)(2,1)S(1)} %pad_maximum_fusion.1), channel_id=1, source_target_pairs={{16,0},{17,1},{18,2},{19,3},{20,4},{21,5},{22,6},{23,7},{24,8},{25... | collective-permute-start | bytes 1572872 | tf_op jit(solution)/shard_map/ppermute | solution.py:30
Sparse Core Ops, SparseCore 0:
  55.6 137.6 all-reduce.5
where the time goes:
time: 222 us
  waiting for transfers between devices  95.7 us (43%)
  blocking collectives  45.2 us (20%)
  local copies, waits for them, and re-layouts  23.8 us (11%)
  matrix products  23 us (10%)
  between operations  14.9 us (7%)
  starting transfers between devices  13.7 us (6%)
  other arithmetic  5.21 us (2%)
    psum x1, waiting for transfers between devices, local(): lax.psum((local_conv, local_conv_bias, local_down, local_down_bias), ('tm...  89.1 us
    psum x1, blocking collectives, local(): lax.psum((local_conv, local_conv_bias, local_down, local_down_bias), ('tm...  45.2 us
    reshape x2, local copies, waits for them, and re-layouts, analyse(): pixels.astype(jnp.float32)  11.8 us
    dot_general x27, matrix products, local(): jnp.einsum('fkrc,ko->frco', window, conv_weight[tap_time, tap_row, tap_co...  8.72 us
    reshape x1, local copies, waits for them, and re-layouts, synthesise(): result.reshape(frame_count, channels // 16, height_cells * 4, width_cells...  7.26 us
    ppermute x2, starting transfers between devices, extended_2(): before = lax.ppermute(last, axis, up)  6.24 us
    dot_general x27, matrix products, local(): jnp.einsum('fkrc,frco->ko', window, slope, preferred_element_type=jnp.flo...  5.61 us
    dot_general x27, matrix products, local(): jnp.einsum('frco,ko->fkrc', window, conv_weight[tap_time, tap_row, tap_co...  5.55 us
  transfers between devices with their start and end apart: 7, of which 3 were waited for; matrix products, arithmetic and copies ran while one was open for 6% of the time, Pallas kernels for 0%

commit v1 on v0

v1 whole, which is shorter than its diff:
```python
import functools
import math

import jax
import jax.numpy as jnp
import numpy as np
from jax import lax
from jax.experimental import pallas as pl
from jax.experimental.pallas import tpu as pltpu
from jax.sharding import Mesh, PartitionSpec as P

BF16, F32 = jnp.bfloat16, jnp.float32
HAAR = np.kron(np.array([[1.0, 1.0], [1.0, -1.0]]), np.array([[1.0, 1.0], [1.0, -1.0]])) * 0.5
VMEM = pl.BlockSpec(memory_space=pltpu.VMEM)
SMEM = pl.BlockSpec(memory_space=pltpu.SMEM)
NN = (((1,), (0,)), ((), ()))
NT = (((1,), (1,)), ((), ()))
SLOT = 16


def mm(a, b, dims=NN):
    return lax.dot_general(a, b, dims, preferred_element_type=F32)


def split(x):
    high = x.astype(BF16)
    return high, (x - high.astype(F32)).astype(BF16)


def column_table(width_cells):
    half = width_cells // 2
    table = np.zeros((4 * width_cells, 4, 2, half), np.float32)
    for parity in range(2):
        for pair in range(half):
            for v in range(4):
                table[8 * pair + 4 * parity + v, :, parity, pair] = HAAR[:, v]
    return table.reshape(4 * width_cells, 4 * width_cells)


def row_table(frames, colors, rows):
    table = np.zeros((frames, rows, SLOT, frames, colors, rows, 4), np.float32)
    for f in range(frames):
        for r in range(rows):
            for k in range(colors):
                table[f, r, 4 * k : 4 * k + 4, f, k, r, :] = HAAR
    return table.reshape(frames * rows * SLOT, frames * colors * rows * 4)


def channel_table(channels):
    table = np.zeros((4 * SLOT, channels), np.float32)
    for channel in range(channels):
        k, i, j = channel // 16, channel // 4 % 4, channel % 4
        table[SLOT * j + 4 * k + i, channel] = 1.0
    return table


def weights_kernel(weight, order, forward, backward, turned):
    slots = 4 * SLOT
    for a in range(3):
        for b in range(3):
            for d in range(3):
                tap = mm(order[...], weight[9 * a + 3 * b + d])
                backward[slots * (3 * a + b) : slots * (3 * a + b + 1), 128 * d : 128 * (d + 1)] = (
                    tap.astype(BF16)
                )
                at = slots * (3 * b + d)
                turned[at : at + slots, :] = tap
        forward[a] = turned[...].T.astype(BF16)


def main_kernel(
    dims,
    place,
    own,
    earlier,
    inner,
    outer,
    table,
    rows_own,
    rows_halo,
    order_back,
    forward,
    backward,
    conv_bias,
    down_weight,
    down_bias,
    cotangent,
    features,
    keep,
    give,
    pixels_own,
    pixels_early,
    send_inner,
    send_outer,
    x,
    acts,
    packed,
    spread,
):
    frames, rows, colors, pair, channels = dims
    slots = 4 * SLOT
    core, plane = place[0], place[1]
    inner_row = jnp.where(core == 0, rows + 1, 0)
    outer_row = jnp.where(core == 0, 0, rows + 1)
    lane = lax.broadcasted_iota(jnp.int32, (1, pair), 1)

    def left(value):
        return jnp.where(lane == pair - 1, 0.0, pltpu.roll(value, pair - 1, 1))

    def right(value):
        return jnp.where(lane == 0, 0.0, pltpu.roll(value, 1, 1))

    def fill(pixels, rows_table, where):
        columns = mm(pixels[...], table[...])
        high, low = split(columns)
        cells = mm(rows_table[...], high) + mm(rows_table[...], low)
        for j in range(4):
            even = cells[:, 2 * j * pair : (2 * j + 1) * pair]
            odd = cells[:, (2 * j + 1) * pair : (2 * j + 2) * pair]
            even, odd = even.astype(BF16).astype(F32), odd.astype(BF16).astype(F32)
            for d, (one, two) in enumerate(((right(odd), even), (even, odd), (odd, left(even)))):
                one, two = one.astype(BF16), two.astype(BF16)
                at = slots * d + SLOT * j
                for block, (f, r) in enumerate(where):
                    take = slice(SLOT * block, SLOT * (block + 1))
                    x[f, r, at : at + SLOT, :pair] = one[take]
                    x[f, r, at : at + SLOT, pair:] = two[take]

    fill(earlier, rows_own, [(f, 1 + r) for f in range(2) for r in range(rows)])
    fill(own, rows_own, [(2 + f, 1 + r) for f in range(frames) for r in range(rows)])
    fill(inner, rows_halo, [(f, inner_row) for f in range(frames + 2)])
    fill(outer, rows_halo, [(f, outer_row) for f in range(frames + 2)])

    bias = jnp.broadcast_to(conv_bias[...], (128, 128)).T
    bias = jnp.concatenate([bias] * (2 * pair // 128), axis=1)

    def window(f, r):
        return x[f, r : r + 3].reshape(3 * 3 * slots, 2 * pair)

    spread[...] = jnp.zeros_like(spread)
    down_total = None
    conv_total = [None] * 3
    ones = jnp.ones((8, 2 * pair), BF16)
    slope_total = None
    cot_total = None
    for f in range(frames):
        for q in range(rows // 2):
            cot = cotangent[f, q]
            dact = mm(down_weight[...], cot, NT)
            for u in range(2):
                r = 2 * q + u
                pre = bias
                for a in range(3):
                    pre = pre + mm(forward[a], window(f + a, r))
                sig = jax.nn.sigmoid(pre)
                act = pre * sig
                acts[(2 * u) * 128 : (2 * u + 1) * 128] = act[:, :pair].astype(BF16)
                acts[(2 * u + 1) * 128 : (2 * u + 2) * 128] = act[:, pair:].astype(BF16)
                here = jnp.concatenate(
                    [
                        dact[2 * u * 128 : (2 * u + 1) * 128],
                        dact[(2 * u + 1) * 128 : (2 * u + 2) * 128],
                    ],
                    axis=1,
                )
                slope = here * sig * (1.0 + pre * (1.0 - sig))
                slope16 = slope.astype(BF16)
                even, odd = slope16[:, :pair].astype(F32), slope16[:, pair:].astype(F32)
                for a in range(3):
                    part = mm(window(f + a, r), slope16, NT)
                    conv_total[a] = part if conv_total[a] is None else conv_total[a] + part
                part = mm(ones, slope16, NT)
                slope_total = part if slope_total is None else slope_total + part
                shifted = jnp.concatenate(
                    [
                        jnp.concatenate([odd, left(even)], axis=1).astype(BF16),
                        slope16,
                        jnp.concatenate([right(odd), even], axis=1).astype(BF16),
                    ],
                    axis=0,
                )
                reach = mm(backward[...], shifted)
                for a in range(3):
                    for b in range(3):
                        at = slots * (3 * a + b)
                        spread[f + a, r + b] += reach[at : at + slots]
            part = mm(acts[...], cot)
            down_total = part if down_total is None else down_total + part
            part = mm(ones[:, :pair], cot)
            cot_total = part if cot_total is None else cot_total + part
            turned = jnp.concatenate(
                [acts[128 * n : 128 * (n + 1)].astype(F32).T.astype(BF16) for n in range(4)], axis=1
            )
            features[f, q] = (mm(turned, down_weight[...]) + down_bias[...]).astype(BF16)

    flat = packed
    at = 0
    for a in range(3):
        for t in range(9):
            part = conv_total[a][slots * t : slots * (t + 1)]
            high, low = split(part)
            flat[at : at + channels] = mm(order_back[...], high) + mm(order_back[...], low)
            at += channels
    for half in range(2):
        flat[at : at + 512] = down_total[:, 128 * half : 128 * (half + 1)]
        at += 512
    sums = [slope_total[0:1], cot_total[0:1, :128], cot_total[0:1, 128:]]
    highs = [value.astype(BF16).astype(F32) for value in sums]
    lows = [value - high for value, high in zip(sums, highs)]
    flat[at : at + 8] = jnp.concatenate(highs + lows + [jnp.zeros((2, 128), F32)], axis=0)
    at += 8
    if at < packed.shape[0]:
        flat[at:] = jnp.zeros((packed.shape[0] - at, 128), F32)
    chunk = keep.shape[1]
    for m in range(4):
        slot = jnp.bitwise_xor(plane, m)
        keep[m] = flat[pl.ds(pl.multiple_of((4 * core + slot) * chunk, 8), chunk)]
        give[m] = flat[pl.ds(pl.multiple_of((4 * (1 - core) + slot) * chunk, 8), chunk)].astype(BF16)

    def synthesise(blocks, rows_table):
        cells = jnp.concatenate(
            [
                jnp.concatenate([spread[f, r, SLOT * j : SLOT * (j + 1)] for j in range(4)], axis=1)
                for f, r in blocks
            ],
            axis=0,
        ).astype(BF16)
        high, low = split(mm(cells, table[...], NT))
        back = (((0,), (0,)), ((), ()))
        return mm(rows_table[...], high, back) + mm(rows_table[...], low, back)

    pixels_early[...] = synthesise([(f, 1 + r) for f in range(2) for r in range(rows)], rows_own)
    pixels_own[...] = synthesise(
        [(2 + f, 1 + r) for f in range(frames) for r in range(rows)], rows_own
    )
    send_inner[...] = synthesise([(f, inner_row) for f in range(frames + 2)], rows_halo).astype(BF16)
    send_outer[...] = synthesise([(f, outer_row) for f in range(frames + 2)], rows_halo).astype(BF16)


def finish_kernel(scale, channels, place, mine, others, theirs, conv, conv_bias, down, down_bias, flat):
    core, plane = place[0], place[1]
    chunk = mine.shape[0]
    for m in range(4):
        slot = jnp.bitwise_xor(plane, m)
        value = mine[...] if m == 0 else others[m - 1]
        flat[pl.ds(pl.multiple_of((4 * core + slot) * chunk, 8), chunk)] = value.astype(F32) * scale
        flat[pl.ds(pl.multiple_of((4 * (1 - core) + slot) * chunk, 8), chunk)] = (
            theirs[m].astype(F32) * scale
        )
    at = 0
    for t in range(27):
        conv[t] = flat[at : at + channels]
        at += channels
    for half in range(2):
        down[:, 128 * half : 128 * (half + 1)] = flat[at : at + 512]
        at += 512
    sums = flat[at : at + 8]
    sums = sums[0:3] + sums[3:6]
    conv_bias[...] = sums[0:1]
    down_bias[:, :128] = sums[1:2]
    down_bias[:, 128:] = sums[2:3]


def local(axes, pixels, conv_weight, conv_bias, down_weight, down_bias, cotangent):
    times, heights = axes["tm"], axes["height"]
    frames, colors, pixel_rows, pixel_columns = pixels.shape
    rows, columns = pixel_rows // 4, pixel_columns // 4
    pair = columns // 2
    channels, width = conv_weight.shape[3:]
    width2 = down_weight.shape[3]
    core = lax.axis_index("core")
    plane = 2 * lax.axis_index("tm_lo") + lax.axis_index("y")
    place = jnp.stack([core, plane]).astype(jnp.int32)
    count_tm, count_height = lax.axis_size(times), lax.axis_size(heights)
    slots = 4 * SLOT

    def along_tm(value, step):
        pairs = [(i, i + step) for i in range(count_tm) if 0 <= i + step < count_tm]
        return lax.ppermute(value, times, pairs)

    def swap_inner(value):
        return lax.ppermute(value, "core", [(0, 1), (1, 0)])

    def swap_outer(value):
        pairs = [(i, i + 1) for i in range(1, count_height - 1, 2)]
        return lax.ppermute(value, heights, pairs + [(j, i) for i, j in pairs])

    def exchange(value, axes, mask):
        size = lax.axis_size(axes)
        return lax.ppermute(value, axes, [(i, i ^ mask) for i in range(size)])

    order = channel_table(channels)
    forward, backward = pl.pallas_call(
        weights_kernel,
        out_shape=(
            jax.ShapeDtypeStruct((3, width, 9 * slots), BF16),
            jax.ShapeDtypeStruct((9 * slots, 3 * width), BF16),
        ),
        in_specs=[VMEM, VMEM],
        out_specs=(VMEM, VMEM),
        scratch_shapes=[pltpu.VMEM((9 * slots, width), F32)],
        name="weights",
    )(conv_weight.reshape(27, channels, width), jnp.asarray(order, BF16))

    own = pixels.reshape(frames * colors * pixel_rows, pixel_columns)
    recent = pixels[frames - 2 :].reshape(2 * colors * pixel_rows, pixel_columns)
    earlier = along_tm(recent, 1)
    tall = jnp.concatenate([earlier, own], axis=0)
    tall = tall.reshape((frames + 2) * colors, pixel_rows, pixel_columns)
    top, bottom = tall[:, :4], tall[:, pixel_rows - 4 :]
    flat_halo = ((frames + 2) * colors * 4, pixel_columns)
    inner = swap_inner(jnp.where(core == 0, bottom, top).reshape(flat_halo))
    outer = swap_outer(jnp.where(core == 0, top, bottom).reshape(flat_halo))

    data_rows = 27 * channels + 4 * width * width2 // 128 + 8
    chunk = -(-data_rows // 64) * 8
    features, keep, give, pixels_own, pixels_early, send_inner, send_outer = pl.pallas_call(
        functools.partial(main_kernel, (frames, rows, colors, pair, channels)),
        out_shape=(
            jax.ShapeDtypeStruct((frames, rows // 2, pair, width2), BF16),
            jax.ShapeDtypeStruct((4, chunk, 128), F32),
            jax.ShapeDtypeStruct((4, chunk, 128), BF16),
            jax.ShapeDtypeStruct(own.shape, F32),
            jax.ShapeDtypeStruct(recent.shape, F32),
            jax.ShapeDtypeStruct(flat_halo, BF16),
            jax.ShapeDtypeStruct(flat_halo, BF16),
        ),
        in_specs=[SMEM] + [VMEM] * 14,
        out_specs=(VMEM,) * 7,
        scratch_shapes=[
            pltpu.VMEM((frames + 2, rows + 2, 3 * slots, columns), BF16),
            pltpu.VMEM((4 * width, pair), BF16),
            pltpu.VMEM((8 * chunk, 128), F32),
            pltpu.VMEM((frames + 2, rows + 2, slots, columns), F32),
        ],
        name="main",
    )(
        place,
        own,
        earlier,
        inner,
        outer,
        jnp.asarray(column_table(columns), BF16),
        jnp.asarray(row_table(frames, colors, rows), BF16),
        jnp.asarray(row_table(frames + 2, colors, 1), BF16),
        jnp.asarray(order.T, BF16),
        forward,
        backward,
        conv_bias.reshape(1, width),
        down_weight.reshape(4 * width, width2),
        down_bias.reshape(1, width2),
        cotangent,
    )

    total = keep + swap_inner(give).astype(F32)
    planes = ("tm_lo", "y")
    parts = [exchange(total[m].astype(BF16), planes, m) for m in (1, 2, 3)]
    mine = total[0] + sum(part.astype(F32) for part in parts)
    for axis in axes["rest"]:
        sent = mine.astype(BF16)
        parts = [exchange(sent, axis, m) for m in range(1, lax.axis_size(axis))]
        mine = mine + sum(part.astype(F32) for part in parts)
    mine = mine.astype(BF16)
    others = jnp.stack([exchange(mine, planes, m) for m in (1, 2, 3)])
    theirs = swap_inner(jnp.concatenate([mine[None], others]))
    count = frames * count_tm * rows * count_height * columns
    grad_conv, grad_conv_bias, grad_down, grad_down_bias = pl.pallas_call(
        functools.partial(finish_kernel, 1.0 / math.sqrt(count), channels),
        out_shape=(
            jax.ShapeDtypeStruct((27, channels, width), F32),
            jax.ShapeDtypeStruct((1, width), F32),
            jax.ShapeDtypeStruct((4 * width, width2), F32),
            jax.ShapeDtypeStruct((1, width2), F32),
        ),
        in_specs=[SMEM, VMEM, VMEM, VMEM],
        out_specs=(VMEM,) * 4,
        scratch_shapes=[pltpu.VMEM((8 * chunk, 128), F32)],
        name="finish",
    )(place, mine, others, theirs)

    from_inner = swap_inner(send_inner).reshape((frames + 2) * colors, 4, pixel_columns)
    from_outer = swap_outer(send_outer).reshape((frames + 2) * colors, 4, pixel_columns)
    above = jnp.where(core == 0, from_outer, from_inner).astype(F32)
    below = jnp.where(core == 0, from_inner, from_outer).astype(F32)
    gap = pixel_rows - 4
    halo = jnp.pad(above, ((0, 0), (0, gap), (0, 0))) + jnp.pad(below, ((0, 0), (gap, 0), (0, 0)))
    early = pixels_early.reshape(2 * colors, pixel_rows, pixel_columns) + halo[: 2 * colors]
    late = pixels_own.reshape(frames * colors, pixel_rows, pixel_columns) + halo[2 * colors :]
    following = along_tm(early.astype(BF16), -1).astype(F32)
    skipped = jnp.zeros(((frames - 2) * colors, pixel_rows, pixel_columns), F32)
    grad_pixels = late + jnp.concatenate([skipped, following], axis=0)
    return (
        features,
        grad_conv.reshape(conv_weight.shape),
        grad_conv_bias.reshape(width),
        grad_down.reshape(down_weight.shape),
        grad_down_bias.reshape(width2),
        grad_pixels.reshape(pixels.shape),
    )


def factors(size):
    parts = []
    while size > 1:
        part = 4 if size % 4 == 0 else 2
        assert size % part == 0
        parts.append(part)
        size //= part
    return parts


def solution(mesh):
    count_tm, count_height = mesh.shape["tm"], mesh.shape["height"]
    tm_parts, height_parts = factors(count_tm // 2), factors(count_height // 4)
    tm_names = tuple(f"tm_{n}" for n in range(len(tm_parts)))
    height_names = tuple(f"z_{n}" for n in range(len(height_parts)))
    axes = {
        "tm": tm_names + ("tm_lo",),
        "height": height_names + ("y", "core"),
        "rest": tm_names + height_names,
    }
    fine = Mesh(
        mesh.devices.reshape(tm_parts + [2] + height_parts + [2, 2]), axes["tm"] + axes["height"]
    )
    tm, height = axes["tm"], axes["height"]
    return jax.shard_map(
        functools.partial(local, axes),
        mesh=fine,
        in_specs=(P(tm, None, height, None), P(), P(), P(), P(), P(tm, height, None, None)),
        out_specs=(
            P(tm, height, None, None),
            P(),
            P(),
            P(),
            P(),
            P(tm, None, height, None),
        ),
        check_vma=False,
    )
```

time: 222 us -> 66.4 us (0.30)
  waiting for transfers between devices: 95.7 us -> 14.4 us
  blocking collectives: 45.2 us -> 0 us
  matrix products: 23 us -> 0 us
  local copies, waits for them, and re-layouts: 23.8 us -> 1.54 us
  Pallas kernels: 0 us -> 16.1 us
  starting transfers between devices: 13.7 us -> 28.6 us
  between operations: 14.9 us -> 0.8 us
    psum x1 -> x0, waiting for transfers between devices: 89.1 us -> none  [local(): lax.psum((local_conv, local_conv_bias, local_down, local_down_bias), ('tm...]
    psum x1 -> x0, blocking collectives: 45.2 us -> none  [local(): lax.psum((local_conv, local_conv_bias, local_down, local_down_bias), ('tm...]
    dot_general x88 -> x0, matrix products: 23 us -> none  [the longest x27 8.72 us: local(): jnp.einsum('fkrc,ko->frco', window, conv_weight[tap_time, tap_row, tap_co...]
    reshape x4 -> x2, local copies, waits for them, and re-layouts: 19.1 us -> 0.06 us  [the longest x1 0.03 us: local(): outer = swap_outer(jnp.where(core == 0, top, bottom).reshape(flat_halo))]
    pallas_call x0 -> x3, Pallas kernels: none -> 16.1 us  [the longest x1 11.6 us: local(): pl.pallas_call(functools.partial(main_kernel, (frames, rows, colors, pair...]
    ppermute x6 -> x17, starting transfers between devices: 13.7 us -> 28.6 us  [the longest x9 12.1 us: exchange(): return lax.ppermute(value, axes, [(i, i ^ mask) for i in range(size)])]
    ppermute x6 -> x17, waiting for transfers between devices: 6.6 us -> 14.4 us  [the longest x9 11.2 us: exchange(): return lax.ppermute(value, axes, [(i, i ^ mask) for i in range(size)])]
    mul x4 -> x0, other arithmetic: 4.95 us -> none  [the longest x1 1.99 us: local(): grad_conv = scale * summed[0]]
  transfers between devices with their start and end apart: 7 -> 17, of which waited for: 3 -> 10; matrix products, arithmetic and copies ran while one was open for 6% -> 5% of each run, Pallas kernels for 0% -> 3%
where the time goes in v1:
time: 66.4 us; the launch traced here: 66.1 us
  starting transfers between devices  28.6 us (43%)
  Pallas kernels  16.1 us (24%)
  waiting for transfers between devices  14.4 us (22%)
  other arithmetic  4.65 us (7%)
  local copies, waits for them, and re-layouts  1.54 us (2%)
  between operations  0.8 us (1%)
    ppermute x9, starting transfers between devices, exchange(): return lax.ppermute(value, axes, [(i, i ^ mask) for i in range(size)])  12.1 us
    pallas_call x1, Pallas kernels, local(): pl.pallas_call(functools.partial(main_kernel, (frames, rows, colors, pair...  11.6 us
    ppermute x9, waiting for transfers between devices, exchange(): return lax.ppermute(value, axes, [(i, i ^ mask) for i in range(size)])  11.2 us
    ppermute x4, starting transfers between devices, swap_inner(): return lax.ppermute(value, 'core', [(0, 1), (1, 0)])  9.02 us
    ppermute x2, starting transfers between devices, along_tm(): return lax.ppermute(value, times, pairs)  6.17 us
    ppermute x2, waiting for transfers between devices, along_tm(): return lax.ppermute(value, times, pairs)  3.19 us
    pallas_call x1, Pallas kernels, local(): pl.pallas_call(functools.partial(finish_kernel, 1.0 / math.sqrt(count), c...  2.29 us
    pallas_call x1, Pallas kernels, local(): pl.pallas_call(weights_kernel, out_shape=(jax.ShapeDtypeStruct((3, width,...  2.16 us
  transfers between devices with their start and end apart: 17, of which 10 were waited for; matrix products, arithmetic and copies ran while one was open for 5% of the time, Pallas kernels for 3%

profile of v1, /device:TPU:0, one launch (start us, length us, event | category | flops | bytes accessed | tf_op | source)
XLA Modules:
  0.0 66.1 jit_solution(14463492170739788146)
XLA Ops:
  0.6 4.9 %collective-permute-start = (bf16[48,1024]{1,0:T(8,128)(2,1)}, bf16[48,1024]{1,0:T(8,128)(2,1)S(1)}, u32[]{:S(2)}, u32[]{:S(2)}) collective-permute-start(bf16[48,1024]{1,0:T(8,128)(2,1)} %bitcast.37), channel_id=1, source_target_pairs={{0,16},{1,17},{2,18},{3,19},{4,20},{5,21},{6,22},{7,23},{8,24},{9,... | collective-permute-start | bytes 294920 | tf_op jit(solution)/shard_map/ppermute | solution.py:279
  5.5 2.2 %weights.1 = (bf16[3,128,576]{2,1,0:T(8,128)(2,1)}, bf16[576,384]{1,0:T(8,128)(2,1)}) custom-call(bf16[27,48,128]{2,1,0:T(8,128)(2,1)} %bitcast.40, bf16[64,48]{1,0:T(8,128)(2,1)} %constant.27.clone.order), custom_call_target="tpu_custom_call" | custom-call | tf_op jit(solution)/shard_map/weights/pallas_call | solution.py:293
  8.0 0.9 %maximum_bitcast_fusion = bf16[12,8,1024]{2,1,0:T(8,128)(2,1)S(1)} fusion(bf16[48,1024]{1,0:T(8,128)(2,1)} %bitcast.38, bf16[48,1024]{1,0:T(8,128)(2,1)S(1)} %collective-permute-done.earlier), kind=kLoop, calls=%fused_computation.8 | loop fusion | flops 393216 | bytes 393216 | tf_op jit(solution)/shard_map/reshape | solution.py:309
  11.2 11.6 %main.1 = (bf16[2,1,128,256]{3,2,1,0:T(8,128)(2,1)}, f32[4,296,128]{2,1,0:T(8,128)}, bf16[4,296,128]{2,1,0:T(8,128)(2,1)}, f32[48,1024]{1,0:T(8,128)}, f32[48,10...) custom-call(s32[2]{0:T(128)} %pad_add_fusion.place, bf16[48,1024]{1,0:T(8,128)(2,1)} %bitcast.39, ...), custom_call_target="tpu_custom_call" | custom-call | tf_op jit(solution)/shard_map/main/pallas_call | solution.py:317
  22.9 5.0 %collective-permute-start.3 = (bf16[4,296,128]{2,1,0:T(8,128)(2,1)}, bf16[4,296,128]{2,1,0:T(8,128)(2,1)S(1)}, u32[]{:S(2)}, u32[]{:S(2)}) collective-permute-start(bf16[4,296,128]{2,1,0:T(8,128)(2,1)} %get-tuple-element.23), channel_id=1, source_target_pairs={{0,1},{1,0},{2,3},{3,2},{4,5},{5,4},{6,7},{7,6},{8,9},{9,8},{10,11... | collective-permute-start | bytes 909320 | tf_op jit(solution)/shard_map/ppermute | solution.py:282
  28.6 3.8 %collective-permute-start.15 = (bf16[48,1024]{1,0:T(8,128)(2,1)}, bf16[48,1024]{1,0:T(8,128)(2,1)S(1)}, u32[]{:S(2)}, u32[]{:S(2)}) collective-permute-start(bf16[48,1024]{1,0:T(8,128)(2,1)} %get-tuple-element.30), channel_id=1, source_target_pairs={{0,1},{1,0},{2,3},{3,2},{4,5},{5,4},{6,7},{7,6},{8,9},{9,8},{10,11... | collective-permute-start | bytes 294920 | tf_op jit(solution)/shard_map/ppermute | solution.py:282
  32.4 1.2 %fusion.4 = (bf16[4,296,128]{2,1,0:T(8,128)(2,1)S(1)}, f32[4,296,128]{2,1,0:T(8,128)S(1)}) fusion(f32[4,296,128]{2,1,0:T(8,128)} %get-tuple-element.22, bf16[4,296,128]{2,1,0:T(8,128)(2,1)S(1)} %collective-permute-done.3), kind=kLoop, calls=%fused_computation.21 | loop fusion | flops 454656 | bytes 1818624 | tf_op jit(solution)/shard_map/convert.8
  33.7 1.7 %collective-permute-start.4 = (bf16[296,128]{1,0:T(8,128)(2,1)S(1)}, bf16[296,128]{1,0:T(8,128)(2,1)S(1)}, u32[]{:S(2)}, u32[]{:S(2)}) collective-permute-start(bf16[296,128]{1,0:T(8,128)(2,1)S(1)} %get-tuple-element.34), channel_id=1, source_target_pairs={{0,2},{2,0},{16,18},{18,16},{1,3},{3,1},{17,19},{19,17},{4,6},{6,4... | collective-permute-start | bytes 227336 | tf_op jit(solution)/shard_map/ppermute | solution.py:290
  35.4 2.1 %collective-permute-start.6 = (bf16[296,128]{1,0:T(8,128)(2,1)S(1)}, bf16[296,128]{1,0:T(8,128)(2,1)S(1)}, u32[]{:S(2)}, u32[]{:S(2)}) collective-permute-start(bf16[296,128]{1,0:T(8,128)(2,1)S(1)} %get-tuple-element.35), channel_id=1, source_target_pairs={{0,18},{2,16},{16,2},{18,0},{1,19},{3,17},{17,3},{19,1},{4,22},{6,... | collective-permute-start | bytes 227336 | tf_op jit(solution)/shard_map/ppermute | solution.py:290
  38.1 2.6 %collective-permute-done.6 = bf16[296,128]{1,0:T(8,128)(2,1)S(1)} collective-permute-done((bf16[296,128]{1,0:T(8,128)(2,1)S(1)}, bf16[296,128]{1,0:T(8,128)(2,1)S(1)}, u32[]{:S(2)}, u32[]{:S(2)}) %collective-permute-start.6) | collective-permute-done | bytes 75808 | tf_op jit(solution)/shard_map/ppermute | solution.py:290
  40.7 1.2 %collective-permute-done.5 = bf16[296,128]{1,0:T(8,128)(2,1)S(1)} collective-permute-done((bf16[296,128]{1,0:T(8,128)(2,1)S(1)}, bf16[296,128]{1,0:T(8,128)(2,1)S(1)}, u32[]{:S(2)}, u32[]{:S(2)}) %collective-permute-start.5) | collective-permute-done | bytes 75808 | tf_op jit(solution)/shard_map/ppermute | solution.py:290
  41.9 3.1 %collective-permute-start.9 = (bf16[296,128]{1,0:T(8,128)(2,1)S(1)}, bf16[296,128]{1,0:T(8,128)(2,1)S(1)}, u32[]{:S(2)}, u32[]{:S(2)}) collective-permute-start(bf16[296,128]{1,0:T(8,128)(2,1)S(1)} %fusion.3), channel_id=1, source_target_pairs={{0,12},{4,8},{8,4},{12,0},{1,13},{5,9},{9,5},{13,1},{2,14},{6,10},... | collective-permute-start | bytes 227336 | tf_op jit(solution)/shard_map/ppermute | solution.py:290
  45.0 1.3 %collective-permute-start.7 = (bf16[296,128]{1,0:T(8,128)(2,1)S(1)}, bf16[296,128]{1,0:T(8,128)(2,1)S(1)}, u32[]{:S(2)}, u32[]{:S(2)}) collective-permute-start(bf16[296,128]{1,0:T(8,128)(2,1)S(1)} %fusion.3), channel_id=1, source_target_pairs={{0,4},{4,0},{8,12},{12,8},{1,5},{5,1},{9,13},{13,9},{2,6},{6,2},{1... | collective-permute-start | bytes 227336 | tf_op jit(solution)/shard_map/ppermute | solution.py:290
  46.5 2.1 %collective-permute-done.9 = bf16[296,128]{1,0:T(8,128)(2,1)S(1)} collective-permute-done((bf16[296,128]{1,0:T(8,128)(2,1)S(1)}, bf16[296,128]{1,0:T(8,128)(2,1)S(1)}, u32[]{:S(2)}, u32[]{:S(2)}) %collective-permute-start.9) | collective-permute-done | bytes 75808 | tf_op jit(solution)/shard_map/ppermute | solution.py:290
  48.6 2.8 %collective-permute-done.8 = bf16[296,128]{1,0:T(8,128)(2,1)S(1)} collective-permute-done((bf16[296,128]{1,0:T(8,128)(2,1)S(1)}, bf16[296,128]{1,0:T(8,128)(2,1)S(1)}, u32[]{:S(2)}, u32[]{:S(2)}) %collective-permute-start.8) | collective-permute-done | bytes 75808 | tf_op jit(solution)/shard_map/ppermute | solution.py:290
  51.5 2.4 %collective-permute-start.12 = (bf16[296,128]{1,0:T(8,128)(2,1)S(1)}, bf16[296,128]{1,0:T(8,128)(2,1)S(1)}, u32[]{:S(2)}, u32[]{:S(2)}) collective-permute-start(bf16[296,128]{1,0:T(8,128)(2,1)S(1)} %add_convert_fusion.mine), channel_id=1, source_target_pairs={{0,18},{2,16},{16,2},{18,0},{1,19},{3,17},{17,3},{19,1},{4,22},{6,... | collective-permute-start | bytes 227336 | tf_op jit(solution)/shard_map/ppermute | solution.py:290
  54.3 0.8 %collective-permute-start.10 = (bf16[296,128]{1,0:T(8,128)(2,1)S(1)}, bf16[296,128]{1,0:T(8,128)(2,1)S(1)}, u32[]{:S(2)}, u32[]{:S(2)}) collective-permute-start(bf16[296,128]{1,0:T(8,128)(2,1)S(1)} %add_convert_fusion.mine), channel_id=1, source_target_pairs={{0,2},{2,0},{16,18},{18,16},{1,3},{3,1},{17,19},{19,17},{4,6},{6,4... | collective-permute-start | bytes 227336 | tf_op jit(solution)/shard_map/ppermute | solution.py:290
  55.1 1.3 %collective-permute-start.16 = (bf16[6,8,1024]{2,1,0:T(8,128)(2,1)S(1)}, bf16[6,8,1024]{2,1,0:T(8,128)(2,1)S(1)}, u32[]{:S(2)}, u32[]{:S(2)}) collective-permute-start(bf16[6,8,1024]{2,1,0:T(8,128)(2,1)S(1)} %fusion), channel_id=1, source_target_pairs={{16,0},{17,1},{18,2},{19,3},{20,4},{21,5},{22,6},{23,7},{24,8},{25... | collective-permute-start | bytes 294920 | tf_op jit(solution)/shard_map/ppermute | solution.py:279
  56.4 0.8 %collective-permute-done.12 = bf16[296,128]{1,0:T(8,128)(2,1)S(1)} collective-permute-done((bf16[296,128]{1,0:T(8,128)(2,1)S(1)}, bf16[296,128]{1,0:T(8,128)(2,1)S(1)}, u32[]{:S(2)}, u32[]{:S(2)}) %collective-permute-start.12) | collective-permute-done | bytes 75808 | tf_op jit(solution)/shard_map/ppermute | solution.py:290
  57.2 1.1 %collective-permute-done.11 = bf16[296,128]{1,0:T(8,128)(2,1)S(1)} collective-permute-done((bf16[296,128]{1,0:T(8,128)(2,1)S(1)}, bf16[296,128]{1,0:T(8,128)(2,1)S(1)}, u32[]{:S(2)}, u32[]{:S(2)}) %collective-permute-start.11) | collective-permute-done | bytes 75808 | tf_op jit(solution)/shard_map/ppermute | solution.py:290
  58.8 2.9 %collective-permute-done.16 = bf16[6,8,1024]{2,1,0:T(8,128)(2,1)S(1)} collective-permute-done((bf16[6,8,1024]{2,1,0:T(8,128)(2,1)S(1)}, bf16[6,8,1024]{2,1,0:T(8,128)(2,1)S(1)}, u32[]{:S(2)}, u32[]{:S(2)}) %collective-permute-start.16) | collective-permute-done | bytes 98336 | tf_op jit(solution)/shard_map/ppermute | solution.py:279
  61.6 0.7 %fusion.1 = f32[6,8,1024]{2,1,0:T(8,128)} fusion(f32[12,8,1024]{2,1,0:T(8,128)S(1)} %convert_add_fusion.1, f32[48,1024]{1,0:T(8,128)S(1)} %copy-done.3, bf16[6,8,1024]{2,1,0:T(8,128)(2,1)S(1)} %collective-permute-done.16), kind=kLoop, calls=%fused_computation.7 | loop fusion | flops 147456 | bytes 688128 | tf_op jit(solution)/shard_map/add | solution.py:391
  62.3 0.7 %pad_maximum_fusion.1.others = bf16[3,296,128]{2,1,0:T(8,128)(2,1)} fusion(bf16[1,296,128]{2,1,0:T(8,128)(2,1)S(1)} %bitcast.42, bf16[1,296,128]{2,1,0:T(8,128)(2,1)S(1)} %bitcast.44, bf16[1,296,128]{2,1,0:T(8,128)(2,1)S(1)} %bitcast.46), kind=kLoop, calls=%fused_computation.3 | loop fusion | flops 227328 | bytes 454656 | tf_op jit(solution)/shard_map/stack | solution.py:364
  63.8 2.3 %finish.1 = (f32[27,48,128]{2,1,0:T(8,128)}, f32[1,128]{1,0:T(1,128)}, f32[512,256]{1,0:T(8,128)}, f32[1,256]{1,0:T(1,128)}) custom-call(s32[2]{0:T(128)} %pad_add_fusion.place, bf16[296,128]{1,0:T(8,128)(2,1)} %copy-done, bf16[3,296,128]{2,1,0:T(8,128)(2,1)} %pad_maximum_fusion.1.others, bf16[4,296,128]{2,1,0:T(8,128)(2,1)} %copy-done.2), custom_call_target="tpu_custom_call" | custom-call | tf_op jit(solution)/shard_map/finish/pallas_call | solution.py:367
  (44 shorter events, 5.6 us)
Async XLA Ops:
  0.6 7.4 %collective-permute-start = (bf16[48,1024]{1,0:T(8,128)(2,1)}, bf16[48,1024]{1,0:T(8,128)(2,1)S(1)}, u32[]{:S(2)}, u32[]{:S(2)}) collective-permute-start(bf16[48,1024]{1,0:T(8,128)(2,1)} %bitcast.37), channel_id=1, source_target_pairs={{0,16},{1,17},{2,18},{3,19},{4,20},{5,21},{6,22},{7,23},{8,24},{9,... | collective-permute-start | bytes 294920 | tf_op jit(solution)/shard_map/ppermute | solution.py:279
  8.0 2.6 %copy-start.1 = (bf16[48,1024]{1,0:T(8,128)(2,1)}, bf16[48,1024]{1,0:T(8,128)(2,1)S(1)}, u32[]{:S(2)}) copy-start(bf16[48,1024]{1,0:T(8,128)(2,1)S(1)} %collective-permute-done.earlier) | copy-start | bytes 294916
  9.2 1.4 %collective-permute-start.1 = (bf16[48,1024]{1,0:T(8,128)(2,1)S(1)}, bf16[48,1024]{1,0:T(8,128)(2,1)S(1)}, u32[]{:S(2)}, u32[]{:S(2)}) collective-permute-start(bf16[48,1024]{1,0:T(8,128)(2,1)S(1)} %reshape.73), channel_id=1, source_target_pairs={{0,1},{1,0},{2,3},{3,2},{4,5},{5,4},{6,7},{7,6},{8,9},{9,8},{10,11... | collective-permute-start | bytes 294920 | tf_op jit(solution)/shard_map/ppermute | solution.py:282
  9.2 1.3 %collective-permute-start.2 = (bf16[48,1024]{1,0:T(8,128)(2,1)S(1)}, bf16[48,1024]{1,0:T(8,128)(2,1)S(1)}, u32[]{:S(2)}, u32[]{:S(2)}) collective-permute-start(bf16[48,1024]{1,0:T(8,128)(2,1)S(1)} %reshape.74), channel_id=1, source_target_pairs={{1,2},{3,4},{5,6},{7,8},{9,10},{11,12},{13,14},{2,1},{4,3},{6,5},{... | collective-permute-start | bytes 294920 | tf_op jit(solution)/shard_map/ppermute | solution.py:286
  10.6 0.6 copy-start.5
  10.6 0.7 %copy-start.6 = (bf16[48,1024]{1,0:T(8,128)(2,1)}, bf16[48,1024]{1,0:T(8,128)(2,1)S(1)}, u32[]{:S(2)}) copy-start(bf16[48,1024]{1,0:T(8,128)(2,1)S(1)} %collective-permute-done.2.outer) | copy-start | bytes 294916
  22.9 9.5 %collective-permute-start.3 = (bf16[4,296,128]{2,1,0:T(8,128)(2,1)}, bf16[4,296,128]{2,1,0:T(8,128)(2,1)S(1)}, u32[]{:S(2)}, u32[]{:S(2)}) collective-permute-start(bf16[4,296,128]{2,1,0:T(8,128)(2,1)} %get-tuple-element.23), channel_id=1, source_target_pairs={{0,1},{1,0},{2,3},{3,2},{4,5},{5,4},{6,7},{7,6},{8,9},{9,8},{10,11... | collective-permute-start | bytes 909320 | tf_op jit(solution)/shard_map/ppermute | solution.py:282
  27.9 9.8 %collective-permute-start.14 = (bf16[48,1024]{1,0:T(8,128)(2,1)}, bf16[48,1024]{1,0:T(8,128)(2,1)S(1)}, u32[]{:S(2)}, u32[]{:S(2)}) collective-permute-start(bf16[48,1024]{1,0:T(8,128)(2,1)} %get-tuple-element.29), channel_id=1, source_target_pairs={{1,2},{3,4},{5,6},{7,8},{9,10},{11,12},{13,14},{2,1},{4,3},{6,5},{... | collective-permute-start | bytes 294920 | tf_op jit(solution)/shard_map/ppermute | solution.py:286
  28.6 9.1 %collective-permute-start.15 = (bf16[48,1024]{1,0:T(8,128)(2,1)}, bf16[48,1024]{1,0:T(8,128)(2,1)S(1)}, u32[]{:S(2)}, u32[]{:S(2)}) collective-permute-start(bf16[48,1024]{1,0:T(8,128)(2,1)} %get-tuple-element.30), channel_id=1, source_target_pairs={{0,1},{1,0},{2,3},{3,2},{4,5},{5,4},{6,7},{7,6},{8,9},{9,8},{10,11... | collective-permute-start | bytes 294920 | tf_op jit(solution)/shard_map/ppermute | solution.py:282
  32.4 22.7 %copy-start.4 = (f32[48,1024]{1,0:T(8,128)S(1)}, f32[48,1024]{1,0:T(8,128)}, u32[]{:S(2)}) copy-start(f32[48,1024]{1,0:T(8,128)} %get-tuple-element.31) | copy-start | bytes 589828
  33.6 28.0 %copy-start.3 = (f32[48,1024]{1,0:T(8,128)S(1)}, f32[48,1024]{1,0:T(8,128)}, u32[]{:S(2)}) copy-start(f32[48,1024]{1,0:T(8,128)} %get-tuple-element.28) | copy-start | bytes 589828
  33.7 4.4 %collective-permute-start.4 = (bf16[296,128]{1,0:T(8,128)(2,1)S(1)}, bf16[296,128]{1,0:T(8,128)(2,1)S(1)}, u32[]{:S(2)}, u32[]{:S(2)}) collective-permute-start(bf16[296,128]{1,0:T(8,128)(2,1)S(1)} %get-tuple-element.34), channel_id=1, source_target_pairs={{0,2},{2,0},{16,18},{18,16},{1,3},{3,1},{17,19},{19,17},{4,6},{6,4... | collective-permute-start | bytes 227336 | tf_op jit(solution)/shard_map/ppermute | solution.py:290
  35.4 5.3 %collective-permute-start.6 = (bf16[296,128]{1,0:T(8,128)(2,1)S(1)}, bf16[296,128]{1,0:T(8,128)(2,1)S(1)}, u32[]{:S(2)}, u32[]{:S(2)}) collective-permute-start(bf16[296,128]{1,0:T(8,128)(2,1)S(1)} %get-tuple-element.35), channel_id=1, source_target_pairs={{0,18},{2,16},{16,2},{18,0},{1,19},{3,17},{17,3},{19,1},{4,22},{6,... | collective-permute-start | bytes 227336 | tf_op jit(solution)/shard_map/ppermute | solution.py:290
  37.5 4.4 %collective-permute-start.5 = (bf16[296,128]{1,0:T(8,128)(2,1)S(1)}, bf16[296,128]{1,0:T(8,128)(2,1)S(1)}, u32[]{:S(2)}, u32[]{:S(2)}) collective-permute-start(bf16[296,128]{1,0:T(8,128)(2,1)S(1)} %get-tuple-element.36), channel_id=1, source_target_pairs={{0,16},{2,18},{16,0},{18,2},{1,17},{3,19},{17,1},{19,3},{4,20},{6,... | collective-permute-start | bytes 227336 | tf_op jit(solution)/shard_map/ppermute | solution.py:290
  41.9 6.7 %collective-permute-start.9 = (bf16[296,128]{1,0:T(8,128)(2,1)S(1)}, bf16[296,128]{1,0:T(8,128)(2,1)S(1)}, u32[]{:S(2)}, u32[]{:S(2)}) collective-permute-start(bf16[296,128]{1,0:T(8,128)(2,1)S(1)} %fusion.3), channel_id=1, source_target_pairs={{0,12},{4,8},{8,4},{12,0},{1,13},{5,9},{9,5},{13,1},{2,14},{6,10},... | collective-permute-start | bytes 227336 | tf_op jit(solution)/shard_map/ppermute | solution.py:290
  45.0 6.4 %collective-permute-start.8 = (bf16[296,128]{1,0:T(8,128)(2,1)S(1)}, bf16[296,128]{1,0:T(8,128)(2,1)S(1)}, u32[]{:S(2)}, u32[]{:S(2)}) collective-permute-start(bf16[296,128]{1,0:T(8,128)(2,1)S(1)} %fusion.3), channel_id=1, source_target_pairs={{0,8},{4,12},{8,0},{12,4},{1,9},{5,13},{9,1},{13,5},{2,10},{6,14},... | collective-permute-start | bytes 227336 | tf_op jit(solution)/shard_map/ppermute | solution.py:290
  45.0 6.4 %collective-permute-start.7 = (bf16[296,128]{1,0:T(8,128)(2,1)S(1)}, bf16[296,128]{1,0:T(8,128)(2,1)S(1)}, u32[]{:S(2)}, u32[]{:S(2)}) collective-permute-start(bf16[296,128]{1,0:T(8,128)(2,1)S(1)} %fusion.3), channel_id=1, source_target_pairs={{0,4},{4,0},{8,12},{12,8},{1,5},{5,1},{9,13},{13,9},{2,6},{6,2},{1... | collective-permute-start | bytes 227336 | tf_op jit(solution)/shard_map/ppermute | solution.py:290
  51.5 11.6 %copy-start = (bf16[296,128]{1,0:T(8,128)(2,1)}, bf16[296,128]{1,0:T(8,128)(2,1)S(1)}, u32[]{:S(2)}) copy-start(bf16[296,128]{1,0:T(8,128)(2,1)S(1)} %add_convert_fusion.mine) | copy-start | bytes 227332
  51.5 5.7 %collective-permute-start.12 = (bf16[296,128]{1,0:T(8,128)(2,1)S(1)}, bf16[296,128]{1,0:T(8,128)(2,1)S(1)}, u32[]{:S(2)}, u32[]{:S(2)}) collective-permute-start(bf16[296,128]{1,0:T(8,128)(2,1)S(1)} %add_convert_fusion.mine), channel_id=1, source_target_pairs={{0,18},{2,16},{16,2},{18,0},{1,19},{3,17},{17,3},{19,1},{4,22},{6,... | collective-permute-start | bytes 227336 | tf_op jit(solution)/shard_map/ppermute | solution.py:290
  53.9 4.4 %collective-permute-start.11 = (bf16[296,128]{1,0:T(8,128)(2,1)S(1)}, bf16[296,128]{1,0:T(8,128)(2,1)S(1)}, u32[]{:S(2)}, u32[]{:S(2)}) collective-permute-start(bf16[296,128]{1,0:T(8,128)(2,1)S(1)} %add_convert_fusion.mine), channel_id=1, source_target_pairs={{0,16},{2,18},{16,0},{18,2},{1,17},{3,19},{17,1},{19,3},{4,20},{6,... | collective-permute-start | bytes 227336 | tf_op jit(solution)/shard_map/ppermute | solution.py:290
  54.3 4.4 %collective-permute-start.10 = (bf16[296,128]{1,0:T(8,128)(2,1)S(1)}, bf16[296,128]{1,0:T(8,128)(2,1)S(1)}, u32[]{:S(2)}, u32[]{:S(2)}) collective-permute-start(bf16[296,128]{1,0:T(8,128)(2,1)S(1)} %add_convert_fusion.mine), channel_id=1, source_target_pairs={{0,2},{2,0},{16,18},{18,16},{1,3},{3,1},{17,19},{19,17},{4,6},{6,4... | collective-permute-start | bytes 227336 | tf_op jit(solution)/shard_map/ppermute | solution.py:290
  55.1 6.5 %collective-permute-start.16 = (bf16[6,8,1024]{2,1,0:T(8,128)(2,1)S(1)}, bf16[6,8,1024]{2,1,0:T(8,128)(2,1)S(1)}, u32[]{:S(2)}, u32[]{:S(2)}) collective-permute-start(bf16[6,8,1024]{2,1,0:T(8,128)(2,1)S(1)} %fusion), channel_id=1, source_target_pairs={{16,0},{17,1},{18,2},{19,3},{20,4},{21,5},{22,6},{23,7},{24,8},{25... | collective-permute-start | bytes 294920 | tf_op jit(solution)/shard_map/ppermute | solution.py:279
  58.7 4.4 %collective-permute-start.13 = (bf16[4,296,128]{2,1,0:T(8,128)(2,1)S(1)}, bf16[4,296,128]{2,1,0:T(8,128)(2,1)S(1)}, u32[]{:S(2)}, u32[]{:S(2)}) collective-permute-start(bf16[4,296,128]{2,1,0:T(8,128)(2,1)S(1)} %pad_maximum_fusion), channel_id=1, source_target_pairs={{0,1},{1,0},{2,3},{3,2},{4,5},{5,4},{6,7},{7,6},{8,9},{9,8},{10,11... | collective-permute-start | bytes 909320 | tf_op jit(solution)/shard_map/ppermute | solution.py:282
  63.1 0.7 %copy-start.2 = (bf16[4,296,128]{2,1,0:T(8,128)(2,1)}, bf16[4,296,128]{2,1,0:T(8,128)(2,1)S(1)}, u32[]{:S(2)}) copy-start(bf16[4,296,128]{2,1,0:T(8,128)(2,1)S(1)} %collective-permute-done.13.theirs) | copy-start | bytes 909316

commit v2 on v0

v2 whole, which is shorter than its diff:
```python
import functools
import math

import jax
import jax.numpy as jnp
import numpy as np
from jax import lax
from jax.experimental import pallas as pl
from jax.experimental.pallas import tpu as pltpu
from jax.sharding import Mesh, PartitionSpec as P


BF16, F32 = jnp.bfloat16, jnp.float32
HAAR = np.kron(np.array([[1.0, 1.0], [1.0, -1.0]]), np.array([[1.0, 1.0], [1.0, -1.0]])) * 0.5
VMEM = pl.BlockSpec(memory_space=pltpu.VMEM)
SMEM = pl.BlockSpec(memory_space=pltpu.SMEM)
ANY = pl.BlockSpec(memory_space=pl.ANY)
NN = (((1,), (0,)), ((), ()))
NT = (((1,), (1,)), ((), ()))
COLORS, CH, WIDTH = 3, 48, 128
TAPS = 3 * CH


def mm(a, b, dims=NN):
    return lax.dot_general(a, b, dims, preferred_element_type=F32)


def split(x):
    high = x.astype(BF16)
    return high, (x - high.astype(F32)).astype(BF16)


def call(body, outs, ins, scratch=(), flops=0, grant=24, **more):
    shapes = [jax.ShapeDtypeStruct(shape, dtype) for shape, dtype in outs]
    return pl.pallas_call(
        body,
        out_shape=shapes,
        scratch_shapes=list(scratch),
        cost_estimate=pl.CostEstimate(flops=flops, bytes_accessed=1 << 20, transcendentals=0),
        compiler_params=pltpu.CompilerParams(vmem_limit_bytes=grant << 20),
        in_specs=ins,
        **{"out_specs": [VMEM] * len(outs), **more},
    )


def column_table(quarter):
    table = np.zeros((8 * quarter, 4, 2, quarter), np.float32)
    for parity in range(2):
        for pair in range(quarter):
            for v in range(4):
                table[8 * pair + 4 * parity + v, :, parity, pair] = HAAR[:, v]
    return table.reshape(8 * quarter, 8 * quarter)


def row_table(frames, rows):
    table = np.zeros((frames, rows, COLORS, 4, 4, 4, frames, COLORS, rows, 4), np.float32)
    for f in range(frames):
        for r in range(rows):
            for k in range(COLORS):
                for j in range(4):
                    table[f, r, k, :, j, j, f, k, r, :] = HAAR
    return table.reshape(frames * rows * CH, 4 * frames * COLORS * rows * 4)


def shifts(pair):
    lane = lax.broadcasted_iota(jnp.int32, (1, pair), 1)

    def left(value):
        return jnp.where(lane == pair - 1, 0.0, pltpu.roll(value, pair - 1, 1))

    def right(value):
        return jnp.where(lane == 0, 0.0, pltpu.roll(value, 1, 1))

    return left, right


def analyse(groups, table, rows_tables, x, places, pair):
    left, right = shifts(pair)
    low_half = lax.broadcasted_iota(jnp.int32, (1, pair), 1) < pair // 2
    size, width = groups[0].shape
    stacked = [group[:, half * width // 2 : (half + 1) * width // 2] for group in groups for half in range(2)]
    columns = mm(jnp.concatenate(stacked, axis=0), table[...])
    for n, (rows_table, where) in enumerate(zip(rows_tables, places)):
        blocks = []
        for j in range(4):
            one = columns[2 * n * size : (2 * n + 1) * size, pair * j : pair * (j + 1)]
            two = columns[(2 * n + 1) * size : (2 * n + 2) * size, pair * j : pair * (j + 1)]
            even = jnp.where(low_half, one, pltpu.roll(two, pair // 2, 1))
            odd = jnp.where(low_half, pltpu.roll(one, pair // 2, 1), two)
            blocks.append(jnp.concatenate([even, odd], axis=1))
        high, low = split(jnp.concatenate(blocks, axis=0))
        cells = (mm(rows_table[...], high) + mm(rows_table[...], low)).astype(BF16)
        even, odd = cells[:, :pair].astype(F32), cells[:, pair:].astype(F32)
        taps = (
            jnp.concatenate([right(odd), even], axis=1).astype(BF16),
            cells,
            jnp.concatenate([odd, left(even)], axis=1).astype(BF16),
        )
        for block, (f, r) in enumerate(where):
            for d in range(3):
                x[f, r, CH * d : CH * (d + 1)] = taps[d][CH * block : CH * (block + 1)]


def synthesise(groups, table, rows_tables, pair):
    low_half = lax.broadcasted_iota(jnp.int32, (1, pair), 1) < pair // 2
    stacked = []
    for cells, rows_table in zip(groups, rows_tables):
        turned = mm(rows_table[...], cells.astype(BF16), (((0,), (0,)), ((), ())))
        size = turned.shape[0] // 4
        ones, twos = [], []
        for j in range(4):
            even = turned[size * j : size * (j + 1), :pair]
            odd = turned[size * j : size * (j + 1), pair:]
            ones.append(jnp.where(low_half, even, pltpu.roll(odd, pair // 2, 1)))
            twos.append(jnp.where(low_half, pltpu.roll(even, pair // 2, 1), odd))
        stacked += [jnp.concatenate(ones, axis=1), jnp.concatenate(twos, axis=1)]
    pixels = mm(jnp.concatenate(stacked, axis=0).astype(BF16), table[...], NT)
    size = stacked[0].shape[0]
    return [
        jnp.concatenate(
            [pixels[2 * n * size : (2 * n + 1) * size], pixels[(2 * n + 1) * size : (2 * n + 2) * size]],
            axis=1,
        )
        for n in range(len(groups))
    ]


def weights_kernel(weight, inside, outside, backward):
    for a in range(3):
        for b in range(3):
            for d in range(3):
                at = CH * (3 * a + b)
                backward[at : at + CH, WIDTH * d : WIDTH * (d + 1)] = weight[9 * a + 3 * b + d]
        taps = weight[9 * a : 9 * a + 9].reshape(3 * TAPS, WIDTH).astype(F32)
        at = slice(WIDTH * a, WIDTH * (a + 1))
        inside[0, at] = taps[TAPS:].T.astype(BF16)
        inside[1, at] = taps[: 2 * TAPS].T.astype(BF16)
        outside[0, at] = taps[:TAPS].T.astype(BF16)
        outside[1, at] = taps[2 * TAPS :].T.astype(BF16)


def pack_kernel(dims, place, own, earlier, inner, outer):
    frames, rows, _ = dims
    core = place[0]
    at = 0
    for part, count in ((earlier, 2), (own, frames)):
        count *= COLORS
        pixels = part[...].astype(F32).reshape(count, 4 * rows, part.shape[1])
        top, bottom = pixels[:, :4], pixels[:, 4 * rows - 4 :]
        size = 4 * count
        for target, first, second in ((inner, bottom, top), (outer, top, bottom)):
            chosen = jnp.where(core == 0, first, second)
            target[at : at + size] = chosen.reshape(size, part.shape[1]).astype(BF16)
        at += size


def taps_of(frame, frames):
    return [(f, frame - f) for f in range(frames) if 0 <= frame - f < 3]


def convolve(total, weights, values, frame, frames):
    used = taps_of(frame, frames)
    first = min(a for _, a in used)
    last = max(a for _, a in used)
    part = mm(weights[WIDTH * first : WIDTH * (last + 1)], values)
    for f, a in used:
        here = part[WIDTH * (a - first) : WIDTH * (a - first + 1)]
        total[f] = here if total[f] is None else total[f] + here


def early_kernel(
    dims, own, earlier, table, rows_own, inside, conv_bias, down_weight, cotangent, x, pre, dact
):
    frames, rows, pair = dims
    places = [
        [(f, r) for f in range(2) for r in range(rows)],
        [(2 + f, r) for f in range(frames) for r in range(rows)],
    ]
    analyse([earlier[...], own[...]], table, [rows_own, rows_own], x, places, pair)
    bias = jnp.broadcast_to(conv_bias[...], (WIDTH, WIDTH)).T
    bias = jnp.concatenate([bias] * (2 * pair // WIDTH), axis=1)
    for r in range(rows):
        total = [bias] * frames
        for frame in range(frames + 2):
            values = x[frame].reshape(rows * TAPS, 2 * pair)
            convolve(total, inside[r], values, frame, frames)
        for f in range(frames):
            pre[f, r] = total[f]
    for f in range(frames):
        dact[f] = mm(down_weight[...], cotangent[f, 0], NT)


def main_kernel(
    dims,
    place,
    inner,
    outer,
    table,
    rows_halo,
    x_own,
    pre_own,
    dact,
    outside,
    cotangent,
    keep,
    give,
    acts,
    slopes,
    x,
    packed,
):
    frames, rows, pair = dims
    core, plane = place[0], place[1]
    inner_row = jnp.where(core == 0, rows + 1, 0)
    outer_row = jnp.where(core == 0, 0, rows + 1)
    for frame in range(frames + 2):
        x[frame, 1 : rows + 1] = x_own[frame]
    places = [
        [(f, inner_row) for f in range(frames + 2)],
        [(f, outer_row) for f in range(frames + 2)],
    ]
    analyse([inner[...], outer[...]], table, [rows_halo, rows_halo], x, places, pair)

    for r in range(rows):
        total = [pre_own[f, r] for f in range(frames)]
        edge = 0 if r == 0 else rows + 1
        for frame in range(frames + 2):
            convolve(total, outside[r], x[frame, edge], frame, frames)
        for f in range(frames):
            pre = total[f]
            sig = jax.nn.sigmoid(pre)
            act = pre * sig
            at = 2 * WIDTH * r
            acts[f, at : at + WIDTH] = act[:, :pair].astype(BF16)
            acts[f, at + WIDTH : at + 2 * WIDTH] = act[:, pair:].astype(BF16)
            here = jnp.concatenate(
                [dact[f, at : at + WIDTH], dact[f, at + WIDTH : at + 2 * WIDTH]], axis=1
            )
            slope = here * sig * (1.0 + pre * (1.0 - sig))
            slopes[WIDTH * f : WIDTH * (f + 1), 2 * pair * r : 2 * pair * (r + 1)] = slope.astype(BF16)

    conv_total = [None] * 3
    for frame in range(frames + 2):
        used = taps_of(frame, frames)
        first, last = used[0][0], used[-1][0]
        values = jnp.concatenate(
            [x[frame, r : r + 3].reshape(3 * TAPS, 2 * pair) for r in range(rows)], axis=1
        )
        part = mm(values, slopes[WIDTH * first : WIDTH * (last + 1)], NT)
        for f, a in used:
            here = part[:, WIDTH * (f - first) : WIDTH * (f - first + 1)]
            conv_total[a] = here if conv_total[a] is None else conv_total[a] + here
    down_total = None
    cot_total = None
    ones = jnp.ones((8, 2 * pair * rows), BF16)
    for f in range(frames):
        part = mm(acts[f], cotangent[f, 0])
        down_total = part if down_total is None else down_total + part
        part = mm(ones[:, :pair], cotangent[f, 0])
        cot_total = part if cot_total is None else cot_total + part
    slope_total = mm(ones, slopes[...], NT)
    slope_total = sum(slope_total[0:1, WIDTH * f : WIDTH * (f + 1)] for f in range(frames))

    chunk = keep.shape[1]
    half = 27 * CH // 2
    conv = jnp.concatenate(conv_total, axis=0)
    sums = [slope_total, cot_total[0:1, :WIDTH], cot_total[0:1, WIDTH:]]
    highs = [value.astype(BF16).astype(F32) for value in sums]
    lows = [value - high for value, high in zip(sums, highs)]
    sums = jnp.concatenate(highs + lows + [jnp.zeros((2, WIDTH), F32)], axis=0)
    down_rows = 2 * rows * WIDTH
    for h in range(2):
        packed[h, :half] = conv[half * h : half * (h + 1)]
        packed[h, half : half + down_rows] = down_total[:, WIDTH * h : WIDTH * (h + 1)]
        packed[h, half + down_rows : half + down_rows + 8] = sums if h == 0 else jnp.zeros_like(sums)
        rest = 4 * chunk - half - down_rows - 8
        if rest:
            packed[h, half + down_rows + 8 :] = jnp.zeros((rest, WIDTH), F32)
    for m in range(4):
        at = pl.multiple_of(jnp.bitwise_xor(plane, m) * chunk, 8)
        keep[m] = packed[core, pl.ds(at, chunk)]
        give[m] = packed[1 - core, pl.ds(at, chunk)].astype(BF16)


def late_kernel(
    dims,
    place,
    acts,
    slopes,
    backward,
    down_weight,
    down_bias,
    table,
    rows_own,
    rows_halo,
    features,
    pixels_own,
    pixels_early,
    send_inner,
    send_outer,
    spread,
):
    frames, rows, pair = dims
    core = place[0]
    inner_row = jnp.where(core == 0, rows + 1, 0)
    outer_row = jnp.where(core == 0, 0, rows + 1)
    left, right = shifts(pair)
    spread[...] = jnp.zeros_like(spread)
    for f in range(frames):
        for r in range(rows):
            slope = slopes[WIDTH * f : WIDTH * (f + 1), 2 * pair * r : 2 * pair * (r + 1)]
            even, odd = slope[:, :pair].astype(F32), slope[:, pair:].astype(F32)
            shifted = jnp.concatenate(
                [
                    jnp.concatenate([odd, left(even)], axis=1).astype(BF16),
                    slope,
                    jnp.concatenate([right(odd), even], axis=1).astype(BF16),
                ],
                axis=0,
            )
            reach = mm(backward[...], shifted)
            for a in range(3):
                for b in range(3):
                    at = CH * (3 * a + b)
                    spread[f + a, r + b] += reach[at : at + CH]

    def rows_of(blocks):
        return jnp.concatenate([spread[f, r] for f, r in blocks], axis=0)

    groups = [
        rows_of([(f, 1 + r) for f in range(2) for r in range(rows)]),
        rows_of([(2 + f, 1 + r) for f in range(frames) for r in range(rows)]),
        rows_of([(f, inner_row) for f in range(frames + 2)]),
        rows_of([(f, outer_row) for f in range(frames + 2)]),
    ]
    tables = [rows_own, rows_own, rows_halo, rows_halo]
    early, own, inner, outer = synthesise(groups, table, tables, pair)
    pixels_early[...] = early
    pixels_own[...] = own
    send_inner[...] = inner.astype(BF16)
    send_outer[...] = outer.astype(BF16)
    for f in range(frames):
        turned = jnp.concatenate(
            [acts[f, WIDTH * n : WIDTH * (n + 1)].astype(F32).T.astype(BF16) for n in range(4)], axis=1
        )
        features[f, 0] = (mm(turned, down_weight[...]) + down_bias[...]).astype(BF16)


def finish_kernel(scale, other, place, *refs):
    pieces, (conv, conv_bias, down, down_bias, flat, sums, sems) = refs[:4], refs[-7:]
    if other:
        pieces = [refs[0].at[m] for m in range(4)]
    core, plane = place[0], place[1]
    which = 1 - core if other else core
    chunk = pieces[0].shape[0]
    for m in range(4):
        at = pl.multiple_of(jnp.bitwise_xor(plane, m) * chunk, 8)
        flat[pl.ds(at, chunk)] = pieces[m][...].astype(F32) * scale
    half, down_rows = conv.shape[0] // 2, down.shape[0]
    at = pl.multiple_of(half * which, 8)
    copies = [
        pltpu.make_async_copy(flat.at[pl.ds(0, half)], conv.at[pl.ds(at, half)], sems.at[0]),
        pltpu.make_async_copy(
            flat.at[pl.ds(half, down_rows)],
            down.at[:, pl.ds(pl.multiple_of(WIDTH * which, WIDTH), WIDTH)],
            sems.at[1],
        ),
    ]
    for copy in copies:
        copy.start()

    @pl.when(which == 0)
    def _():
        at = half + down_rows
        total = flat[at : at + 8]
        total = total[0:3] + total[3:6]
        for n in range(3):
            sums[n] = total[n : n + 1]
        targets = [conv_bias, down_bias.at[:, pl.ds(0, WIDTH)], down_bias.at[:, pl.ds(WIDTH, WIDTH)]]
        small = [
            pltpu.make_async_copy(sums.at[n], target, sems.at[2 + n]) for n, target in enumerate(targets)
        ]
        for copy in small:
            copy.start()
        for copy in small:
            copy.wait()

    for copy in copies:
        copy.wait()


def local(axes, pixels, conv_weight, conv_bias, down_weight, down_bias, cotangent):
    times, heights = axes["tm"], axes["height"]
    frames, colors, pixel_rows, pixel_columns = pixels.shape
    rows, columns = pixel_rows // 4, pixel_columns // 4
    assert frames == 2 and rows == 2 and colors == COLORS
    assert conv_weight.shape[3:] == (CH, WIDTH)
    pair = columns // 2
    width2 = down_weight.shape[3]
    core = lax.axis_index("core")
    plane = 2 * lax.axis_index("tm_lo") + lax.axis_index("y")
    place = jnp.stack([core, plane]).astype(jnp.int32)
    count_tm, count_height = lax.axis_size(times), lax.axis_size(heights)
    dims = (frames, rows, pair)

    def along_tm(value, step):
        pairs = [(i, i + step) for i in range(count_tm) if 0 <= i + step < count_tm]
        return lax.ppermute(value, times, pairs)

    def swap_inner(value):
        return lax.ppermute(value, "core", [(0, 1), (1, 0)])

    def swap_outer(value):
        pairs = [(i, i + 1) for i in range(1, count_height - 1, 2)]
        return lax.ppermute(value, heights, pairs + [(j, i) for i, j in pairs])

    def exchange(value, axes, mask):
        size = lax.axis_size(axes)
        return lax.ppermute(value, axes, [(i, i ^ mask) for i in range(size)])

    table = jnp.asarray(column_table(pair // 2), BF16)
    rows_own = jnp.asarray(row_table(frames, rows), BF16)
    rows_halo = jnp.asarray(row_table(frames + 2, 1), BF16)

    own = pixels.reshape(frames * colors * pixel_rows, pixel_columns)
    earlier = along_tm(own, 1)
    inside, outside, backward = call(
        weights_kernel,
        [((2, 3 * WIDTH, 2 * TAPS), BF16), ((2, 3 * WIDTH, TAPS), BF16), ((9 * CH, 3 * WIDTH), BF16)],
        [VMEM],
        flops=10**9,
    )(conv_weight.reshape(27, CH, WIDTH))
    frame_shape = (2 * colors, pixel_rows, pixel_columns)
    flat_halo = ((frames + 2) * colors * 4, pixel_columns)
    send_inner, send_outer = call(
        functools.partial(pack_kernel, dims),
        [(flat_halo, BF16), (flat_halo, BF16)],
        [SMEM, VMEM, VMEM],
    )(place, own, earlier)
    inner = swap_inner(send_inner)
    outer = swap_outer(send_outer)

    down_flat = down_weight.reshape(4 * WIDTH, width2)
    x_own, pre_own, dact = call(
        functools.partial(early_kernel, dims),
        [
            ((frames + 2, rows, TAPS, columns), BF16),
            ((frames, rows, WIDTH, columns), F32),
            ((frames, 4 * WIDTH, pair), F32),
        ],
        [VMEM] * 8,
        flops=10**9,
    )(own, earlier, table, rows_own, inside, conv_bias.reshape(1, WIDTH), down_flat, cotangent)

    data_rows = 27 * CH // 2 + 4 * WIDTH + 8
    chunk = -(-data_rows // 32) * 8
    keep, give, acts, slopes = call(
        functools.partial(main_kernel, dims),
        [
            ((4, chunk, WIDTH), F32),
            ((4, chunk, WIDTH), BF16),
            ((frames, 4 * WIDTH, pair), BF16),
            ((frames * WIDTH, rows * columns), BF16),
        ],
        [SMEM] + [VMEM] * 9,
        [
            pltpu.VMEM((frames + 2, rows + 2, TAPS, columns), BF16),
            pltpu.VMEM((2, 4 * chunk, WIDTH), F32),
        ],
        flops=10**9,
    )(place, inner, outer, table, rows_halo, x_own, pre_own, dact, outside, cotangent)

    features, pixels_own, pixels_early, send_inner, send_outer = call(
        functools.partial(late_kernel, dims),
        [
            ((frames, rows // 2, pair, width2), BF16),
            (own.shape, F32),
            (own.shape, F32),
            (flat_halo, BF16),
            (flat_halo, BF16),
        ],
        [SMEM] + [VMEM] * 8,
        [pltpu.VMEM((frames + 2, rows + 2, CH, columns), F32)],
        flops=10**9,
    )(
        place,
        acts,
        slopes,
        backward,
        down_flat,
        down_bias.reshape(1, width2),
        table,
        rows_own,
        rows_halo,
    )

    total = keep + swap_inner(give).astype(F32)
    planes = ("tm_lo", "y")
    parts = [exchange(total[m].astype(BF16), planes, m) for m in (1, 2, 3)]
    mine = total[0] + sum(part.astype(F32) for part in parts)
    for axis in axes["rest"]:
        sent = mine.astype(BF16)
        parts = [exchange(sent, axis, m) for m in range(1, lax.axis_size(axis))]
        mine = mine + sum(part.astype(F32) for part in parts)
    mine = mine.astype(BF16)
    pieces = [mine] + [exchange(mine, planes, m) for m in (1, 2, 3)]
    theirs = swap_inner(jnp.stack(pieces))
    count = frames * count_tm * rows * count_height * columns
    scale = 1.0 / math.sqrt(count)
    outs = [
        ((27 * CH, WIDTH), F32),
        ((1, WIDTH), F32),
        ((4 * WIDTH, width2), F32),
        ((1, width2), F32),
    ]
    scratch = [
        pltpu.VMEM((4 * chunk, WIDTH), F32),
        pltpu.VMEM((3, 1, WIDTH), F32),
        pltpu.SemaphoreType.DMA((5,)),
    ]
    grads = call(
        functools.partial(finish_kernel, scale, False),
        outs,
        [SMEM] + [VMEM] * 4,
        scratch,
        out_specs=[ANY] * 4,
    )(place, *pieces)
    grad_conv, grad_conv_bias, grad_down, grad_down_bias = call(
        functools.partial(finish_kernel, scale, True),
        outs,
        [SMEM, VMEM] + [ANY] * 4,
        scratch,
        out_specs=[ANY] * 4,
        input_output_aliases={2: 0, 3: 1, 4: 2, 5: 3},
    )(place, theirs, *grads)

    from_inner = swap_inner(send_inner).reshape((frames + 2) * colors, 4, pixel_columns)
    from_outer = swap_outer(send_outer).reshape((frames + 2) * colors, 4, pixel_columns)
    above = jnp.where(core == 0, from_outer, from_inner).astype(F32)
    below = jnp.where(core == 0, from_inner, from_outer).astype(F32)
    halo = jnp.concatenate([above, below], axis=1)
    early = pixels_early.reshape(frame_shape) + halo[: 2 * colors]
    late = pixels_own.reshape(frame_shape) + halo[2 * colors :]
    grad_pixels = late + along_tm(early.astype(BF16), -1).astype(F32)
    return (
        features,
        grad_conv.reshape(conv_weight.shape),
        grad_conv_bias.reshape(WIDTH),
        grad_down.reshape(down_weight.shape),
        grad_down_bias.reshape(width2),
        grad_pixels.reshape(pixels.shape),
    )


def factors(size):
    parts = []
    while size > 1:
        part = 4 if size % 4 == 0 else 2
        assert size % part == 0
        parts.append(part)
        size //= part
    return parts


def solution(mesh):
    count_tm, count_height = mesh.shape["tm"], mesh.shape["height"]
    tm_parts, height_parts = factors(count_tm // 2), factors(count_height // 4)
    tm_names = tuple(f"tm_{n}" for n in range(len(tm_parts)))
    height_names = tuple(f"z_{n}" for n in range(len(height_parts)))
    axes = {
        "tm": tm_names + ("tm_lo",),
        "height": height_names + ("y", "core"),
        "rest": tm_names + height_names,
    }
    fine = Mesh(
        mesh.devices.reshape(tm_parts + [2] + height_parts + [2, 2]), axes["tm"] + axes["height"]
    )
    tm, height = axes["tm"], axes["height"]

    def body(*args):
        return local(axes, *args)

    return jax.shard_map(
        body,
        mesh=fine,
        in_specs=(P(tm, None, height, None), P(), P(), P(), P(), P(tm, height, None, None)),
        out_specs=(
            P(tm, height, None, None),
            P(),
            P(),
            P(),
            P(),
            P(tm, None, height, None),
        ),
        check_vma=False,
    )
```

time: 222 us -> 59 us (0.27)
  waiting for transfers between devices: 95.7 us -> 16.5 us
  blocking collectives: 45.2 us -> 0 us
  matrix products: 23 us -> 0 us
  local copies, waits for them, and re-layouts: 23.8 us -> 3.53 us
  between operations: 14.9 us -> 0.84 us
  starting transfers between devices: 13.7 us -> 25.8 us
  Pallas kernels: 0 us -> 10.9 us
  other arithmetic: 5.21 us -> 1.16 us
    psum x1 -> x0, waiting for transfers between devices: 89.1 us -> none  [local(): lax.psum((local_conv, local_conv_bias, local_down, local_down_bias), ('tm...]
    psum x1 -> x0, blocking collectives: 45.2 us -> none  [local(): lax.psum((local_conv, local_conv_bias, local_down, local_down_bias), ('tm...]
    dot_general x88 -> x0, matrix products: 23 us -> none  [the longest x27 8.72 us: local(): jnp.einsum('fkrc,ko->frco', window, conv_weight[tap_time, tap_row, tap_co...]
    reshape x4 -> x0, local copies, waits for them, and re-layouts: 19.1 us -> none  [the longest x2 11.8 us: analyse(): pixels.astype(jnp.float32)]
    ppermute x6 -> x17, starting transfers between devices: 13.7 us -> 25.8 us  [the longest x9 12 us: exchange(): return lax.ppermute(value, axes, [(i, i ^ mask) for i in range(size)])]
    pallas_call x0 -> x7, Pallas kernels: none -> 10.9 us  [the longest x1 3.19 us: local(): call(functools.partial(late_kernel, dims), [((frames, rows // 2, pair, wi...]
    ppermute x6 -> x17, waiting for transfers between devices: 6.6 us -> 16.5 us  [the longest x9 11.2 us: exchange(): return lax.ppermute(value, axes, [(i, i ^ mask) for i in range(size)])]
    mul x4 -> x0, other arithmetic: 4.95 us -> none  [the longest x1 1.99 us: local(): grad_conv = scale * summed[0]]
  transfers between devices with their start and end apart: 7 -> 17, of which waited for: 3 -> 10; matrix products, arithmetic and copies ran while one was open for 6% -> 2% of each run, Pallas kernels for 0% -> 11%
where the time goes in v2:
time: 59 us; the launch traced here: 58.7 us
  starting transfers between devices  25.8 us (44%)
  waiting for transfers between devices  16.5 us (28%)
  Pallas kernels  10.9 us (18%)
  local copies, waits for them, and re-layouts  3.53 us (6%)
  other arithmetic  1.16 us (2%)
  between operations  0.84 us (1%)
    ppermute x9, starting transfers between devices, exchange(): return lax.ppermute(value, axes, [(i, i ^ mask) for i in range(size)])  12 us
    ppermute x9, waiting for transfers between devices, exchange(): return lax.ppermute(value, axes, [(i, i ^ mask) for i in range(size)])  11.2 us
    ppermute x4, starting transfers between devices, swap_inner(): return lax.ppermute(value, 'core', [(0, 1), (1, 0)])  6.22 us
    ppermute x2, starting transfers between devices, along_tm(): return lax.ppermute(value, times, pairs)  6.17 us
    ppermute x2, waiting for transfers between devices, along_tm(): return lax.ppermute(value, times, pairs)  5.27 us
    unnamed x20, local copies, waits for them, and re-layouts  3.42 us
    pallas_call x1, Pallas kernels, local(): call(functools.partial(late_kernel, dims), [((frames, rows // 2, pair, wi...  3.19 us
    pallas_call x1, Pallas kernels, local(): call(functools.partial(main_kernel, dims), [((4, chunk, WIDTH), F32), ((4...  2.58 us
  transfers between devices with their start and end apart: 17, of which 10 were waited for; matrix products, arithmetic and copies ran while one was open for 2% of the time, Pallas kernels for 11%

profile of v2, /device:TPU:0, one launch (start us, length us, event | category | flops | bytes accessed | tf_op | source)
XLA Modules:
  0.0 58.7 jit_solution(16256539274630539599)
XLA Ops:
  0.6 4.9 %collective-permute-start = (bf16[48,1024]{1,0:T(8,128)(2,1)}, bf16[48,1024]{1,0:T(8,128)(2,1)S(1)}, u32[]{:S(2)}, u32[]{:S(2)}) collective-permute-start(bf16[48,1024]{1,0:T(8,128)(2,1)} %bitcast.38), channel_id=1, source_target_pairs={{0,16},{1,17},{2,18},{3,19},{4,20},{5,21},{6,22},{7,23},{8,24},{9,... | collective-permute-start | bytes 294920 | tf_op jit(solution)/shard_map/ppermute | solution.py:408
  5.6 2.4 %collective-permute-done.earlier = bf16[48,1024]{1,0:T(8,128)(2,1)S(1)} collective-permute-done((bf16[48,1024]{1,0:T(8,128)(2,1)}, bf16[48,1024]{1,0:T(8,128)(2,1)S(1)}, u32[]{:S(2)}, u32[]{:S(2)}) %collective-permute-start) | collective-permute-done | bytes 98336 | tf_op jit(solution)/shard_map/ppermute | solution.py:408
  10.3 1.0 %copy-done.2 = bf16[3,3,3,48,128]{4,3,2,1,0:T(8,128)(2,1)S(1)} copy-done((bf16[3,3,3,48,128]{4,3,2,1,0:T(8,128)(2,1)S(1)}, bf16[3,3,3,48,128]{4,3,2,1,0:T(8,128)(2,1)}, u32[]{:S(2)}) %copy-start.2) | copy-done | bytes 331800
  12.5 1.3 %shard_map.138 = (bf16[4,2,144,256]{3,2,1,0:T(8,128)(2,1)S(1)}, f32[2,2,128,256]{3,2,1,0:T(8,128)S(1)}, f32[2,512,128]{2,1,0:T(8,128)S(1)}) custom-call(bf16[48,1024]{1,0:T(8,128)(2,1)S(1)} %bitcast.40, bf16[48,1024]{1,0:T(8,128)(2,1)S(1)} %collective-permute-done.earlier, bf16[512,512]{1,0:T(8,128)(2,1)S(1)} %copy-done.7, bf16[192,192]{1,0:T(8,128)(2,1)S(1)} %copy-done.8, ...), custom_call_target="tpu_custom_call" | custom-call | flops 1000000000 | bytes 1048576 | tf_op jit(solution)/shard_map/pallas_call | solution.py:444
  13.9 2.6 %shard_map.139 = (f32[4,296,128]{2,1,0:T(8,128)S(1)}, bf16[4,296,128]{2,1,0:T(8,128)(2,1)S(1)}, bf16[2,512,128]{2,1,0:T(8,128)(2,1)S(1)}, bf16[256,512]{1,0:T(8,128)(2,1)S(1)}) custom-call(s32[2]{0:T(128)S(1)} %pad_add_fusion.place, bf16[48,1024]{1,0:T(8,128)(2,1)S(1)} %collective-permute-done.1.inner, bf16[48,1024]{1,0:T(8,128)(2,1)S(1)} %collective-permute-done.2.outer, ...), custom_call_target="tpu_custom_call" | custom-call | flops 1000000000 | bytes 1048576 | tf_op jit(solution)/shard_map/pallas_call | solution.py:457
  16.4 2.9 %collective-permute-start.3 = (bf16[4,296,128]{2,1,0:T(8,128)(2,1)S(1)}, bf16[4,296,128]{2,1,0:T(8,128)(2,1)S(1)}, u32[]{:S(2)}, u32[]{:S(2)}) collective-permute-start(bf16[4,296,128]{2,1,0:T(8,128)(2,1)S(1)} %get-tuple-element.43), channel_id=1, source_target_pairs={{0,1},{1,0},{2,3},{3,2},{4,5},{5,4},{6,7},{7,6},{8,9},{9,8},{10,11... | collective-permute-start | bytes 909320 | tf_op jit(solution)/shard_map/ppermute | solution.py:411
  20.1 3.2 %shard_map.140 = (bf16[2,1,128,256]{3,2,1,0:T(8,128)(2,1)}, f32[48,1024]{1,0:T(8,128)S(1)}, f32[48,1024]{1,0:T(8,128)S(1)}, bf16[48,1024]{1,0:T(8,128)(2,1)S(1)}, bf16[48,1024]{1,0:T(8,128)(2,1)S(1)}) custom-call(s32[2]{0:T(128)S(1)} %pad_add_fusion.place, bf16[2,512,128]{2,1,0:T(8,128)(2,1)S(1)} %get-tuple-element.38.acts, ...), custom_call_target="tpu_custom_call" | custom-call | flops 1000000000 | bytes 1048576 | tf_op jit(solution)/shard_map/pallas_call | solution.py:473
  23.9 3.1 %collective-permute-start.15 = (bf16[48,1024]{1,0:T(8,128)(2,1)S(1)}, bf16[48,1024]{1,0:T(8,128)(2,1)S(1)}, u32[]{:S(2)}, u32[]{:S(2)}) collective-permute-start(bf16[48,1024]{1,0:T(8,128)(2,1)S(1)} %get-tuple-element.54), channel_id=1, source_target_pairs={{0,1},{1,0},{2,3},{3,2},{4,5},{5,4},{6,7},{7,6},{8,9},{9,8},{10,11... | collective-permute-start | bytes 294920 | tf_op jit(solution)/shard_map/ppermute | solution.py:411
  27.2 1.7 %collective-permute-start.4 = (bf16[296,128]{1,0:T(8,128)(2,1)S(1)}, bf16[296,128]{1,0:T(8,128)(2,1)S(1)}, u32[]{:S(2)}, u32[]{:S(2)}) collective-permute-start(bf16[296,128]{1,0:T(8,128)(2,1)S(1)} %get-tuple-element.58), channel_id=1, source_target_pairs={{0,2},{2,0},{16,18},{18,16},{1,3},{3,1},{17,19},{19,17},{4,6},{6,4... | collective-permute-start | bytes 227336 | tf_op jit(solution)/shard_map/ppermute | solution.py:419
  28.9 2.1 %collective-permute-start.6 = (bf16[296,128]{1,0:T(8,128)(2,1)S(1)}, bf16[296,128]{1,0:T(8,128)(2,1)S(1)}, u32[]{:S(2)}, u32[]{:S(2)}) collective-permute-start(bf16[296,128]{1,0:T(8,128)(2,1)S(1)} %get-tuple-element.59), channel_id=1, source_target_pairs={{0,18},{2,16},{16,2},{18,0},{1,19},{3,17},{17,3},{19,1},{4,22},{6,... | collective-permute-start | bytes 227336 | tf_op jit(solution)/shard_map/ppermute | solution.py:419
  31.3 1.0 %collective-permute-done.4 = bf16[296,128]{1,0:T(8,128)(2,1)S(1)} collective-permute-done((bf16[296,128]{1,0:T(8,128)(2,1)S(1)}, bf16[296,128]{1,0:T(8,128)(2,1)S(1)}, u32[]{:S(2)}, u32[]{:S(2)}) %collective-permute-start.4) | collective-permute-done | bytes 75808 | tf_op jit(solution)/shard_map/ppermute | solution.py:419
  32.3 1.9 %collective-permute-done.6 = bf16[296,128]{1,0:T(8,128)(2,1)S(1)} collective-permute-done((bf16[296,128]{1,0:T(8,128)(2,1)S(1)}, bf16[296,128]{1,0:T(8,128)(2,1)S(1)}, u32[]{:S(2)}, u32[]{:S(2)}) %collective-permute-start.6) | collective-permute-done | bytes 75808 | tf_op jit(solution)/shard_map/ppermute | solution.py:419
  34.2 1.2 %collective-permute-done.5 = bf16[296,128]{1,0:T(8,128)(2,1)S(1)} collective-permute-done((bf16[296,128]{1,0:T(8,128)(2,1)S(1)}, bf16[296,128]{1,0:T(8,128)(2,1)S(1)}, u32[]{:S(2)}, u32[]{:S(2)}) %collective-permute-start.5) | collective-permute-done | bytes 75808 | tf_op jit(solution)/shard_map/ppermute | solution.py:419
  35.4 3.1 %collective-permute-start.9 = (bf16[296,128]{1,0:T(8,128)(2,1)S(1)}, bf16[296,128]{1,0:T(8,128)(2,1)S(1)}, u32[]{:S(2)}, u32[]{:S(2)}) collective-permute-start(bf16[296,128]{1,0:T(8,128)(2,1)S(1)} %fusion.3), channel_id=1, source_target_pairs={{0,12},{4,8},{8,4},{12,0},{1,13},{5,9},{9,5},{13,1},{2,14},{6,10},... | collective-permute-start | bytes 227336 | tf_op jit(solution)/shard_map/ppermute | solution.py:419
  38.5 1.3 %collective-permute-start.7 = (bf16[296,128]{1,0:T(8,128)(2,1)S(1)}, bf16[296,128]{1,0:T(8,128)(2,1)S(1)}, u32[]{:S(2)}, u32[]{:S(2)}) collective-permute-start(bf16[296,128]{1,0:T(8,128)(2,1)S(1)} %fusion.3), channel_id=1, source_target_pairs={{0,4},{4,0},{8,12},{12,8},{1,5},{5,1},{9,13},{13,9},{2,6},{6,2},{1... | collective-permute-start | bytes 227336 | tf_op jit(solution)/shard_map/ppermute | solution.py:419
  40.0 2.0 %collective-permute-done.9 = bf16[296,128]{1,0:T(8,128)(2,1)S(1)} collective-permute-done((bf16[296,128]{1,0:T(8,128)(2,1)S(1)}, bf16[296,128]{1,0:T(8,128)(2,1)S(1)}, u32[]{:S(2)}, u32[]{:S(2)}) %collective-permute-start.9) | collective-permute-done | bytes 75808 | tf_op jit(solution)/shard_map/ppermute | solution.py:419
  42.0 3.0 %collective-permute-done.8 = bf16[296,128]{1,0:T(8,128)(2,1)S(1)} collective-permute-done((bf16[296,128]{1,0:T(8,128)(2,1)S(1)}, bf16[296,128]{1,0:T(8,128)(2,1)S(1)}, u32[]{:S(2)}, u32[]{:S(2)}) %collective-permute-start.8) | collective-permute-done | bytes 75808 | tf_op jit(solution)/shard_map/ppermute | solution.py:419
  45.0 2.4 %collective-permute-start.12 = (bf16[296,128]{1,0:T(8,128)(2,1)S(1)}, bf16[296,128]{1,0:T(8,128)(2,1)S(1)}, u32[]{:S(2)}, u32[]{:S(2)}) collective-permute-start(bf16[296,128]{1,0:T(8,128)(2,1)S(1)} %add_convert_fusion.refs_0_), channel_id=1, source_target_pairs={{0,18},{2,16},{16,2},{18,0},{1,19},{3,17},{17,3},{19,1},{4,22},{6,... | collective-permute-start | bytes 227336 | tf_op jit(solution)/shard_map/ppermute | solution.py:419
  48.6 1.3 %collective-permute-start.16 = (bf16[6,8,1024]{2,1,0:T(8,128)(2,1)S(1)}, bf16[6,8,1024]{2,1,0:T(8,128)(2,1)S(1)}, u32[]{:S(2)}, u32[]{:S(2)}) collective-permute-start(bf16[6,8,1024]{2,1,0:T(8,128)(2,1)S(1)} %fusion), channel_id=1, source_target_pairs={{16,0},{17,1},{18,2},{19,3},{20,4},{21,5},{22,6},{23,7},{24,8},{25... | collective-permute-start | bytes 294920 | tf_op jit(solution)/shard_map/ppermute | solution.py:408
  49.9 1.0 %collective-permute-done.12.refs_3_ = bf16[296,128]{1,0:T(8,128)(2,1)S(1)} collective-permute-done((bf16[296,128]{1,0:T(8,128)(2,1)S(1)}, bf16[296,128]{1,0:T(8,128)(2,1)S(1)}, u32[]{:S(2)}, u32[]{:S(2)}) %collective-permute-start.12) | collective-permute-done | bytes 75808 | tf_op jit(solution)/shard_map/ppermute | solution.py:419
  50.9 0.9 %collective-permute-done.11.refs_2_ = bf16[296,128]{1,0:T(8,128)(2,1)S(1)} collective-permute-done((bf16[296,128]{1,0:T(8,128)(2,1)S(1)}, bf16[296,128]{1,0:T(8,128)(2,1)S(1)}, u32[]{:S(2)}, u32[]{:S(2)}) %collective-permute-start.11) | collective-permute-done | bytes 75808 | tf_op jit(solution)/shard_map/ppermute | solution.py:419
  52.3 2.9 %collective-permute-done.16 = bf16[6,8,1024]{2,1,0:T(8,128)(2,1)S(1)} collective-permute-done((bf16[6,8,1024]{2,1,0:T(8,128)(2,1)S(1)}, bf16[6,8,1024]{2,1,0:T(8,128)(2,1)S(1)}, u32[]{:S(2)}, u32[]{:S(2)}) %collective-permute-start.16) | collective-permute-done | bytes 98336 | tf_op jit(solution)/shard_map/ppermute | solution.py:408
  55.8 1.4 %shard_map.141 = (f32[1296,128]{1,0:T(8,128)}, f32[1,128]{1,0:T(1,128)}, f32[512,256]{1,0:T(8,128)}, f32[1,256]{1,0:T(1,128)}) custom-call(s32[2]{0:T(128)S(1)} %pad_add_fusion.place, bf16[296,128]{1,0:T(8,128)(2,1)S(1)} %add_convert_fusion.refs_0_, bf16[296,128]{1,0:T(8,128)(2,1)S(1)} %collective-permute-done.10.refs_1_, ...), custom_call_target="tpu_custom_call" | custom-call | bytes 1048576 | tf_op jit(solution)/shard_map/pallas_call | solution.py:521
  57.3 1.4 %shard_map.142 = (f32[1296,128]{1,0:T(8,128)}, f32[1,128]{1,0:T(1,128)}, f32[512,256]{1,0:T(8,128)}, f32[1,256]{1,0:T(1,128)}) custom-call(s32[2]{0:T(128)S(1)} %pad_add_fusion.place, bf16[4,296,128]{2,1,0:T(8,128)(2,1)S(1)} %collective-permute-done.13.refs_0_, ...), custom_call_target="tpu_custom_call", output_to_operand_aliasing={{0}: (2, {}), {1}: (3, {}), {2}: (4, {}), {3}: (5, {})} | custom-call | bytes 1048576 | tf_op jit(solution)/shard_map/pallas_call | solution.py:528
  (49 shorter events, 7.9 us)
Async XLA Ops:
  0.6 7.4 %collective-permute-start = (bf16[48,1024]{1,0:T(8,128)(2,1)}, bf16[48,1024]{1,0:T(8,128)(2,1)S(1)}, u32[]{:S(2)}, u32[]{:S(2)}) collective-permute-start(bf16[48,1024]{1,0:T(8,128)(2,1)} %bitcast.38), channel_id=1, source_target_pairs={{0,16},{1,17},{2,18},{3,19},{4,20},{5,21},{6,22},{7,23},{8,24},{9,... | collective-permute-start | bytes 294920 | tf_op jit(solution)/shard_map/ppermute | solution.py:408
  8.0 0.9 %copy-start = (bf16[2,3,8,1024]{3,2,1,0:T(8,128)(2,1)S(1)}, bf16[2,3,8,1024]{3,2,1,0:T(8,128)(2,1)}, u32[]{:S(2)}) copy-start(bf16[2,3,8,1024]{3,2,1,0:T(8,128)(2,1)} %param.9) | copy-start | bytes 294916
  9.5 4.3 %collective-permute-start.1 = (bf16[48,1024]{1,0:T(8,128)(2,1)S(1)}, bf16[48,1024]{1,0:T(8,128)(2,1)S(1)}, u32[]{:S(2)}, u32[]{:S(2)}) collective-permute-start(bf16[48,1024]{1,0:T(8,128)(2,1)S(1)} %get-tuple-element.31), channel_id=1, source_target_pairs={{0,1},{1,0},{2,3},{3,2},{4,5},{5,4},{6,7},{7,6},{8,9},{9,8},{10,11... | collective-permute-start | bytes 294920 | tf_op jit(solution)/shard_map/ppermute | solution.py:411
  9.6 4.2 %collective-permute-start.2 = (bf16[48,1024]{1,0:T(8,128)(2,1)S(1)}, bf16[48,1024]{1,0:T(8,128)(2,1)S(1)}, u32[]{:S(2)}, u32[]{:S(2)}) collective-permute-start(bf16[48,1024]{1,0:T(8,128)(2,1)S(1)} %get-tuple-element.32), channel_id=1, source_target_pairs={{1,2},{3,4},{5,6},{7,8},{9,10},{11,12},{13,14},{2,1},{4,3},{6,5},{... | collective-permute-start | bytes 294920 | tf_op jit(solution)/shard_map/ppermute | solution.py:415
  10.3 1.0 %copy-start.2 = (bf16[3,3,3,48,128]{4,3,2,1,0:T(8,128)(2,1)S(1)}, bf16[3,3,3,48,128]{4,3,2,1,0:T(8,128)(2,1)}, u32[]{:S(2)}) copy-start(bf16[3,3,3,48,128]{4,3,2,1,0:T(8,128)(2,1)} %param.10) | copy-start | bytes 995332
  11.3 1.0 %copy-start.3 = (bf16[2,2,128,256]{3,2,1,0:T(8,128)(2,1)S(1)}, bf16[2,2,128,256]{3,2,1,0:T(8,128)(2,1)}, u32[]{:S(2)}) copy-start(bf16[2,2,128,256]{3,2,1,0:T(8,128)(2,1)} %param.12) | copy-start | bytes 786436
  11.3 1.0 %copy-start.4 = (bf16[2,1,128,256]{3,2,1,0:T(8,128)(2,1)S(1)}, bf16[2,1,128,256]{3,2,1,0:T(8,128)(2,1)}, u32[]{:S(2)}) copy-start(bf16[2,1,128,256]{3,2,1,0:T(8,128)(2,1)} %cotangent.3) | copy-start | bytes 393220
  11.3 1.2 %copy-start.7 = (bf16[512,512]{1,0:T(8,128)(2,1)S(1)}, bf16[512,512]{1,0:T(8,128)(2,1)}, u32[]{:S(2)}) copy-start(bf16[512,512]{1,0:T(8,128)(2,1)} %constant.20.clone.table) | copy-start | bytes 1572868
  11.3 1.2 %copy-start.8 = (bf16[192,192]{1,0:T(8,128)(2,1)S(1)}, bf16[192,192]{1,0:T(8,128)(2,1)}, u32[]{:S(2)}) copy-start(bf16[192,192]{1,0:T(8,128)(2,1)} %constant.21.clone.rows_own) | copy-start | bytes 221188
  12.5 1.3 %copy-start.9 = (bf16[192,192]{1,0:T(8,128)(2,1)S(1)}, bf16[192,192]{1,0:T(8,128)(2,1)}, u32[]{:S(2)}) copy-start(bf16[192,192]{1,0:T(8,128)(2,1)} %constant.22.clone.rows_halo) | copy-start | bytes 221188
  16.4 10.6 %collective-permute-start.3 = (bf16[4,296,128]{2,1,0:T(8,128)(2,1)S(1)}, bf16[4,296,128]{2,1,0:T(8,128)(2,1)S(1)}, u32[]{:S(2)}, u32[]{:S(2)}) collective-permute-start(bf16[4,296,128]{2,1,0:T(8,128)(2,1)S(1)} %get-tuple-element.43), channel_id=1, source_target_pairs={{0,1},{1,0},{2,3},{3,2},{4,5},{5,4},{6,7},{7,6},{8,9},{9,8},{10,11... | collective-permute-start | bytes 909320 | tf_op jit(solution)/shard_map/ppermute | solution.py:411
  23.3 8.0 %collective-permute-start.14 = (bf16[48,1024]{1,0:T(8,128)(2,1)S(1)}, bf16[48,1024]{1,0:T(8,128)(2,1)S(1)}, u32[]{:S(2)}, u32[]{:S(2)}) collective-permute-start(bf16[48,1024]{1,0:T(8,128)(2,1)S(1)} %get-tuple-element.53), channel_id=1, source_target_pairs={{1,2},{3,4},{5,6},{7,8},{9,10},{11,12},{13,14},{2,1},{4,3},{6,5},{... | collective-permute-start | bytes 294920 | tf_op jit(solution)/shard_map/ppermute | solution.py:415
  23.9 7.3 %collective-permute-start.15 = (bf16[48,1024]{1,0:T(8,128)(2,1)S(1)}, bf16[48,1024]{1,0:T(8,128)(2,1)S(1)}, u32[]{:S(2)}, u32[]{:S(2)}) collective-permute-start(bf16[48,1024]{1,0:T(8,128)(2,1)S(1)} %get-tuple-element.54), channel_id=1, source_target_pairs={{0,1},{1,0},{2,3},{3,2},{4,5},{5,4},{6,7},{7,6},{8,9},{9,8},{10,11... | collective-permute-start | bytes 294920 | tf_op jit(solution)/shard_map/ppermute | solution.py:411
  27.2 5.2 %collective-permute-start.4 = (bf16[296,128]{1,0:T(8,128)(2,1)S(1)}, bf16[296,128]{1,0:T(8,128)(2,1)S(1)}, u32[]{:S(2)}, u32[]{:S(2)}) collective-permute-start(bf16[296,128]{1,0:T(8,128)(2,1)S(1)} %get-tuple-element.58), channel_id=1, source_target_pairs={{0,2},{2,0},{16,18},{18,16},{1,3},{3,1},{17,19},{19,17},{4,6},{6,4... | collective-permute-start | bytes 227336 | tf_op jit(solution)/shard_map/ppermute | solution.py:419
  28.9 5.3 %collective-permute-start.6 = (bf16[296,128]{1,0:T(8,128)(2,1)S(1)}, bf16[296,128]{1,0:T(8,128)(2,1)S(1)}, u32[]{:S(2)}, u32[]{:S(2)}) collective-permute-start(bf16[296,128]{1,0:T(8,128)(2,1)S(1)} %get-tuple-element.59), channel_id=1, source_target_pairs={{0,18},{2,16},{16,2},{18,0},{1,19},{3,17},{17,3},{19,1},{4,22},{6,... | collective-permute-start | bytes 227336 | tf_op jit(solution)/shard_map/ppermute | solution.py:419
  31.0 4.4 %collective-permute-start.5 = (bf16[296,128]{1,0:T(8,128)(2,1)S(1)}, bf16[296,128]{1,0:T(8,128)(2,1)S(1)}, u32[]{:S(2)}, u32[]{:S(2)}) collective-permute-start(bf16[296,128]{1,0:T(8,128)(2,1)S(1)} %get-tuple-element.60), channel_id=1, source_target_pairs={{0,16},{2,18},{16,0},{18,2},{1,17},{3,19},{17,1},{19,3},{4,20},{6,... | collective-permute-start | bytes 227336 | tf_op jit(solution)/shard_map/ppermute | solution.py:419
  35.4 6.5 %collective-permute-start.9 = (bf16[296,128]{1,0:T(8,128)(2,1)S(1)}, bf16[296,128]{1,0:T(8,128)(2,1)S(1)}, u32[]{:S(2)}, u32[]{:S(2)}) collective-permute-start(bf16[296,128]{1,0:T(8,128)(2,1)S(1)} %fusion.3), channel_id=1, source_target_pairs={{0,12},{4,8},{8,4},{12,0},{1,13},{5,9},{9,5},{13,1},{2,14},{6,10},... | collective-permute-start | bytes 227336 | tf_op jit(solution)/shard_map/ppermute | solution.py:419
  38.5 6.4 %collective-permute-start.8 = (bf16[296,128]{1,0:T(8,128)(2,1)S(1)}, bf16[296,128]{1,0:T(8,128)(2,1)S(1)}, u32[]{:S(2)}, u32[]{:S(2)}) collective-permute-start(bf16[296,128]{1,0:T(8,128)(2,1)S(1)} %fusion.3), channel_id=1, source_target_pairs={{0,8},{4,12},{8,0},{12,4},{1,9},{5,13},{9,1},{13,5},{2,10},{6,14},... | collective-permute-start | bytes 227336 | tf_op jit(solution)/shard_map/ppermute | solution.py:419
  38.5 6.4 %collective-permute-start.7 = (bf16[296,128]{1,0:T(8,128)(2,1)S(1)}, bf16[296,128]{1,0:T(8,128)(2,1)S(1)}, u32[]{:S(2)}, u32[]{:S(2)}) collective-permute-start(bf16[296,128]{1,0:T(8,128)(2,1)S(1)} %fusion.3), channel_id=1, source_target_pairs={{0,4},{4,0},{8,12},{12,8},{1,5},{5,1},{9,13},{13,9},{2,6},{6,2},{1... | collective-permute-start | bytes 227336 | tf_op jit(solution)/shard_map/ppermute | solution.py:419
  45.0 5.8 %collective-permute-start.12 = (bf16[296,128]{1,0:T(8,128)(2,1)S(1)}, bf16[296,128]{1,0:T(8,128)(2,1)S(1)}, u32[]{:S(2)}, u32[]{:S(2)}) collective-permute-start(bf16[296,128]{1,0:T(8,128)(2,1)S(1)} %add_convert_fusion.refs_0_), channel_id=1, source_target_pairs={{0,18},{2,16},{16,2},{18,0},{1,19},{3,17},{17,3},{19,1},{4,22},{6,... | collective-permute-start | bytes 227336 | tf_op jit(solution)/shard_map/ppermute | solution.py:419
  47.4 4.4 %collective-permute-start.11 = (bf16[296,128]{1,0:T(8,128)(2,1)S(1)}, bf16[296,128]{1,0:T(8,128)(2,1)S(1)}, u32[]{:S(2)}, u32[]{:S(2)}) collective-permute-start(bf16[296,128]{1,0:T(8,128)(2,1)S(1)} %add_convert_fusion.refs_0_), channel_id=1, source_target_pairs={{0,16},{2,18},{16,0},{18,2},{1,17},{3,19},{17,1},{19,3},{4,20},{6,... | collective-permute-start | bytes 227336 | tf_op jit(solution)/shard_map/ppermute | solution.py:419
  47.8 4.4 %collective-permute-start.10 = (bf16[296,128]{1,0:T(8,128)(2,1)S(1)}, bf16[296,128]{1,0:T(8,128)(2,1)S(1)}, u32[]{:S(2)}, u32[]{:S(2)}) collective-permute-start(bf16[296,128]{1,0:T(8,128)(2,1)S(1)} %add_convert_fusion.refs_0_), channel_id=1, source_target_pairs={{0,2},{2,0},{16,18},{18,16},{1,3},{3,1},{17,19},{19,17},{4,6},{6,4... | collective-permute-start | bytes 227336 | tf_op jit(solution)/shard_map/ppermute | solution.py:419
  48.6 6.5 %collective-permute-start.16 = (bf16[6,8,1024]{2,1,0:T(8,128)(2,1)S(1)}, bf16[6,8,1024]{2,1,0:T(8,128)(2,1)S(1)}, u32[]{:S(2)}, u32[]{:S(2)}) collective-permute-start(bf16[6,8,1024]{2,1,0:T(8,128)(2,1)S(1)} %fusion), channel_id=1, source_target_pairs={{16,0},{17,1},{18,2},{19,3},{20,4},{21,5},{22,6},{23,7},{24,8},{25... | collective-permute-start | bytes 294920 | tf_op jit(solution)/shard_map/ppermute | solution.py:408
  52.2 5.1 %collective-permute-start.13 = (bf16[4,296,128]{2,1,0:T(8,128)(2,1)S(1)}, bf16[4,296,128]{2,1,0:T(8,128)(2,1)S(1)}, u32[]{:S(2)}, u32[]{:S(2)}) collective-permute-start(bf16[4,296,128]{2,1,0:T(8,128)(2,1)S(1)} %pad_maximum_fusion), channel_id=1, source_target_pairs={{0,1},{1,0},{2,3},{3,2},{4,5},{5,4},{6,7},{7,6},{8,9},{9,8},{10,11... | collective-permute-start | bytes 909320 | tf_op jit(solution)/shard_map/ppermute | solution.py:411
  (3 other events, 2.4 us)

commit v3 on v2

--- a/solution.py
+++ b/solution.py
@@ -13,8 +13,7 @@
 BF16, F32 = jnp.bfloat16, jnp.float32
 HAAR = np.kron(np.array([[1.0, 1.0], [1.0, -1.0]]), np.array([[1.0, 1.0], [1.0, -1.0]])) * 0.5
 VMEM = pl.BlockSpec(memory_space=pltpu.VMEM)
-SMEM = pl.BlockSpec(memory_space=pltpu.SMEM)
-ANY = pl.BlockSpec(memory_space=pl.ANY)
+HBM = pl.BlockSpec(memory_space=pltpu.HBM)
 NN = (((1,), (0,)), ((), ()))
 NT = (((1,), (1,)), ((), ()))
 COLORS, CH, WIDTH = 3, 48, 128
@@ -28,6 +27,10 @@
 def split(x):
     high = x.astype(BF16)
     return high, (x - high.astype(F32)).astype(BF16)
+
+
+def position():
+    return lax.axis_index("core"), 2 * lax.axis_index("tm_lo") + lax.axis_index("y")
 
 
 def call(body, outs, ins, scratch=(), flops=0, grant=24, **more):
@@ -60,6 +63,18 @@
                 for j in range(4):
                     table[f, r, k, :, j, j, f, k, r, :] = HAAR
     return table.reshape(frames * rows * CH, 4 * frames * COLORS * rows * 4)
+
+
+def choose_table(frames, rows):
+    table = np.zeros((2, 2, frames + 2, COLORS, 4, frames + 2, COLORS, 4 * rows), np.float32)
+    for core in range(2):
+        for way in range(2):
+            at = 4 * rows - 4 if core == way else 0
+            for f in range(frames + 2):
+                for k in range(COLORS):
+                    for u in range(4):
+                        table[core, way, f, k, u, f, k, at + u] = 1.0
+    return table.reshape(2, 2 * (frames + 2) * COLORS * 4, (frames + 2) * COLORS * 4 * rows)
 
 
 def shifts(pair):
@@ -125,33 +140,43 @@
     ]
 
 
-def weights_kernel(weight, inside, outside, backward):
+def first_kernel(dims, count, *refs):
+    frames, rows, pair = dims
+    sources, targets = refs[:count], refs[count : 2 * count - 1]
+    inside, outside, backward, x, dact, raw, sems = refs[2 * count - 1 :]
+    copies = [
+        pltpu.make_async_copy(source, target, sems.at[n])
+        for n, (source, target) in enumerate(zip(sources, (raw, *targets)))
+    ]
+    for copy in copies:
+        copy.start()
+    own, table, rows_own, down_weight, cotangent = targets[:5]
+    copies[0].wait()
     for a in range(3):
         for b in range(3):
             for d in range(3):
-                at = CH * (3 * a + b)
-                backward[at : at + CH, WIDTH * d : WIDTH * (d + 1)] = weight[9 * a + 3 * b + d]
-        taps = weight[9 * a : 9 * a + 9].reshape(3 * TAPS, WIDTH).astype(F32)
+                at = CH * (3 * b + a)
+                backward[at : at + CH, WIDTH * d : WIDTH * (d + 1)] = raw[9 * a + 3 * b + d]
+        taps = raw[9 * a : 9 * a + 9].reshape(3 * TAPS, WIDTH).astype(F32)
         at = slice(WIDTH * a, WIDTH * (a + 1))
         inside[0, at] = taps[TAPS:].T.astype(BF16)
         inside[1, at] = taps[: 2 * TAPS].T.astype(BF16)
         outside[0, at] = taps[:TAPS].T.astype(BF16)
         outside[1, at] = taps[2 * TAPS :].T.astype(BF16)
-
-
-def pack_kernel(dims, place, own, earlier, inner, outer):
-    frames, rows, _ = dims
-    core = place[0]
-    at = 0
-    for part, count in ((earlier, 2), (own, frames)):
-        count *= COLORS
-        pixels = part[...].astype(F32).reshape(count, 4 * rows, part.shape[1])
-        top, bottom = pixels[:, :4], pixels[:, 4 * rows - 4 :]
-        size = 4 * count
-        for target, first, second in ((inner, bottom, top), (outer, top, bottom)):
-            chosen = jnp.where(core == 0, first, second)
-            target[at : at + size] = chosen.reshape(size, part.shape[1]).astype(BF16)
-        at += size
+    for copy in copies[1:]:
+        copy.wait()
+    where = [(f, r) for f in range(frames) for r in range(rows)]
+    analyse([own[...]], table, [rows_own], x, [where], pair)
+    for f in range(frames):
+        dact[f] = mm(down_weight[...], cotangent[f, 0], NT)
+
+
+def pack_kernel(own, earlier, chosen, inner, outer):
+    core, _ = position()
+    both = mm(chosen[core], jnp.concatenate([earlier[...], own[...]], axis=0)).astype(BF16)
+    size = inner.shape[0]
+    inner[...] = both[:size]
+    outer[...] = both[size:]
 
 
 def taps_of(frame, frames):
@@ -168,35 +193,28 @@
         total[f] = here if total[f] is None else total[f] + here
 
 
-def early_kernel(
-    dims, own, earlier, table, rows_own, inside, conv_bias, down_weight, cotangent, x, pre, dact
-):
+def early_kernel(dims, earlier, table, rows_own, inside, conv_bias, x_own, x, pre):
     frames, rows, pair = dims
-    places = [
-        [(f, r) for f in range(2) for r in range(rows)],
-        [(2 + f, r) for f in range(frames) for r in range(rows)],
-    ]
-    analyse([earlier[...], own[...]], table, [rows_own, rows_own], x, places, pair)
+    where = [(f, r) for f in range(2) for r in range(rows)]
+    analyse([earlier[...]], table, [rows_own], x, [where], pair)
     bias = jnp.broadcast_to(conv_bias[...], (WIDTH, WIDTH)).T
     bias = jnp.concatenate([bias] * (2 * pair // WIDTH), axis=1)
     for r in range(rows):
         total = [bias] * frames
         for frame in range(frames + 2):
-            values = x[frame].reshape(rows * TAPS, 2 * pair)
+            values = (x[frame] if frame < 2 else x_own[frame - 2]).reshape(rows * TAPS, 2 * pair)
             convolve(total, inside[r], values, frame, frames)
         for f in range(frames):
             pre[f, r] = total[f]
-    for f in range(frames):
-        dact[f] = mm(down_weight[...], cotangent[f, 0], NT)
 
 
 def main_kernel(
     dims,
-    place,
     inner,
     outer,
     table,
     rows_halo,
+    x_early,
     x_own,
     pre_own,
     dact,
@@ -210,11 +228,11 @@
     packed,
 ):
     frames, rows, pair = dims
-    core, plane = place[0], place[1]
+    core, plane = position()
     inner_row = jnp.where(core == 0, rows + 1, 0)
     outer_row = jnp.where(core == 0, 0, rows + 1)
     for frame in range(frames + 2):
-        x[frame, 1 : rows + 1] = x_own[frame]
+        x[frame, 1 : rows + 1] = x_early[frame] if frame < 2 else x_own[frame - 2]
     places = [
         [(f, inner_row) for f in range(frames + 2)],
         [(f, outer_row) for f in range(frames + 2)],
@@ -282,9 +300,49 @@
         give[m] = packed[1 - core, pl.ds(at, chunk)].astype(BF16)
 
 
+def shifted_slope(slopes, f, r, pair):
+    left, right = shifts(pair)
+    slope = slopes[WIDTH * f : WIDTH * (f + 1), 2 * pair * r : 2 * pair * (r + 1)]
+    even, odd = slope[:, :pair].astype(F32), slope[:, pair:].astype(F32)
+    return jnp.concatenate(
+        [
+            jnp.concatenate([odd, left(even)], axis=1).astype(BF16),
+            slope,
+            jnp.concatenate([right(odd), even], axis=1).astype(BF16),
+        ],
+        axis=0,
+    )
+
+
+def spread_slope(total, slopes, backward, frames, reach, pair):
+    for f in range(frames):
+        for r in sorted({r for r, _, _ in reach}):
+            taps = [(b, row) for here, b, row in reach if here == r]
+            first, last = min(taps)[0], max(taps)[0]
+            part = mm(backward[TAPS * first : TAPS * (last + 1)], shifted_slope(slopes, f, r, pair))
+            for b, row in taps:
+                for a in range(3):
+                    at = TAPS * (b - first) + CH * a
+                    here = part[at : at + CH]
+                    key = (f + a, row)
+                    total[key] = here if key not in total else total[key] + here
+
+
+def edge_kernel(dims, slopes, backward, table, rows_halo, send_inner, send_outer):
+    frames, rows, pair = dims
+    core, _ = position()
+    total = {}
+    spread_slope(total, slopes, backward, frames, [(0, 0, 0), (rows - 1, 2, 1)], pair)
+    groups = [
+        jnp.concatenate([total[frame, row] for frame in range(frames + 2)], axis=0) for row in range(2)
+    ]
+    above, below = synthesise(groups, table, [rows_halo, rows_halo], pair)
+    send_inner[...] = jnp.where(core == 0, below, above).astype(BF16)
+    send_outer[...] = jnp.where(core == 0, above, below).astype(BF16)
+
+
 def late_kernel(
     dims,
-    place,
     acts,
     slopes,
     backward,
@@ -292,53 +350,19 @@
     down_bias,
     table,
     rows_own,
-    rows_halo,
     features,
     pixels_own,
     pixels_early,
-    send_inner,
-    send_outer,
-    spread,
 ):
     frames, rows, pair = dims
-    core = place[0]
-    inner_row = jnp.where(core == 0, rows + 1, 0)
-    outer_row = jnp.where(core == 0, 0, rows + 1)
-    left, right = shifts(pair)
-    spread[...] = jnp.zeros_like(spread)
-    for f in range(frames):
-        for r in range(rows):
-            slope = slopes[WIDTH * f : WIDTH * (f + 1), 2 * pair * r : 2 * pair * (r + 1)]
-            even, odd = slope[:, :pair].astype(F32), slope[:, pair:].astype(F32)
-            shifted = jnp.concatenate(
-                [
-                    jnp.concatenate([odd, left(even)], axis=1).astype(BF16),
-                    slope,
-                    jnp.concatenate([right(odd), even], axis=1).astype(BF16),
-                ],
-                axis=0,
-            )
-            reach = mm(backward[...], shifted)
-            for a in range(3):
-                for b in range(3):
-                    at = CH * (3 * a + b)
-                    spread[f + a, r + b] += reach[at : at + CH]
-
-    def rows_of(blocks):
-        return jnp.concatenate([spread[f, r] for f, r in blocks], axis=0)
-
+    total = {}
+    reach = [(r, b, r + b - 1) for r in range(rows) for b in range(3) if 0 <= r + b - 1 < rows]
+    spread_slope(total, slopes, backward, frames, reach, pair)
     groups = [
-        rows_of([(f, 1 + r) for f in range(2) for r in range(rows)]),
-        rows_of([(2 + f, 1 + r) for f in range(frames) for r in range(rows)]),
-        rows_of([(f, inner_row) for f in range(frames + 2)]),
-        rows_of([(f, outer_row) for f in range(frames + 2)]),
-    ]
-    tables = [rows_own, rows_own, rows_halo, rows_halo]
-    early, own, inner, outer = synthesise(groups, table, tables, pair)
-    pixels_early[...] = early
-    pixels_own[...] = own
-    send_inner[...] = inner.astype(BF16)
-    send_outer[...] = outer.astype(BF16)
+        jnp.concatenate([total[first + f, r] for f in range(frames) for r in range(rows)], axis=0)
+        for first in (0, 2)
+    ]
+    pixels_early[...], pixels_own[...] = synthesise(groups, table, [rows_own, rows_own], pair)
     for f in range(frames):
         turned = jnp.concatenate(
             [acts[f, WIDTH * n : WIDTH * (n + 1)].astype(F32).T.astype(BF16) for n in range(4)], axis=1
@@ -346,11 +370,11 @@
         features[f, 0] = (mm(turned, down_weight[...]) + down_bias[...]).astype(BF16)
 
 
-def finish_kernel(scale, other, place, *refs):
+def finish_kernel(scale, other, *refs):
     pieces, (conv, conv_bias, down, down_bias, flat, sums, sems) = refs[:4], refs[-7:]
     if other:
         pieces = [refs[0].at[m] for m in range(4)]
-    core, plane = place[0], place[1]
+    core, plane = position()
     which = 1 - core if other else core
     chunk = pieces[0].shape[0]
     for m in range(4):
@@ -398,8 +422,6 @@
     pair = columns // 2
     width2 = down_weight.shape[3]
     core = lax.axis_index("core")
-    plane = 2 * lax.axis_index("tm_lo") + lax.axis_index("y")
-    place = jnp.stack([core, plane]).astype(jnp.int32)
     count_tm, count_height = lax.axis_size(times), lax.axis_size(heights)
     dims = (frames, rows, pair)
 
@@ -418,39 +440,48 @@
         size = lax.axis_size(axes)
         return lax.ppermute(value, axes, [(i, i ^ mask) for i in range(size)])
 
-    table = jnp.asarray(column_table(pair // 2), BF16)
-    rows_own = jnp.asarray(row_table(frames, rows), BF16)
-    rows_halo = jnp.asarray(row_table(frames + 2, 1), BF16)
-
     own = pixels.reshape(frames * colors * pixel_rows, pixel_columns)
     earlier = along_tm(own, 1)
-    inside, outside, backward = call(
-        weights_kernel,
-        [((2, 3 * WIDTH, 2 * TAPS), BF16), ((2, 3 * WIDTH, TAPS), BF16), ((9 * CH, 3 * WIDTH), BF16)],
-        [VMEM],
+    flat_halo = ((frames + 2) * colors * 4, pixel_columns)
+    frame_shape = (2 * colors, pixel_rows, pixel_columns)
+    sources = [
+        conv_weight.reshape(27, CH, WIDTH),
+        own,
+        jnp.asarray(column_table(pair // 2), BF16),
+        jnp.asarray(row_table(frames, rows), BF16),
+        down_weight.reshape(4 * WIDTH, width2),
+        cotangent,
+        jnp.asarray(row_table(frames + 2, 1), BF16),
+        jnp.asarray(choose_table(frames, rows), BF16),
+        conv_bias.reshape(1, WIDTH),
+        down_bias.reshape(1, width2),
+    ]
+    outs = call(
+        functools.partial(first_kernel, dims, len(sources)),
+        [(source.shape, source.dtype) for source in sources[1:]]
+        + [
+            ((2, 3 * WIDTH, 2 * TAPS), BF16),
+            ((2, 3 * WIDTH, TAPS), BF16),
+            ((9 * CH, 3 * WIDTH), BF16),
+            ((frames, rows, TAPS, columns), BF16),
+            ((frames, 4 * WIDTH, pair), F32),
+        ],
+        [HBM] * len(sources),
+        [pltpu.VMEM((27, CH, WIDTH), BF16), pltpu.SemaphoreType.DMA((len(sources),))],
         flops=10**9,
-    )(conv_weight.reshape(27, CH, WIDTH))
-    frame_shape = (2 * colors, pixel_rows, pixel_columns)
-    flat_halo = ((frames + 2) * colors * 4, pixel_columns)
-    send_inner, send_outer = call(
-        functools.partial(pack_kernel, dims),
-        [(flat_halo, BF16), (flat_halo, BF16)],
-        [SMEM, VMEM, VMEM],
-    )(place, own, earlier)
+    )(*(pltpu.with_memory_space_constraint(source, pltpu.HBM) for source in sources))
+    own, table, rows_own, down_flat, cot, rows_halo, chosen, bias, bias2 = outs[:9]
+    inside, outside, backward, x_own, dact = outs[9:]
+    send_inner, send_outer = call(pack_kernel, [(flat_halo, BF16), (flat_halo, BF16)], [VMEM] * 3)(own, earlier, chosen)
     inner = swap_inner(send_inner)
     outer = swap_outer(send_outer)
 
-    down_flat = down_weight.reshape(4 * WIDTH, width2)
-    x_own, pre_own, dact = call(
+    x_early, pre_own = call(
         functools.partial(early_kernel, dims),
-        [
-            ((frames + 2, rows, TAPS, columns), BF16),
-            ((frames, rows, WIDTH, columns), F32),
-            ((frames, 4 * WIDTH, pair), F32),
-        ],
-        [VMEM] * 8,
+        [((2, rows, TAPS, columns), BF16), ((frames, rows, WIDTH, columns), F32)],
+        [VMEM] * 6,
         flops=10**9,
-    )(own, earlier, table, rows_own, inside, conv_bias.reshape(1, WIDTH), down_flat, cotangent)
+    )(earlier, table, rows_own, inside, bias, x_own)
 
     data_rows = 27 * CH // 2 + 4 * WIDTH + 8
     chunk = -(-data_rows // 32) * 8
@@ -462,37 +493,23 @@
             ((frames, 4 * WIDTH, pair), BF16),
             ((frames * WIDTH, rows * columns), BF16),
         ],
-        [SMEM] + [VMEM] * 9,
+        [VMEM] * 10,
         [
             pltpu.VMEM((frames + 2, rows + 2, TAPS, columns), BF16),
             pltpu.VMEM((2, 4 * chunk, WIDTH), F32),
         ],
         flops=10**9,
-    )(place, inner, outer, table, rows_halo, x_own, pre_own, dact, outside, cotangent)
-
-    features, pixels_own, pixels_early, send_inner, send_outer = call(
+    )(inner, outer, table, rows_halo, x_early, x_own, pre_own, dact, outside, cot)
+
+    send_inner, send_outer = call(
+        functools.partial(edge_kernel, dims), [(flat_halo, BF16), (flat_halo, BF16)], [VMEM] * 4, flops=10**9
+    )(slopes, backward, table, rows_halo)
+    features, pixels_own, pixels_early = call(
         functools.partial(late_kernel, dims),
-        [
-            ((frames, rows // 2, pair, width2), BF16),
-            (own.shape, F32),
-            (own.shape, F32),
-            (flat_halo, BF16),
-            (flat_halo, BF16),
-        ],
-        [SMEM] + [VMEM] * 8,
-        [pltpu.VMEM((frames + 2, rows + 2, CH, columns), F32)],
+        [((frames, rows // 2, pair, width2), BF16), (own.shape, F32), (own.shape, F32)],
+        [VMEM] * 7,
         flops=10**9,
-    )(
-        place,
-        acts,
-        slopes,
-        backward,
-        down_flat,
-        down_bias.reshape(1, width2),
-        table,
-        rows_own,
-        rows_halo,
-    )
+    )(acts, slopes, backward, down_flat, bias2, table, rows_own)
 
     total = keep + swap_inner(give).astype(F32)
     planes = ("tm_lo", "y")
@@ -519,20 +536,16 @@
         pltpu.SemaphoreType.DMA((5,)),
     ]
     grads = call(
-        functools.partial(finish_kernel, scale, False),
-        outs,
-        [SMEM] + [VMEM] * 4,
-        scratch,
-        out_specs=[ANY] * 4,
-    )(place, *pieces)
+        functools.partial(finish_kernel, scale, False), outs, [VMEM] * 4, scratch, out_specs=[HBM] * 4
+    )(*pieces)
     grad_conv, grad_conv_bias, grad_down, grad_down_bias = call(
         functools.partial(finish_kernel, scale, True),
         outs,
-        [SMEM, VMEM] + [ANY] * 4,
+        [VMEM] + [HBM] * 4,
         scratch,
-        out_specs=[ANY] * 4,
-        input_output_aliases={2: 0, 3: 1, 4: 2, 5: 3},
-    )(place, theirs, *grads)
+        out_specs=[HBM] * 4,
+        input_output_aliases={1: 0, 2: 1, 3: 2, 4: 3},
+    )(theirs, *grads)
 
     from_inner = swap_inner(send_inner).reshape((frames + 2) * colors, 4, pixel_columns)
     from_outer = swap_outer(send_outer).reshape((frames + 2) * colors, 4, pixel_columns)
@@ -541,7 +554,8 @@
     halo = jnp.concatenate([above, below], axis=1)
     early = pixels_early.reshape(frame_shape) + halo[: 2 * colors]
     late = pixels_own.reshape(frame_shape) + halo[2 * colors :]
-    grad_pixels = late + along_tm(early.astype(BF16), -1).astype(F32)
+    following = along_tm(early.astype(BF16), -1)
+    grad_pixels = late + following.astype(F32)
     return (
         features,
         grad_conv.reshape(conv_weight.shape),

time: 59 us -> 55.7 us (0.944)
  local copies, waits for them, and re-layouts: 3.53 us -> 0.11 us
  starting transfers between devices: 25.8 us -> 28.2 us
  waiting for transfers between devices: 16.5 us -> 15 us
  Pallas kernels: 10.9 us -> 10.3 us
    unnamed x20 -> x0, local copies, waits for them, and re-layouts: 3.42 us -> none
    ppermute x2, waiting for transfers between devices: 5.27 us -> 2.57 us  [along_tm(): return lax.ppermute(value, times, pairs)]
    ppermute x4, starting transfers between devices: 6.22 us -> 8.64 us  [swap_inner(): return lax.ppermute(value, 'core', [(0, 1), (1, 0)])]
    ppermute x9, waiting for transfers between devices: 11.2 us -> 12.4 us  [exchange(): return lax.ppermute(value, axes, [(i, i ^ mask) for i in range(size)])]
    pallas_call x1, Pallas kernels: 3.19 us -> 2.16 us  [local(): call(functools.partial(late_kernel, dims), [((frames, rows // 2, pair, wi...]
    pallas_call x5 -> x6, Pallas kernels: 5.14 us -> 6.14 us  [the longest x1 2.13 us: local(): call(functools.partial(first_kernel, dims, len(sources)), [(source.shape,...]
  transfers between devices with their start and end apart: 17 -> 17, of which waited for: 10 -> 11; matrix products, arithmetic and copies ran while one was open for 2% -> 2% of each run, Pallas kernels for 11% -> 13%
where the time goes in v3:
time: 55.7 us; the launch traced here: 55.5 us
  starting transfers between devices  28.2 us (51%)
  waiting for transfers between devices  15 us (27%)
  Pallas kernels  10.3 us (18%)
  other arithmetic  1.09 us (2%)
  between operations  0.8 us (1%)
    ppermute x9, waiting for transfers between devices, exchange(): return lax.ppermute(value, axes, [(i, i ^ mask) for i in range(size)])  12.4 us
    ppermute x9, starting transfers between devices, exchange(): return lax.ppermute(value, axes, [(i, i ^ mask) for i in range(size)])  12.1 us
    ppermute x4, starting transfers between devices, swap_inner(): return lax.ppermute(value, 'core', [(0, 1), (1, 0)])  8.64 us
    ppermute x2, starting transfers between devices, along_tm(): return lax.ppermute(value, times, pairs)  6.17 us
    ppermute x2, waiting for transfers between devices, along_tm(): return lax.ppermute(value, times, pairs)  2.57 us
    pallas_call x1, Pallas kernels, local(): call(functools.partial(late_kernel, dims), [((frames, rows // 2, pair, wi...  2.16 us
    pallas_call x1, Pallas kernels, local(): call(functools.partial(first_kernel, dims, len(sources)), [(source.shape,...  2.13 us
    pallas_call x1, Pallas kernels, local(): call(functools.partial(main_kernel, dims), [((4, chunk, WIDTH), F32), ((4...  2.04 us
  transfers between devices with their start and end apart: 17, of which 11 were waited for; matrix products, arithmetic and copies ran while one was open for 2% of the time, Pallas kernels for 13%

profile of v3, /device:TPU:0, one launch (start us, length us, event | category | flops | bytes accessed | tf_op | source)
XLA Modules:
  0.0 55.5 jit_solution(906397501285066528)
XLA Ops:
  0.6 4.9 %collective-permute-start = (bf16[48,1024]{1,0:T(8,128)(2,1)}, bf16[48,1024]{1,0:T(8,128)(2,1)S(1)}, u32[]{:S(2)}, u32[]{:S(2)}) collective-permute-start(bf16[48,1024]{1,0:T(8,128)(2,1)} %bitcast.43), channel_id=1, source_target_pairs={{0,16},{1,17},{2,18},{3,19},{4,20},{5,21},{6,22},{7,23},{8,24},{9,... | collective-permute-start | bytes 294920 | tf_op jit(solution)/shard_map/ppermute | solution.py:430
  5.5 2.1 %shard_map.145 = (bf16[48,1024]{1,0:T(8,128)(2,1)S(1)}, bf16[512,512]{1,0:T(8,128)(2,1)S(1)}, bf16[192,192]{1,0:T(8,128)(2,1)S(1)}, bf16[512,256]{1,0:T(8,128)(2...) custom-call(bf16[27,48,128]{2,1,0:T(8,128)(2,1)} %bitcast.41, ...), custom_call_target="tpu_custom_call" | custom-call | flops 1000000000 | bytes 1048576 | tf_op jit(solution)/shard_map/pallas_call | solution.py:459
  9.0 1.1 %shard_map.147 = (bf16[2,2,144,256]{3,2,1,0:T(8,128)(2,1)S(1)}, f32[2,2,128,256]{3,2,1,0:T(8,128)S(1)}) custom-call(bf16[48,1024]{1,0:T(8,128)(2,1)S(1)} %collective-permute-done.earlier, bf16[512,512]{1,0:T(8,128)(2,1)S(1)} %get-tuple-element.45.table, bf16[192,192]{1,0:T(8,128)(2,1)S(1)} %get-tuple-element.47.rows_own, ...), custom_call_target="tpu_custom_call" | custom-call | flops 1000000000 | bytes 1048576 | tf_op jit(solution)/shard_map/pallas_call | solution.py:479
  10.1 2.0 %shard_map.148 = (f32[4,296,128]{2,1,0:T(8,128)S(1)}, bf16[4,296,128]{2,1,0:T(8,128)(2,1)S(1)}, bf16[2,512,128]{2,1,0:T(8,128)(2,1)S(1)}, bf16[256,512]{1,0:T(8,128)(2,1)S(1)}) custom-call(bf16[48,1024]{1,0:T(8,128)(2,1)S(1)} %collective-permute-done.1.inner, bf16[48,1024]{1,0:T(8,128)(2,1)S(1)} %collective-permute-done.2.outer, ...), custom_call_target="tpu_custom_call" | custom-call | flops 1000000000 | bytes 1048576 | tf_op jit(solution)/shard_map/pallas_call | solution.py:488
  12.2 4.7 %collective-permute-start.3 = (bf16[4,296,128]{2,1,0:T(8,128)(2,1)S(1)}, bf16[4,296,128]{2,1,0:T(8,128)(2,1)S(1)}, u32[]{:S(2)}, u32[]{:S(2)}) collective-permute-start(bf16[4,296,128]{2,1,0:T(8,128)(2,1)S(1)} %get-tuple-element.63), channel_id=1, source_target_pairs={{0,1},{1,0},{2,3},{3,2},{4,5},{5,4},{6,7},{7,6},{8,9},{9,8},{10,11... | collective-permute-start | bytes 909320 | tf_op jit(solution)/shard_map/ppermute | solution.py:433
  18.4 3.8 %collective-permute-start.15 = (bf16[48,1024]{1,0:T(8,128)(2,1)S(1)}, bf16[48,1024]{1,0:T(8,128)(2,1)S(1)}, u32[]{:S(2)}, u32[]{:S(2)}) collective-permute-start(bf16[48,1024]{1,0:T(8,128)(2,1)S(1)} %get-tuple-element.74), channel_id=1, source_target_pairs={{0,1},{1,0},{2,3},{3,2},{4,5},{5,4},{6,7},{7,6},{8,9},{9,8},{10,11... | collective-permute-start | bytes 294920 | tf_op jit(solution)/shard_map/ppermute | solution.py:433
  22.2 2.2 %shard_map.149 = (bf16[2,1,128,256]{3,2,1,0:T(8,128)(2,1)}, f32[48,1024]{1,0:T(8,128)S(1)}, f32[48,1024]{1,0:T(8,128)S(1)}) custom-call(bf16[2,512,128]{2,1,0:T(8,128)(2,1)S(1)} %get-tuple-element.56.acts, bf16[256,512]{1,0:T(8,128)(2,1)S(1)} %get-tuple-element.57.slopes, bf16[432,384]{1,0:T(8,128)(2,1)S(1)} %get-tuple-element.58.backward, ...), custom_call_target="tpu_custom_call" | custom-call | flops 1000000000 | bytes 1048576 | tf_op jit(solution)/shard_map/pallas_call | solution.py:507
  24.5 1.7 %collective-permute-start.4 = (bf16[296,128]{1,0:T(8,128)(2,1)S(1)}, bf16[296,128]{1,0:T(8,128)(2,1)S(1)}, u32[]{:S(2)}, u32[]{:S(2)}) collective-permute-start(bf16[296,128]{1,0:T(8,128)(2,1)S(1)} %get-tuple-element.78), channel_id=1, source_target_pairs={{0,2},{2,0},{16,18},{18,16},{1,3},{3,1},{17,19},{19,17},{4,6},{6,4... | collective-permute-start | bytes 227336 | tf_op jit(solution)/shard_map/ppermute | solution.py:441
  26.3 2.3 %collective-permute-start.5 = (bf16[296,128]{1,0:T(8,128)(2,1)S(1)}, bf16[296,128]{1,0:T(8,128)(2,1)S(1)}, u32[]{:S(2)}, u32[]{:S(2)}) collective-permute-start(bf16[296,128]{1,0:T(8,128)(2,1)S(1)} %get-tuple-element.80), channel_id=1, source_target_pairs={{0,16},{2,18},{16,0},{18,2},{1,17},{3,19},{17,1},{19,3},{4,20},{6,... | collective-permute-start | bytes 227336 | tf_op jit(solution)/shard_map/ppermute | solution.py:441
  29.0 2.5 %collective-permute-done.5 = bf16[296,128]{1,0:T(8,128)(2,1)S(1)} collective-permute-done((bf16[296,128]{1,0:T(8,128)(2,1)S(1)}, bf16[296,128]{1,0:T(8,128)(2,1)S(1)}, u32[]{:S(2)}, u32[]{:S(2)}) %collective-permute-start.5) | collective-permute-done | bytes 75808 | tf_op jit(solution)/shard_map/ppermute | solution.py:441
  31.4 2.4 %collective-permute-done.6 = bf16[296,128]{1,0:T(8,128)(2,1)S(1)} collective-permute-done((bf16[296,128]{1,0:T(8,128)(2,1)S(1)}, bf16[296,128]{1,0:T(8,128)(2,1)S(1)}, u32[]{:S(2)}, u32[]{:S(2)}) %collective-permute-start.6) | collective-permute-done | bytes 75808 | tf_op jit(solution)/shard_map/ppermute | solution.py:441
  33.9 1.6 %collective-permute-start.7 = (bf16[296,128]{1,0:T(8,128)(2,1)S(1)}, bf16[296,128]{1,0:T(8,128)(2,1)S(1)}, u32[]{:S(2)}, u32[]{:S(2)}) collective-permute-start(bf16[296,128]{1,0:T(8,128)(2,1)S(1)} %fusion.3), channel_id=1, source_target_pairs={{0,4},{4,0},{8,12},{12,8},{1,5},{5,1},{9,13},{13,9},{2,6},{6,2},{1... | collective-permute-start | bytes 227336 | tf_op jit(solution)/shard_map/ppermute | solution.py:441
  35.5 1.1 %collective-permute-start.8 = (bf16[296,128]{1,0:T(8,128)(2,1)S(1)}, bf16[296,128]{1,0:T(8,128)(2,1)S(1)}, u32[]{:S(2)}, u32[]{:S(2)}) collective-permute-start(bf16[296,128]{1,0:T(8,128)(2,1)S(1)} %fusion.3), channel_id=1, source_target_pairs={{0,8},{4,12},{8,0},{12,4},{1,9},{5,13},{9,1},{13,5},{2,10},{6,14},... | collective-permute-start | bytes 227336 | tf_op jit(solution)/shard_map/ppermute | solution.py:441
  36.6 1.7 %collective-permute-start.9 = (bf16[296,128]{1,0:T(8,128)(2,1)S(1)}, bf16[296,128]{1,0:T(8,128)(2,1)S(1)}, u32[]{:S(2)}, u32[]{:S(2)}) collective-permute-start(bf16[296,128]{1,0:T(8,128)(2,1)S(1)} %fusion.3), channel_id=1, source_target_pairs={{0,12},{4,8},{8,4},{12,0},{1,13},{5,9},{9,5},{13,1},{2,14},{6,10},... | collective-permute-start | bytes 227336 | tf_op jit(solution)/shard_map/ppermute | solution.py:441
  38.6 3.3 %collective-permute-done.8 = bf16[296,128]{1,0:T(8,128)(2,1)S(1)} collective-permute-done((bf16[296,128]{1,0:T(8,128)(2,1)S(1)}, bf16[296,128]{1,0:T(8,128)(2,1)S(1)}, u32[]{:S(2)}, u32[]{:S(2)}) %collective-permute-start.8) | collective-permute-done | bytes 75808 | tf_op jit(solution)/shard_map/ppermute | solution.py:441
  41.9 0.9 %collective-permute-done.9 = bf16[296,128]{1,0:T(8,128)(2,1)S(1)} collective-permute-done((bf16[296,128]{1,0:T(8,128)(2,1)S(1)}, bf16[296,128]{1,0:T(8,128)(2,1)S(1)}, u32[]{:S(2)}, u32[]{:S(2)}) %collective-permute-start.9) | collective-permute-done | bytes 75808 | tf_op jit(solution)/shard_map/ppermute | solution.py:441
  42.9 1.4 %collective-permute-start.10 = (bf16[296,128]{1,0:T(8,128)(2,1)S(1)}, bf16[296,128]{1,0:T(8,128)(2,1)S(1)}, u32[]{:S(2)}, u32[]{:S(2)}) collective-permute-start(bf16[296,128]{1,0:T(8,128)(2,1)S(1)} %add_convert_fusion.refs_0_), channel_id=1, source_target_pairs={{0,2},{2,0},{16,18},{18,16},{1,3},{3,1},{17,19},{19,17},{4,6},{6,4... | collective-permute-start | bytes 227336 | tf_op jit(solution)/shard_map/ppermute | solution.py:441
  45.2 1.2 %collective-permute-start.12 = (bf16[296,128]{1,0:T(8,128)(2,1)S(1)}, bf16[296,128]{1,0:T(8,128)(2,1)S(1)}, u32[]{:S(2)}, u32[]{:S(2)}) collective-permute-start(bf16[296,128]{1,0:T(8,128)(2,1)S(1)} %add_convert_fusion.refs_0_), channel_id=1, source_target_pairs={{0,18},{2,16},{16,2},{18,0},{1,19},{3,17},{17,3},{19,1},{4,22},{6,... | collective-permute-start | bytes 227336 | tf_op jit(solution)/shard_map/ppermute | solution.py:441
  46.4 1.3 %collective-permute-start.16 = (bf16[6,8,1024]{2,1,0:T(8,128)(2,1)S(1)}, bf16[6,8,1024]{2,1,0:T(8,128)(2,1)S(1)}, u32[]{:S(2)}, u32[]{:S(2)}) collective-permute-start(bf16[6,8,1024]{2,1,0:T(8,128)(2,1)S(1)} %fusion), channel_id=1, source_target_pairs={{16,0},{17,1},{18,2},{19,3},{20,4},{21,5},{22,6},{23,7},{24,8},{25... | collective-permute-start | bytes 294920 | tf_op jit(solution)/shard_map/ppermute | solution.py:430
  48.1 1.3 %collective-permute-done.11.refs_2_ = bf16[296,128]{1,0:T(8,128)(2,1)S(1)} collective-permute-done((bf16[296,128]{1,0:T(8,128)(2,1)S(1)}, bf16[296,128]{1,0:T(8,128)(2,1)S(1)}, u32[]{:S(2)}, u32[]{:S(2)}) %collective-permute-start.11) | collective-permute-done | bytes 75808 | tf_op jit(solution)/shard_map/ppermute | solution.py:441
  49.5 1.2 %collective-permute-done.12.refs_3_ = bf16[296,128]{1,0:T(8,128)(2,1)S(1)} collective-permute-done((bf16[296,128]{1,0:T(8,128)(2,1)S(1)}, bf16[296,128]{1,0:T(8,128)(2,1)S(1)}, u32[]{:S(2)}, u32[]{:S(2)}) %collective-permute-start.12) | collective-permute-done | bytes 75808 | tf_op jit(solution)/shard_map/ppermute | solution.py:441
  50.8 2.2 %collective-permute-done.16 = bf16[6,8,1024]{2,1,0:T(8,128)(2,1)S(1)} collective-permute-done((bf16[6,8,1024]{2,1,0:T(8,128)(2,1)S(1)}, bf16[6,8,1024]{2,1,0:T(8,128)(2,1)S(1)}, u32[]{:S(2)}, u32[]{:S(2)}) %collective-permute-start.16) | collective-permute-done | bytes 98336 | tf_op jit(solution)/shard_map/ppermute | solution.py:430
  53.7 0.9 %shard_map.150 = (f32[1296,128]{1,0:T(8,128)}, f32[1,128]{1,0:T(1,128)}, f32[512,256]{1,0:T(8,128)}, f32[1,256]{1,0:T(1,128)}) custom-call(bf16[296,128]{1,0:T(8,128)(2,1)S(1)} %add_convert_fusion.refs_0_, bf16[296,128]{1,0:T(8,128)(2,1)S(1)} %collective-permute-done.10.refs_1_, bf16[296,128]{1,0:T(8,128)(2,1)S(1)} %collective-permute-done.11.refs_2_, ...), custom_call_target="tpu_custom_call" | custom-call | bytes 1048576 | tf_op jit(solution)/shard_map/pallas_call | solution.py:538
  54.6 0.9 %shard_map.151 = (f32[1296,128]{1,0:T(8,128)}, f32[1,128]{1,0:T(1,128)}, f32[512,256]{1,0:T(8,128)}, f32[1,256]{1,0:T(1,128)}) custom-call(bf16[4,296,128]{2,1,0:T(8,128)(2,1)S(1)} %collective-permute-done.13.refs_0_, f32[1296,128]{1,0:T(8,128)} %get-tuple-element.64.refs_1_, ...), custom_call_target="tpu_custom_call", output_to_operand_aliasing={{0}: (1, {}), {1}: (2, {}), {2}: (3, {}), {3}: (4, {})} | custom-call | bytes 1048576 | tf_op jit(solution)/shard_map/pallas_call | solution.py:541
  (29 shorter events, 5.8 us)
Async XLA Ops:
  0.6 7.4 %collective-permute-start = (bf16[48,1024]{1,0:T(8,128)(2,1)}, bf16[48,1024]{1,0:T(8,128)(2,1)S(1)}, u32[]{:S(2)}, u32[]{:S(2)}) collective-permute-start(bf16[48,1024]{1,0:T(8,128)(2,1)} %bitcast.43), channel_id=1, source_target_pairs={{0,16},{1,17},{2,18},{3,19},{4,20},{5,21},{6,22},{7,23},{8,24},{9,... | collective-permute-start | bytes 294920 | tf_op jit(solution)/shard_map/ppermute | solution.py:430
  8.2 1.9 %collective-permute-start.1 = (bf16[48,1024]{1,0:T(8,128)(2,1)S(1)}, bf16[48,1024]{1,0:T(8,128)(2,1)S(1)}, u32[]{:S(2)}, u32[]{:S(2)}) collective-permute-start(bf16[48,1024]{1,0:T(8,128)(2,1)S(1)} %get-tuple-element.43), channel_id=1, source_target_pairs={{0,1},{1,0},{2,3},{3,2},{4,5},{5,4},{6,7},{7,6},{8,9},{9,8},{10,11... | collective-permute-start | bytes 294920 | tf_op jit(solution)/shard_map/ppermute | solution.py:433
  8.3 1.8 %collective-permute-start.2 = (bf16[48,1024]{1,0:T(8,128)(2,1)S(1)}, bf16[48,1024]{1,0:T(8,128)(2,1)S(1)}, u32[]{:S(2)}, u32[]{:S(2)}) collective-permute-start(bf16[48,1024]{1,0:T(8,128)(2,1)S(1)} %get-tuple-element.44), channel_id=1, source_target_pairs={{1,2},{3,4},{5,6},{7,8},{9,10},{11,12},{13,14},{2,1},{4,3},{6,5},{... | collective-permute-start | bytes 294920 | tf_op jit(solution)/shard_map/ppermute | solution.py:437
  12.2 12.2 %collective-permute-start.3 = (bf16[4,296,128]{2,1,0:T(8,128)(2,1)S(1)}, bf16[4,296,128]{2,1,0:T(8,128)(2,1)S(1)}, u32[]{:S(2)}, u32[]{:S(2)}) collective-permute-start(bf16[4,296,128]{2,1,0:T(8,128)(2,1)S(1)} %get-tuple-element.63), channel_id=1, source_target_pairs={{0,1},{1,0},{2,3},{3,2},{4,5},{5,4},{6,7},{7,6},{8,9},{9,8},{10,11... | collective-permute-start | bytes 909320 | tf_op jit(solution)/shard_map/ppermute | solution.py:433
  17.7 10.8 %collective-permute-start.14 = (bf16[48,1024]{1,0:T(8,128)(2,1)S(1)}, bf16[48,1024]{1,0:T(8,128)(2,1)S(1)}, u32[]{:S(2)}, u32[]{:S(2)}) collective-permute-start(bf16[48,1024]{1,0:T(8,128)(2,1)S(1)} %get-tuple-element.73), channel_id=1, source_target_pairs={{1,2},{3,4},{5,6},{7,8},{9,10},{11,12},{13,14},{2,1},{4,3},{6,5},{... | collective-permute-start | bytes 294920 | tf_op jit(solution)/shard_map/ppermute | solution.py:437
  18.4 10.2 %collective-permute-start.15 = (bf16[48,1024]{1,0:T(8,128)(2,1)S(1)}, bf16[48,1024]{1,0:T(8,128)(2,1)S(1)}, u32[]{:S(2)}, u32[]{:S(2)}) collective-permute-start(bf16[48,1024]{1,0:T(8,128)(2,1)S(1)} %get-tuple-element.74), channel_id=1, source_target_pairs={{0,1},{1,0},{2,3},{3,2},{4,5},{5,4},{6,7},{7,6},{8,9},{9,8},{10,11... | collective-permute-start | bytes 294920 | tf_op jit(solution)/shard_map/ppermute | solution.py:433
  24.5 4.4 %collective-permute-start.4 = (bf16[296,128]{1,0:T(8,128)(2,1)S(1)}, bf16[296,128]{1,0:T(8,128)(2,1)S(1)}, u32[]{:S(2)}, u32[]{:S(2)}) collective-permute-start(bf16[296,128]{1,0:T(8,128)(2,1)S(1)} %get-tuple-element.78), channel_id=1, source_target_pairs={{0,2},{2,0},{16,18},{18,16},{1,3},{3,1},{17,19},{19,17},{4,6},{6,4... | collective-permute-start | bytes 227336 | tf_op jit(solution)/shard_map/ppermute | solution.py:441
  26.3 5.2 %collective-permute-start.5 = (bf16[296,128]{1,0:T(8,128)(2,1)S(1)}, bf16[296,128]{1,0:T(8,128)(2,1)S(1)}, u32[]{:S(2)}, u32[]{:S(2)}) collective-permute-start(bf16[296,128]{1,0:T(8,128)(2,1)S(1)} %get-tuple-element.80), channel_id=1, source_target_pairs={{0,16},{2,18},{16,0},{18,2},{1,17},{3,19},{17,1},{19,3},{4,20},{6,... | collective-permute-start | bytes 227336 | tf_op jit(solution)/shard_map/ppermute | solution.py:441
  28.6 5.3 %collective-permute-start.6 = (bf16[296,128]{1,0:T(8,128)(2,1)S(1)}, bf16[296,128]{1,0:T(8,128)(2,1)S(1)}, u32[]{:S(2)}, u32[]{:S(2)}) collective-permute-start(bf16[296,128]{1,0:T(8,128)(2,1)S(1)} %get-tuple-element.79), channel_id=1, source_target_pairs={{0,18},{2,16},{16,2},{18,0},{1,19},{3,17},{17,3},{19,1},{4,22},{6,... | collective-permute-start | bytes 227336 | tf_op jit(solution)/shard_map/ppermute | solution.py:441
  33.9 4.7 %collective-permute-start.7 = (bf16[296,128]{1,0:T(8,128)(2,1)S(1)}, bf16[296,128]{1,0:T(8,128)(2,1)S(1)}, u32[]{:S(2)}, u32[]{:S(2)}) collective-permute-start(bf16[296,128]{1,0:T(8,128)(2,1)S(1)} %fusion.3), channel_id=1, source_target_pairs={{0,4},{4,0},{8,12},{12,8},{1,5},{5,1},{9,13},{13,9},{2,6},{6,2},{1... | collective-permute-start | bytes 227336 | tf_op jit(solution)/shard_map/ppermute | solution.py:441
  35.5 6.4 %collective-permute-start.8 = (bf16[296,128]{1,0:T(8,128)(2,1)S(1)}, bf16[296,128]{1,0:T(8,128)(2,1)S(1)}, u32[]{:S(2)}, u32[]{:S(2)}) collective-permute-start(bf16[296,128]{1,0:T(8,128)(2,1)S(1)} %fusion.3), channel_id=1, source_target_pairs={{0,8},{4,12},{8,0},{12,4},{1,9},{5,13},{9,1},{13,5},{2,10},{6,14},... | collective-permute-start | bytes 227336 | tf_op jit(solution)/shard_map/ppermute | solution.py:441
  36.6 6.2 %collective-permute-start.9 = (bf16[296,128]{1,0:T(8,128)(2,1)S(1)}, bf16[296,128]{1,0:T(8,128)(2,1)S(1)}, u32[]{:S(2)}, u32[]{:S(2)}) collective-permute-start(bf16[296,128]{1,0:T(8,128)(2,1)S(1)} %fusion.3), channel_id=1, source_target_pairs={{0,12},{4,8},{8,4},{12,0},{1,13},{5,9},{9,5},{13,1},{2,14},{6,10},... | collective-permute-start | bytes 227336 | tf_op jit(solution)/shard_map/ppermute | solution.py:441
  42.9 5.3 %collective-permute-start.10 = (bf16[296,128]{1,0:T(8,128)(2,1)S(1)}, bf16[296,128]{1,0:T(8,128)(2,1)S(1)}, u32[]{:S(2)}, u32[]{:S(2)}) collective-permute-start(bf16[296,128]{1,0:T(8,128)(2,1)S(1)} %add_convert_fusion.refs_0_), channel_id=1, source_target_pairs={{0,2},{2,0},{16,18},{18,16},{1,3},{3,1},{17,19},{19,17},{4,6},{6,4... | collective-permute-start | bytes 227336 | tf_op jit(solution)/shard_map/ppermute | solution.py:441
  44.3 5.2 %collective-permute-start.11 = (bf16[296,128]{1,0:T(8,128)(2,1)S(1)}, bf16[296,128]{1,0:T(8,128)(2,1)S(1)}, u32[]{:S(2)}, u32[]{:S(2)}) collective-permute-start(bf16[296,128]{1,0:T(8,128)(2,1)S(1)} %add_convert_fusion.refs_0_), channel_id=1, source_target_pairs={{0,16},{2,18},{16,0},{18,2},{1,17},{3,19},{17,1},{19,3},{4,20},{6,... | collective-permute-start | bytes 227336 | tf_op jit(solution)/shard_map/ppermute | solution.py:441
  45.2 5.5 %collective-permute-start.12 = (bf16[296,128]{1,0:T(8,128)(2,1)S(1)}, bf16[296,128]{1,0:T(8,128)(2,1)S(1)}, u32[]{:S(2)}, u32[]{:S(2)}) collective-permute-start(bf16[296,128]{1,0:T(8,128)(2,1)S(1)} %add_convert_fusion.refs_0_), channel_id=1, source_target_pairs={{0,18},{2,16},{16,2},{18,0},{1,19},{3,17},{17,3},{19,1},{4,22},{6,... | collective-permute-start | bytes 227336 | tf_op jit(solution)/shard_map/ppermute | solution.py:441
  46.4 6.5 %collective-permute-start.16 = (bf16[6,8,1024]{2,1,0:T(8,128)(2,1)S(1)}, bf16[6,8,1024]{2,1,0:T(8,128)(2,1)S(1)}, u32[]{:S(2)}, u32[]{:S(2)}) collective-permute-start(bf16[6,8,1024]{2,1,0:T(8,128)(2,1)S(1)} %fusion), channel_id=1, source_target_pairs={{16,0},{17,1},{18,2},{19,3},{20,4},{21,5},{22,6},{23,7},{24,8},{25... | collective-permute-start | bytes 294920 | tf_op jit(solution)/shard_map/ppermute | solution.py:430
  50.7 3.9 %collective-permute-start.13 = (bf16[4,296,128]{2,1,0:T(8,128)(2,1)S(1)}, bf16[4,296,128]{2,1,0:T(8,128)(2,1)S(1)}, u32[]{:S(2)}, u32[]{:S(2)}) collective-permute-start(bf16[4,296,128]{2,1,0:T(8,128)(2,1)S(1)} %pad_maximum_fusion), channel_id=1, source_target_pairs={{0,1},{1,0},{2,3},{3,2},{4,5},{5,4},{6,7},{7,6},{8,9},{9,8},{10,11... | collective-permute-start | bytes 909320 | tf_op jit(solution)/shard_map/ppermute | solution.py:433

commit v4 on v3

--- a/solution.py
+++ b/solution.py
@@ -171,8 +171,10 @@
         dact[f] = mm(down_weight[...], cotangent[f, 0], NT)
 
 
-def pack_kernel(own, earlier, chosen, inner, outer):
+def pack_kernel(times, own, came, chosen, inner, outer, earlier):
     core, _ = position()
+    used = jnp.where(lax.axis_index(times) == 0, 0.0, 1.0)
+    earlier[...] = (came[...].astype(F32) * used).astype(BF16)
     both = mm(chosen[core], jnp.concatenate([earlier[...], own[...]], axis=0)).astype(BF16)
     size = inner.shape[0]
     inner[...] = both[:size]
@@ -208,101 +210,100 @@
             pre[f, r] = total[f]
 
 
-def main_kernel(
-    dims,
-    inner,
-    outer,
-    table,
-    rows_halo,
-    x_early,
-    x_own,
-    pre_own,
-    dact,
-    outside,
-    cotangent,
-    keep,
-    give,
-    acts,
-    slopes,
-    x,
-    packed,
-):
+def one_row(dims, r, halo, table, rows_halo, x_early, x_own, pre_own, dact, outside, cotangent, acts, slopes, x):
     frames, rows, pair = dims
-    core, plane = position()
-    inner_row = jnp.where(core == 0, rows + 1, 0)
-    outer_row = jnp.where(core == 0, 0, rows + 1)
     for frame in range(frames + 2):
-        x[frame, 1 : rows + 1] = x_early[frame] if frame < 2 else x_own[frame - 2]
-    places = [
-        [(f, inner_row) for f in range(frames + 2)],
-        [(f, outer_row) for f in range(frames + 2)],
-    ]
-    analyse([inner[...], outer[...]], table, [rows_halo, rows_halo], x, places, pair)
-
-    for r in range(rows):
-        total = [pre_own[f, r] for f in range(frames)]
-        edge = 0 if r == 0 else rows + 1
-        for frame in range(frames + 2):
-            convolve(total, outside[r], x[frame, edge], frame, frames)
-        for f in range(frames):
-            pre = total[f]
-            sig = jax.nn.sigmoid(pre)
-            act = pre * sig
-            at = 2 * WIDTH * r
-            acts[f, at : at + WIDTH] = act[:, :pair].astype(BF16)
-            acts[f, at + WIDTH : at + 2 * WIDTH] = act[:, pair:].astype(BF16)
-            here = jnp.concatenate(
-                [dact[f, at : at + WIDTH], dact[f, at + WIDTH : at + 2 * WIDTH]], axis=1
-            )
-            slope = here * sig * (1.0 + pre * (1.0 - sig))
-            slopes[WIDTH * f : WIDTH * (f + 1), 2 * pair * r : 2 * pair * (r + 1)] = slope.astype(BF16)
-
+        here = x_early[frame] if frame < 2 else x_own[frame - 2]
+        x[frame, pl.ds(1 - r, rows)] = here
+    analyse([halo], table, [rows_halo], x, [[(f, 2 * r) for f in range(frames + 2)]], pair)
+    total = [pre_own[f, r] for f in range(frames)]
+    for frame in range(frames + 2):
+        convolve(total, outside[r], x[frame, 2 * r], frame, frames)
+    down_total = None
+    for f in range(frames):
+        pre = total[f]
+        sig = jax.nn.sigmoid(pre)
+        act = pre * sig
+        acts[f, :WIDTH] = act[:, :pair].astype(BF16)
+        acts[f, WIDTH:] = act[:, pair:].astype(BF16)
+        here = dact[f, pl.ds(pl.multiple_of(2 * WIDTH * r, 2 * WIDTH), 2 * WIDTH)]
+        here = jnp.concatenate([here[:WIDTH], here[WIDTH:]], axis=1)
+        slope = here * sig * (1.0 + pre * (1.0 - sig))
+        slopes[WIDTH * f : WIDTH * (f + 1)] = slope.astype(BF16)
+        part = mm(acts[f], cotangent[f, 0])
+        down_total = part if down_total is None else down_total + part
     conv_total = [None] * 3
     for frame in range(frames + 2):
         used = taps_of(frame, frames)
         first, last = used[0][0], used[-1][0]
-        values = jnp.concatenate(
-            [x[frame, r : r + 3].reshape(3 * TAPS, 2 * pair) for r in range(rows)], axis=1
-        )
+        values = x[frame].reshape(3 * TAPS, 2 * pair)
         part = mm(values, slopes[WIDTH * first : WIDTH * (last + 1)], NT)
         for f, a in used:
             here = part[:, WIDTH * (f - first) : WIDTH * (f - first + 1)]
             conv_total[a] = here if conv_total[a] is None else conv_total[a] + here
-    down_total = None
-    cot_total = None
-    ones = jnp.ones((8, 2 * pair * rows), BF16)
-    for f in range(frames):
-        part = mm(acts[f], cotangent[f, 0])
-        down_total = part if down_total is None else down_total + part
-        part = mm(ones[:, :pair], cotangent[f, 0])
-        cot_total = part if cot_total is None else cot_total + part
-    slope_total = mm(ones, slopes[...], NT)
-    slope_total = sum(slope_total[0:1, WIDTH * f : WIDTH * (f + 1)] for f in range(frames))
+    slope_total = mm(jnp.ones((8, 2 * pair), BF16), slopes[...], NT)
+    slope_total = sum(slope_total[:, WIDTH * f : WIDTH * (f + 1)] for f in range(frames))
+    return jnp.concatenate(conv_total, axis=0), down_total, slope_total
+
+
+def mid_kernel(dims, halo, *refs):
+    table, rows_halo, x_early, x_own, pre_own, dact, outside, cotangent = refs[:8]
+    acts, slopes, conv, down, total, x = refs[8:]
+    core, _ = position()
+    conv[...], down[...], total[...] = one_row(
+        dims, 1 - core, halo[...], *refs[:8], acts, slopes, x
+    )
+
+
+def at_end(heights):
+    height = lax.axis_index(heights)
+    return (height == 0) | (height == lax.axis_size(heights) - 1)
+
+
+def main_kernel(dims, heights, halo, *refs):
+    frames, rows, pair = dims
+    _, _, _, _, _, _, _, cotangent = refs[:8]
+    acts_in, slopes_in, conv_in, down_in, total_in, mine, keep, give, acts, slopes, x, packed = refs[8:]
+    core, plane = position()
+    halo = (halo[...].astype(F32) * jnp.where(at_end(heights), 0.0, 1.0)).astype(BF16)
+    acts[1 - core] = acts_in[...]
+    slopes[1 - core] = slopes_in[...]
+    conv, down, total = one_row(
+        dims, core, halo, *refs[:8], acts.at[core], slopes.at[core], x
+    )
+    conv = conv + conv_in[...]
+    slope_total = (total + total_in[...])[0:1]
+    ones = jnp.ones((8, pair), BF16)
+    cot_total = sum(mm(ones, cotangent[f, 0]) for f in range(frames))
 
     chunk = keep.shape[1]
     half = 27 * CH // 2
-    conv = jnp.concatenate(conv_total, axis=0)
     sums = [slope_total, cot_total[0:1, :WIDTH], cot_total[0:1, WIDTH:]]
     highs = [value.astype(BF16).astype(F32) for value in sums]
     lows = [value - high for value, high in zip(sums, highs)]
     sums = jnp.concatenate(highs + lows + [jnp.zeros((2, WIDTH), F32)], axis=0)
     down_rows = 2 * rows * WIDTH
     for h in range(2):
+        columns = slice(WIDTH * h, WIDTH * (h + 1))
         packed[h, :half] = conv[half * h : half * (h + 1)]
-        packed[h, half : half + down_rows] = down_total[:, WIDTH * h : WIDTH * (h + 1)]
+        for r, part in ((1 - core, down_in[:, columns]), (core, down[:, columns])):
+            packed[h, pl.ds(pl.multiple_of(half + 2 * WIDTH * r, 8), 2 * WIDTH)] = part
         packed[h, half + down_rows : half + down_rows + 8] = sums if h == 0 else jnp.zeros_like(sums)
         rest = 4 * chunk - half - down_rows - 8
         if rest:
             packed[h, half + down_rows + 8 :] = jnp.zeros((rest, WIDTH), F32)
     for m in range(4):
         at = pl.multiple_of(jnp.bitwise_xor(plane, m) * chunk, 8)
-        keep[m] = packed[core, pl.ds(at, chunk)]
+        if m:
+            keep[m - 1] = packed[core, pl.ds(at, chunk)]
+        else:
+            mine[...] = packed[core, pl.ds(at, chunk)]
         give[m] = packed[1 - core, pl.ds(at, chunk)].astype(BF16)
 
 
 def shifted_slope(slopes, f, r, pair):
     left, right = shifts(pair)
-    slope = slopes[WIDTH * f : WIDTH * (f + 1), 2 * pair * r : 2 * pair * (r + 1)]
+    slope = slopes[r, WIDTH * f : WIDTH * (f + 1)]
     even, odd = slope[:, :pair].astype(F32), slope[:, pair:].astype(F32)
     return jnp.concatenate(
         [
@@ -364,9 +365,8 @@
     ]
     pixels_early[...], pixels_own[...] = synthesise(groups, table, [rows_own, rows_own], pair)
     for f in range(frames):
-        turned = jnp.concatenate(
-            [acts[f, WIDTH * n : WIDTH * (n + 1)].astype(F32).T.astype(BF16) for n in range(4)], axis=1
-        )
+        blocks = [acts[u, f, WIDTH * v : WIDTH * (v + 1)] for u in range(2) for v in range(2)]
+        turned = jnp.concatenate([block.astype(F32).T.astype(BF16) for block in blocks], axis=1)
         features[f, 0] = (mm(turned, down_weight[...]) + down_bias[...]).astype(BF16)
 
 
@@ -426,22 +426,26 @@
     dims = (frames, rows, pair)
 
     def along_tm(value, step):
-        pairs = [(i, i + step) for i in range(count_tm) if 0 <= i + step < count_tm]
+        pairs = [(i, (i + step) % count_tm) for i in range(count_tm)]
         return lax.ppermute(value, times, pairs)
 
     def swap_inner(value):
         return lax.ppermute(value, "core", [(0, 1), (1, 0)])
 
     def swap_outer(value):
-        pairs = [(i, i + 1) for i in range(1, count_height - 1, 2)]
-        return lax.ppermute(value, heights, pairs + [(j, i) for i, j in pairs])
+        inside = [(i, i + 1) for i in range(1, count_height - 1, 2)]
+        inside += [(j, i) for i, j in inside]
+        pairs = [(count_height * t + i, count_height * t + j) for t in range(count_tm) for i, j in inside]
+        for end in (0, count_height - 1):
+            pairs += [(count_height * t + end, count_height * (t ^ 1) + end) for t in range(count_tm)]
+        return lax.ppermute(value, times + heights, pairs)
 
     def exchange(value, axes, mask):
         size = lax.axis_size(axes)
         return lax.ppermute(value, axes, [(i, i ^ mask) for i in range(size)])
 
     own = pixels.reshape(frames * colors * pixel_rows, pixel_columns)
-    earlier = along_tm(own, 1)
+    came = along_tm(own, 1)
     flat_halo = ((frames + 2) * colors * 4, pixel_columns)
     frame_shape = (2 * colors, pixel_rows, pixel_columns)
     sources = [
@@ -472,7 +476,9 @@
     )(*(pltpu.with_memory_space_constraint(source, pltpu.HBM) for source in sources))
     own, table, rows_own, down_flat, cot, rows_halo, chosen, bias, bias2 = outs[:9]
     inside, outside, backward, x_own, dact = outs[9:]
-    send_inner, send_outer = call(pack_kernel, [(flat_halo, BF16), (flat_halo, BF16)], [VMEM] * 3)(own, earlier, chosen)
+    send_inner, send_outer, earlier = call(
+        functools.partial(pack_kernel, times), [(flat_halo, BF16), (flat_halo, BF16), (own.shape, BF16)], [VMEM] * 3
+    )(own, came, chosen)
     inner = swap_inner(send_inner)
     outer = swap_outer(send_outer)
 
@@ -485,21 +491,36 @@
 
     data_rows = 27 * CH // 2 + 4 * WIDTH + 8
     chunk = -(-data_rows // 32) * 8
-    keep, give, acts, slopes = call(
-        functools.partial(main_kernel, dims),
+    common = (table, rows_halo, x_early, x_own, pre_own, dact, outside, cot)
+    rows_scratch = pltpu.VMEM((frames + 2, 3, TAPS, columns), BF16)
+    acts_shape = (frames, 2 * WIDTH, pair)
+    slopes_shape = (frames * WIDTH, columns)
+    inside_parts = call(
+        functools.partial(mid_kernel, dims),
         [
-            ((4, chunk, WIDTH), F32),
+            (acts_shape, BF16),
+            (slopes_shape, BF16),
+            ((27 * CH, WIDTH), F32),
+            ((2 * WIDTH, width2), F32),
+            ((8, WIDTH), F32),
+        ],
+        [VMEM] * 9,
+        [rows_scratch],
+        flops=10**9,
+    )(inner, *common)
+    mine, keep, give, acts, slopes = call(
+        functools.partial(main_kernel, dims, heights),
+        [
+            ((chunk, WIDTH), F32),
+            ((3, chunk, WIDTH), F32),
             ((4, chunk, WIDTH), BF16),
-            ((frames, 4 * WIDTH, pair), BF16),
-            ((frames * WIDTH, rows * columns), BF16),
+            ((rows, *acts_shape), BF16),
+            ((rows, *slopes_shape), BF16),
         ],
-        [VMEM] * 10,
-        [
-            pltpu.VMEM((frames + 2, rows + 2, TAPS, columns), BF16),
-            pltpu.VMEM((2, 4 * chunk, WIDTH), F32),
-        ],
+        [VMEM] * 14,
+        [rows_scratch, pltpu.VMEM((2, 4 * chunk, WIDTH), F32)],
         flops=10**9,
-    )(inner, outer, table, rows_halo, x_early, x_own, pre_own, dact, outside, cot)
+    )(outer, *common, *inside_parts)
 
     send_inner, send_outer = call(
         functools.partial(edge_kernel, dims), [(flat_halo, BF16), (flat_halo, BF16)], [VMEM] * 4, flops=10**9
@@ -511,15 +532,16 @@
         flops=10**9,
     )(acts, slopes, backward, down_flat, bias2, table, rows_own)
 
-    total = keep + swap_inner(give).astype(F32)
+    given = swap_inner(give)
+    rest = (keep + given[1:].astype(F32)).astype(BF16)
     planes = ("tm_lo", "y")
-    parts = [exchange(total[m].astype(BF16), planes, m) for m in (1, 2, 3)]
-    mine = total[0] + sum(part.astype(F32) for part in parts)
+    parts = [exchange(rest[m - 1], planes, m) for m in (1, 2, 3)]
+    mine = mine + given[0].astype(F32) + sum(part.astype(F32) for part in parts)
+    mine = mine.astype(BF16)
     for axis in axes["rest"]:
-        sent = mine.astype(BF16)
-        parts = [exchange(sent, axis, m) for m in range(1, lax.axis_size(axis))]
-        mine = mine + sum(part.astype(F32) for part in parts)
-    mine = mine.astype(BF16)
+        parts = [exchange(mine, axis, m) for m in range(1, lax.axis_size(axis))]
+        mine = mine.astype(F32) + sum(part.astype(F32) for part in parts)
+        mine = mine.astype(BF16)
     pieces = [mine] + [exchange(mine, planes, m) for m in (1, 2, 3)]
     theirs = swap_inner(jnp.stack(pieces))
     count = frames * count_tm * rows * count_height * columns
@@ -549,13 +571,15 @@
 
     from_inner = swap_inner(send_inner).reshape((frames + 2) * colors, 4, pixel_columns)
     from_outer = swap_outer(send_outer).reshape((frames + 2) * colors, 4, pixel_columns)
+    from_outer = jnp.where(at_end(heights), 0, from_outer)
     above = jnp.where(core == 0, from_outer, from_inner).astype(F32)
     below = jnp.where(core == 0, from_inner, from_outer).astype(F32)
     halo = jnp.concatenate([above, below], axis=1)
     early = pixels_early.reshape(frame_shape) + halo[: 2 * colors]
     late = pixels_own.reshape(frame_shape) + halo[2 * colors :]
     following = along_tm(early.astype(BF16), -1)
-    grad_pixels = late + following.astype(F32)
+    last = lax.axis_index(times) == count_tm - 1
+    grad_pixels = late + jnp.where(last, 0.0, following.astype(F32))
     return (
         features,
         grad_conv.reshape(conv_weight.shape),

time: 55.7 us -> 47.9 us (0.86)
  starting transfers between devices: 28.2 us -> 21 us
  waiting for transfers between devices: 15 us -> 13.7 us
  Pallas kernels: 10.3 us -> 11.2 us
    ppermute x4, starting transfers between devices: 8.64 us -> 1.11 us  [swap_inner(): return lax.ppermute(value, 'core', [(0, 1), (1, 0)])]
    ppermute x2, starting transfers between devices: 1.33 us -> 3.78 us  [swap_outer(): return lax.ppermute(value, times + heights, pairs)]
    ppermute x2, starting transfers between devices: 6.17 us -> 4.54 us  [along_tm(): return lax.ppermute(value, times, pairs)]
    ppermute x2, waiting for transfers between devices: 2.57 us -> 1.68 us  [along_tm(): return lax.ppermute(value, times, pairs)]
    pallas_call x2 -> x3, Pallas kernels: 2.23 us -> 3.08 us  [the longest x1 1.49 us: local(): call(functools.partial(main_kernel, dims, heights), [((chunk, WIDTH), F32...]
    ppermute x9, waiting for transfers between devices: 12.4 us -> 11.7 us  [exchange(): return lax.ppermute(value, axes, [(i, i ^ mask) for i in range(size)])]
  transfers between devices with their start and end apart: 17 -> 17, of which waited for: 11 -> 11; matrix products, arithmetic and copies ran while one was open for 2% -> 2% of each run, Pallas kernels for 13% -> 18%
where the time goes in v4:
time: 47.9 us; the launch traced here: 47.7 us
  starting transfers between devices  21 us (44%)
  waiting for transfers between devices  13.7 us (29%)
  Pallas kernels  11.2 us (23%)
  other arithmetic  1.03 us (2%)
  between operations  0.77 us (2%)
    ppermute x9, waiting for transfers between devices, exchange(): return lax.ppermute(value, axes, [(i, i ^ mask) for i in range(size)])  11.7 us
    ppermute x9, starting transfers between devices, exchange(): return lax.ppermute(value, axes, [(i, i ^ mask) for i in range(size)])  11.6 us
    ppermute x2, starting transfers between devices, along_tm(): return lax.ppermute(value, times, pairs)  4.54 us
    ppermute x2, starting transfers between devices, swap_outer(): return lax.ppermute(value, times + heights, pairs)  3.78 us
    pallas_call x1, Pallas kernels, local(): call(functools.partial(late_kernel, dims), [((frames, rows // 2, pair, wi...  2.16 us
    pallas_call x1, Pallas kernels, local(): call(functools.partial(first_kernel, dims, len(sources)), [(source.shape,...  2.12 us
    ppermute x2, waiting for transfers between devices, along_tm(): return lax.ppermute(value, times, pairs)  1.68 us
    pallas_call x1, Pallas kernels, local(): call(functools.partial(main_kernel, dims, heights), [((chunk, WIDTH), F32...  1.49 us
  transfers between devices with their start and end apart: 17, of which 11 were waited for; matrix products, arithmetic and copies ran while one was open for 2% of the time, Pallas kernels for 18%

profile of v4, /device:TPU:0, one launch (start us, length us, event | category | flops | bytes accessed | tf_op | source)
XLA Modules:
  0.0 47.7 jit_solution(13653508442942218651)
XLA Ops:
  0.6 3.0 %collective-permute-start = (bf16[48,1024]{1,0:T(8,128)(2,1)}, bf16[48,1024]{1,0:T(8,128)(2,1)S(1)}, u32[]{:S(2)}, u32[]{:S(2)}) collective-permute-start(bf16[48,1024]{1,0:T(8,128)(2,1)} %bitcast.40), channel_id=1, source_target_pairs={{0,16},{16,0},{1,17},{17,1},{2,18},{18,2},{3,19},{19,3},{4,20},{20... | collective-permute-start | bytes 294920 | tf_op jit(solution)/shard_map/ppermute | solution.py:430
  3.7 2.1 %shard_map.145 = (bf16[48,1024]{1,0:T(8,128)(2,1)S(1)}, bf16[512,512]{1,0:T(8,128)(2,1)S(1)}, bf16[192,192]{1,0:T(8,128)(2,1)S(1)}, bf16[512,256]{1,0:T(8,128)(2...) custom-call(bf16[27,48,128]{2,1,0:T(8,128)(2,1)} %bitcast.38, ...), custom_call_target="tpu_custom_call" | custom-call | flops 1000000000 | bytes 1048576 | tf_op jit(solution)/shard_map/pallas_call | solution.py:463
  5.8 0.9 %collective-permute-done.came = bf16[48,1024]{1,0:T(8,128)(2,1)S(1)} collective-permute-done((bf16[48,1024]{1,0:T(8,128)(2,1)}, bf16[48,1024]{1,0:T(8,128)(2,1)S(1)}, u32[]{:S(2)}, u32[]{:S(2)}) %collective-permute-start) | collective-permute-done | bytes 98336 | tf_op jit(solution)/shard_map/ppermute | solution.py:430
  7.0 1.9 %collective-permute-start.1 = (bf16[48,1024]{1,0:T(8,128)(2,1)S(1)}, bf16[48,1024]{1,0:T(8,128)(2,1)S(1)}, u32[]{:S(2)}, u32[]{:S(2)}) collective-permute-start(bf16[48,1024]{1,0:T(8,128)(2,1)S(1)} %get-tuple-element.50), channel_id=1, source_target_pairs={{1,2},{3,4},{5,6},{7,8},{9,10},{11,12},{13,14},{2,1},{4,3},{6,5},{... | collective-permute-start | bytes 294920 | tf_op jit(solution)/shard_map/ppermute | solution.py:441
  8.8 1.1 %shard_map.147 = (bf16[2,2,144,256]{3,2,1,0:T(8,128)(2,1)S(1)}, f32[2,2,128,256]{3,2,1,0:T(8,128)S(1)}) custom-call(bf16[48,1024]{1,0:T(8,128)(2,1)S(1)} %get-tuple-element.53.earlier, bf16[512,512]{1,0:T(8,128)(2,1)S(1)} %get-tuple-element.51.table.refs_0_, bf16[192,192]{1,0:T(8,128)(2,1)S(1)} %get-tuple-element.54.rows_own, ...), custom_call_target="tpu_custom_call" | custom-call | flops 1000000000 | bytes 1048576 | tf_op jit(solution)/shard_map/pallas_call | solution.py:485
  10.0 1.4 %shard_map.148 = (bf16[2,256,128]{2,1,0:T(8,128)(2,1)S(1)}, bf16[256,256]{1,0:T(8,128)(2,1)S(1)}, f32[1296,128]{1,0:T(8,128)S(1)}, f32[256,256]{1,0:T(8,128)S(1)}, f32[8,128]{1,0:T(8,128)S(1)}) custom-call(bf16[48,1024]{1,0:T(8,128)(2,1)S(1)} %collective-permute-done.2.halo, bf16[512,512]{1,0:T(8,128)(2,1)S(1)} %get-tuple-element.51.table.refs_0_, ...), custom_call_target="tpu_custom_call" | custom-call | flops 1000000000 | bytes 1048576 | tf_op jit(solution)/shard_map/pallas_call | solution.py:498
  11.6 1.5 %shard_map.149 = (f32[296,128]{1,0:T(8,128)S(1)}, f32[3,296,128]{2,1,0:T(8,128)S(1)}, bf16[4,296,128]{2,1,0:T(8,128)(2,1)S(1)}, bf16[2,2,256,128]{3,2,1,0:T(8,128)(2,1)S(1)}, bf16[2,256,256]{2,1,0:T(8,128)(2,1)S(1)}) custom-call(bf16[48,1024]{1,0:T(8,128)(2,1)S(1)} %collective-permute-done.1.halo, bf16[512,512]{1,0:T(8,128)(2,1)S(1)} %get-tuple-element.51.table.refs_0_, ...), custom_call_target="tpu_custom_call" | custom-call | flops 1000000000 | bytes 1048576 | tf_op jit(solution)/shard_map/pallas_call | solution.py:511
  14.2 1.9 %collective-permute-start.14 = (bf16[48,1024]{1,0:T(8,128)(2,1)S(1)}, bf16[48,1024]{1,0:T(8,128)(2,1)S(1)}, u32[]{:S(2)}, u32[]{:S(2)}) collective-permute-start(bf16[48,1024]{1,0:T(8,128)(2,1)S(1)} %get-tuple-element.87), channel_id=1, source_target_pairs={{1,2},{3,4},{5,6},{7,8},{9,10},{11,12},{13,14},{2,1},{4,3},{6,5},{... | collective-permute-start | bytes 294920 | tf_op jit(solution)/shard_map/ppermute | solution.py:441
  16.9 2.2 %shard_map.150 = (bf16[2,1,128,256]{3,2,1,0:T(8,128)(2,1)}, f32[48,1024]{1,0:T(8,128)S(1)}, f32[48,1024]{1,0:T(8,128)S(1)}) custom-call(bf16[2,2,256,128]{3,2,1,0:T(8,128)(2,1)S(1)} %get-tuple-element.69.acts, bf16[2,256,256]{2,1,0:T(8,128)(2,1)S(1)} %get-tuple-element.70.slopes, bf16[432,384]{1,0:T(8,128)(2,1)S(1)} %get-tuple-element.71.backward, ...), custom_call_target="tpu_custom_call" | custom-call | flops 1000000000 | bytes 1048576 | tf_op jit(solution)/shard_map/pallas_call | solution.py:528
  19.1 1.7 %collective-permute-start.4 = (bf16[296,128]{1,0:T(8,128)(2,1)S(1)}, bf16[296,128]{1,0:T(8,128)(2,1)S(1)}, u32[]{:S(2)}, u32[]{:S(2)}) collective-permute-start(bf16[296,128]{1,0:T(8,128)(2,1)S(1)} %get-tuple-element.90), channel_id=1, source_target_pairs={{0,2},{2,0},{16,18},{18,16},{1,3},{3,1},{17,19},{19,17},{4,6},{6,4... | collective-permute-start | bytes 227336 | tf_op jit(solution)/shard_map/ppermute | solution.py:445
  20.8 1.5 %collective-permute-start.5 = (bf16[296,128]{1,0:T(8,128)(2,1)S(1)}, bf16[296,128]{1,0:T(8,128)(2,1)S(1)}, u32[]{:S(2)}, u32[]{:S(2)}) collective-permute-start(bf16[296,128]{1,0:T(8,128)(2,1)S(1)} %get-tuple-element.92), channel_id=1, source_target_pairs={{0,16},{2,18},{16,0},{18,2},{1,17},{3,19},{17,1},{19,3},{4,20},{6,... | collective-permute-start | bytes 227336 | tf_op jit(solution)/shard_map/ppermute | solution.py:445
  23.6 2.3 %collective-permute-done.5 = bf16[296,128]{1,0:T(8,128)(2,1)S(1)} collective-permute-done((bf16[296,128]{1,0:T(8,128)(2,1)S(1)}, bf16[296,128]{1,0:T(8,128)(2,1)S(1)}, u32[]{:S(2)}, u32[]{:S(2)}) %collective-permute-start.5) | collective-permute-done | bytes 75808 | tf_op jit(solution)/shard_map/ppermute | solution.py:445
  25.8 1.8 %collective-permute-done.6 = bf16[296,128]{1,0:T(8,128)(2,1)S(1)} collective-permute-done((bf16[296,128]{1,0:T(8,128)(2,1)S(1)}, bf16[296,128]{1,0:T(8,128)(2,1)S(1)}, u32[]{:S(2)}, u32[]{:S(2)}) %collective-permute-start.6) | collective-permute-done | bytes 75808 | tf_op jit(solution)/shard_map/ppermute | solution.py:445
  27.7 1.6 %collective-permute-start.7 = (bf16[296,128]{1,0:T(8,128)(2,1)S(1)}, bf16[296,128]{1,0:T(8,128)(2,1)S(1)}, u32[]{:S(2)}, u32[]{:S(2)}) collective-permute-start(bf16[296,128]{1,0:T(8,128)(2,1)S(1)} %fusion.3), channel_id=1, source_target_pairs={{0,4},{4,0},{8,12},{12,8},{1,5},{5,1},{9,13},{13,9},{2,6},{6,2},{1... | collective-permute-start | bytes 227336 | tf_op jit(solution)/shard_map/ppermute | solution.py:445
  29.3 1.1 %collective-permute-start.8 = (bf16[296,128]{1,0:T(8,128)(2,1)S(1)}, bf16[296,128]{1,0:T(8,128)(2,1)S(1)}, u32[]{:S(2)}, u32[]{:S(2)}) collective-permute-start(bf16[296,128]{1,0:T(8,128)(2,1)S(1)} %fusion.3), channel_id=1, source_target_pairs={{0,8},{4,12},{8,0},{12,4},{1,9},{5,13},{9,1},{13,5},{2,10},{6,14},... | collective-permute-start | bytes 227336 | tf_op jit(solution)/shard_map/ppermute | solution.py:445
  30.4 1.7 %collective-permute-start.9 = (bf16[296,128]{1,0:T(8,128)(2,1)S(1)}, bf16[296,128]{1,0:T(8,128)(2,1)S(1)}, u32[]{:S(2)}, u32[]{:S(2)}) collective-permute-start(bf16[296,128]{1,0:T(8,128)(2,1)S(1)} %fusion.3), channel_id=1, source_target_pairs={{0,12},{4,8},{8,4},{12,0},{1,13},{5,9},{9,5},{13,1},{2,14},{6,10},... | collective-permute-start | bytes 227336 | tf_op jit(solution)/shard_map/ppermute | solution.py:445
  32.4 4.4 %collective-permute-done.8 = bf16[296,128]{1,0:T(8,128)(2,1)S(1)} collective-permute-done((bf16[296,128]{1,0:T(8,128)(2,1)S(1)}, bf16[296,128]{1,0:T(8,128)(2,1)S(1)}, u32[]{:S(2)}, u32[]{:S(2)}) %collective-permute-start.8) | collective-permute-done | bytes 75808 | tf_op jit(solution)/shard_map/ppermute | solution.py:445
  36.8 1.3 %collective-permute-start.10 = (bf16[296,128]{1,0:T(8,128)(2,1)S(1)}, bf16[296,128]{1,0:T(8,128)(2,1)S(1)}, u32[]{:S(2)}, u32[]{:S(2)}) collective-permute-start(bf16[296,128]{1,0:T(8,128)(2,1)S(1)} %add_convert_fusion.1.refs_0_), channel_id=1, source_target_pairs={{0,2},{2,0},{16,18},{18,16},{1,3},{3,1},{17,19},{19,17},{4,6},{6,4... | collective-permute-start | bytes 227336 | tf_op jit(solution)/shard_map/ppermute | solution.py:445
  38.1 0.9 %collective-permute-start.11 = (bf16[296,128]{1,0:T(8,128)(2,1)S(1)}, bf16[296,128]{1,0:T(8,128)(2,1)S(1)}, u32[]{:S(2)}, u32[]{:S(2)}) collective-permute-start(bf16[296,128]{1,0:T(8,128)(2,1)S(1)} %add_convert_fusion.1.refs_0_), channel_id=1, source_target_pairs={{0,16},{2,18},{16,0},{18,2},{1,17},{3,19},{17,1},{19,3},{4,20},{6,... | collective-permute-start | bytes 227336 | tf_op jit(solution)/shard_map/ppermute | solution.py:445
  39.0 1.4 %collective-permute-start.12 = (bf16[296,128]{1,0:T(8,128)(2,1)S(1)}, bf16[296,128]{1,0:T(8,128)(2,1)S(1)}, u32[]{:S(2)}, u32[]{:S(2)}) collective-permute-start(bf16[296,128]{1,0:T(8,128)(2,1)S(1)} %add_convert_fusion.1.refs_0_), channel_id=1, source_target_pairs={{0,18},{2,16},{16,2},{18,0},{1,19},{3,17},{17,3},{19,1},{4,22},{6,... | collective-permute-start | bytes 227336 | tf_op jit(solution)/shard_map/ppermute | solution.py:445
  40.4 1.5 %collective-permute-start.16 = (bf16[6,8,1024]{2,1,0:T(8,128)(2,1)S(1)}, bf16[6,8,1024]{2,1,0:T(8,128)(2,1)S(1)}, u32[]{:S(2)}, u32[]{:S(2)}) collective-permute-start(bf16[6,8,1024]{2,1,0:T(8,128)(2,1)S(1)} %fusion), channel_id=1, source_target_pairs={{0,16},{16,0},{1,17},{17,1},{2,18},{18,2},{3,19},{19,3},{4,20},{20... | collective-permute-start | bytes 294920 | tf_op jit(solution)/shard_map/ppermute | solution.py:430
  42.5 1.7 %collective-permute-done.12.refs_3_ = bf16[296,128]{1,0:T(8,128)(2,1)S(1)} collective-permute-done((bf16[296,128]{1,0:T(8,128)(2,1)S(1)}, bf16[296,128]{1,0:T(8,128)(2,1)S(1)}, u32[]{:S(2)}, u32[]{:S(2)}) %collective-permute-start.12) | collective-permute-done | bytes 75808 | tf_op jit(solution)/shard_map/ppermute | solution.py:445
  45.9 0.9 %shard_map.151 = (f32[1296,128]{1,0:T(8,128)}, f32[1,128]{1,0:T(1,128)}, f32[512,256]{1,0:T(8,128)}, f32[1,256]{1,0:T(1,128)}) custom-call(bf16[296,128]{1,0:T(8,128)(2,1)S(1)} %add_convert_fusion.1.refs_0_, bf16[296,128]{1,0:T(8,128)(2,1)S(1)} %collective-permute-done.10.refs_1_, bf16[296,128]{1,0:T(8,128)(2,1)S(1)} %collective-permute-done.11.refs_2_, ...), custom_call_target="tpu_custom_call" | custom-call | bytes 1048576 | tf_op jit(solution)/shard_map/pallas_call | solution.py:560
  46.8 0.9 %shard_map.152 = (f32[1296,128]{1,0:T(8,128)}, f32[1,128]{1,0:T(1,128)}, f32[512,256]{1,0:T(8,128)}, f32[1,256]{1,0:T(1,128)}) custom-call(bf16[4,296,128]{2,1,0:T(8,128)(2,1)S(1)} %collective-permute-done.13.refs_0_, f32[1296,128]{1,0:T(8,128)} %get-tuple-element.78.refs_1_, ...), custom_call_target="tpu_custom_call", output_to_operand_aliasing={{0}: (1, {}), {1}: (2, {}), {2}: (3, {}), {3}: (4, {})} | custom-call | bytes 1048576 | tf_op jit(solution)/shard_map/pallas_call | solution.py:563
  (30 shorter events, 6.3 us)
Async XLA Ops:
  0.6 6.0 %collective-permute-start = (bf16[48,1024]{1,0:T(8,128)(2,1)}, bf16[48,1024]{1,0:T(8,128)(2,1)S(1)}, u32[]{:S(2)}, u32[]{:S(2)}) collective-permute-start(bf16[48,1024]{1,0:T(8,128)(2,1)} %bitcast.40), channel_id=1, source_target_pairs={{0,16},{16,0},{1,17},{17,1},{2,18},{18,2},{3,19},{19,3},{4,20},{20... | collective-permute-start | bytes 294920 | tf_op jit(solution)/shard_map/ppermute | solution.py:430
  6.9 3.1 %collective-permute-start.2 = (bf16[48,1024]{1,0:T(8,128)(2,1)S(1)}, bf16[48,1024]{1,0:T(8,128)(2,1)S(1)}, u32[]{:S(2)}, u32[]{:S(2)}) collective-permute-start(bf16[48,1024]{1,0:T(8,128)(2,1)S(1)} %get-tuple-element.63), channel_id=1, source_target_pairs={{0,1},{1,0},{2,3},{3,2},{4,5},{5,4},{6,7},{7,6},{8,9},{9,8},{10,11... | collective-permute-start | bytes 294920 | tf_op jit(solution)/shard_map/ppermute | solution.py:433
  7.0 4.7 %collective-permute-start.1 = (bf16[48,1024]{1,0:T(8,128)(2,1)S(1)}, bf16[48,1024]{1,0:T(8,128)(2,1)S(1)}, u32[]{:S(2)}, u32[]{:S(2)}) collective-permute-start(bf16[48,1024]{1,0:T(8,128)(2,1)S(1)} %get-tuple-element.50), channel_id=1, source_target_pairs={{1,2},{3,4},{5,6},{7,8},{9,10},{11,12},{13,14},{2,1},{4,3},{6,5},{... | collective-permute-start | bytes 294920 | tf_op jit(solution)/shard_map/ppermute | solution.py:441
  13.1 5.9 %collective-permute-start.3 = (bf16[4,296,128]{2,1,0:T(8,128)(2,1)S(1)}, bf16[4,296,128]{2,1,0:T(8,128)(2,1)S(1)}, u32[]{:S(2)}, u32[]{:S(2)}) collective-permute-start(bf16[4,296,128]{2,1,0:T(8,128)(2,1)S(1)} %get-tuple-element.76), channel_id=1, source_target_pairs={{0,1},{1,0},{2,3},{3,2},{4,5},{5,4},{6,7},{7,6},{8,9},{9,8},{10,11... | collective-permute-start | bytes 909320 | tf_op jit(solution)/shard_map/ppermute | solution.py:433
  14.2 8.5 %collective-permute-start.14 = (bf16[48,1024]{1,0:T(8,128)(2,1)S(1)}, bf16[48,1024]{1,0:T(8,128)(2,1)S(1)}, u32[]{:S(2)}, u32[]{:S(2)}) collective-permute-start(bf16[48,1024]{1,0:T(8,128)(2,1)S(1)} %get-tuple-element.87), channel_id=1, source_target_pairs={{1,2},{3,4},{5,6},{7,8},{9,10},{11,12},{13,14},{2,1},{4,3},{6,5},{... | collective-permute-start | bytes 294920 | tf_op jit(solution)/shard_map/ppermute | solution.py:441
  16.1 6.6 %collective-permute-start.15 = (bf16[48,1024]{1,0:T(8,128)(2,1)S(1)}, bf16[48,1024]{1,0:T(8,128)(2,1)S(1)}, u32[]{:S(2)}, u32[]{:S(2)}) collective-permute-start(bf16[48,1024]{1,0:T(8,128)(2,1)S(1)} %get-tuple-element.88), channel_id=1, source_target_pairs={{0,1},{1,0},{2,3},{3,2},{4,5},{5,4},{6,7},{7,6},{8,9},{9,8},{10,11... | collective-permute-start | bytes 294920 | tf_op jit(solution)/shard_map/ppermute | solution.py:433
  19.1 4.4 %collective-permute-start.4 = (bf16[296,128]{1,0:T(8,128)(2,1)S(1)}, bf16[296,128]{1,0:T(8,128)(2,1)S(1)}, u32[]{:S(2)}, u32[]{:S(2)}) collective-permute-start(bf16[296,128]{1,0:T(8,128)(2,1)S(1)} %get-tuple-element.90), channel_id=1, source_target_pairs={{0,2},{2,0},{16,18},{18,16},{1,3},{3,1},{17,19},{19,17},{4,6},{6,4... | collective-permute-start | bytes 227336 | tf_op jit(solution)/shard_map/ppermute | solution.py:445
  20.8 5.0 %collective-permute-start.5 = (bf16[296,128]{1,0:T(8,128)(2,1)S(1)}, bf16[296,128]{1,0:T(8,128)(2,1)S(1)}, u32[]{:S(2)}, u32[]{:S(2)}) collective-permute-start(bf16[296,128]{1,0:T(8,128)(2,1)S(1)} %get-tuple-element.92), channel_id=1, source_target_pairs={{0,16},{2,18},{16,0},{18,2},{1,17},{3,19},{17,1},{19,3},{4,20},{6,... | collective-permute-start | bytes 227336 | tf_op jit(solution)/shard_map/ppermute | solution.py:445
  22.3 5.3 %collective-permute-start.6 = (bf16[296,128]{1,0:T(8,128)(2,1)S(1)}, bf16[296,128]{1,0:T(8,128)(2,1)S(1)}, u32[]{:S(2)}, u32[]{:S(2)}) collective-permute-start(bf16[296,128]{1,0:T(8,128)(2,1)S(1)} %get-tuple-element.91), channel_id=1, source_target_pairs={{0,18},{2,16},{16,2},{18,0},{1,19},{3,17},{17,3},{19,1},{4,22},{6,... | collective-permute-start | bytes 227336 | tf_op jit(solution)/shard_map/ppermute | solution.py:445
  27.7 4.7 %collective-permute-start.7 = (bf16[296,128]{1,0:T(8,128)(2,1)S(1)}, bf16[296,128]{1,0:T(8,128)(2,1)S(1)}, u32[]{:S(2)}, u32[]{:S(2)}) collective-permute-start(bf16[296,128]{1,0:T(8,128)(2,1)S(1)} %fusion.3), channel_id=1, source_target_pairs={{0,4},{4,0},{8,12},{12,8},{1,5},{5,1},{9,13},{13,9},{2,6},{6,2},{1... | collective-permute-start | bytes 227336 | tf_op jit(solution)/shard_map/ppermute | solution.py:445
  29.3 7.4 %collective-permute-start.8 = (bf16[296,128]{1,0:T(8,128)(2,1)S(1)}, bf16[296,128]{1,0:T(8,128)(2,1)S(1)}, u32[]{:S(2)}, u32[]{:S(2)}) collective-permute-start(bf16[296,128]{1,0:T(8,128)(2,1)S(1)} %fusion.3), channel_id=1, source_target_pairs={{0,8},{4,12},{8,0},{12,4},{1,9},{5,13},{9,1},{13,5},{2,10},{6,14},... | collective-permute-start | bytes 227336 | tf_op jit(solution)/shard_map/ppermute | solution.py:445
  30.4 6.3 %collective-permute-start.9 = (bf16[296,128]{1,0:T(8,128)(2,1)S(1)}, bf16[296,128]{1,0:T(8,128)(2,1)S(1)}, u32[]{:S(2)}, u32[]{:S(2)}) collective-permute-start(bf16[296,128]{1,0:T(8,128)(2,1)S(1)} %fusion.3), channel_id=1, source_target_pairs={{0,12},{4,8},{8,4},{12,0},{1,13},{5,9},{9,5},{13,1},{2,14},{6,10},... | collective-permute-start | bytes 227336 | tf_op jit(solution)/shard_map/ppermute | solution.py:445
  36.8 5.3 %collective-permute-start.10 = (bf16[296,128]{1,0:T(8,128)(2,1)S(1)}, bf16[296,128]{1,0:T(8,128)(2,1)S(1)}, u32[]{:S(2)}, u32[]{:S(2)}) collective-permute-start(bf16[296,128]{1,0:T(8,128)(2,1)S(1)} %add_convert_fusion.1.refs_0_), channel_id=1, source_target_pairs={{0,2},{2,0},{16,18},{18,16},{1,3},{3,1},{17,19},{19,17},{4,6},{6,4... | collective-permute-start | bytes 227336 | tf_op jit(solution)/shard_map/ppermute | solution.py:445
  38.1 4.5 %collective-permute-start.11 = (bf16[296,128]{1,0:T(8,128)(2,1)S(1)}, bf16[296,128]{1,0:T(8,128)(2,1)S(1)}, u32[]{:S(2)}, u32[]{:S(2)}) collective-permute-start(bf16[296,128]{1,0:T(8,128)(2,1)S(1)} %add_convert_fusion.1.refs_0_), channel_id=1, source_target_pairs={{0,16},{2,18},{16,0},{18,2},{1,17},{3,19},{17,1},{19,3},{4,20},{6,... | collective-permute-start | bytes 227336 | tf_op jit(solution)/shard_map/ppermute | solution.py:445
  39.0 5.3 %collective-permute-start.12 = (bf16[296,128]{1,0:T(8,128)(2,1)S(1)}, bf16[296,128]{1,0:T(8,128)(2,1)S(1)}, u32[]{:S(2)}, u32[]{:S(2)}) collective-permute-start(bf16[296,128]{1,0:T(8,128)(2,1)S(1)} %add_convert_fusion.1.refs_0_), channel_id=1, source_target_pairs={{0,18},{2,16},{16,2},{18,0},{1,19},{3,17},{17,3},{19,1},{4,22},{6,... | collective-permute-start | bytes 227336 | tf_op jit(solution)/shard_map/ppermute | solution.py:445
  40.4 4.8 %collective-permute-start.16 = (bf16[6,8,1024]{2,1,0:T(8,128)(2,1)S(1)}, bf16[6,8,1024]{2,1,0:T(8,128)(2,1)S(1)}, u32[]{:S(2)}, u32[]{:S(2)}) collective-permute-start(bf16[6,8,1024]{2,1,0:T(8,128)(2,1)S(1)} %fusion), channel_id=1, source_target_pairs={{0,16},{16,0},{1,17},{17,1},{2,18},{18,2},{3,19},{19,3},{4,20},{20... | collective-permute-start | bytes 294920 | tf_op jit(solution)/shard_map/ppermute | solution.py:430
  44.3 2.5 %collective-permute-start.13 = (bf16[4,296,128]{2,1,0:T(8,128)(2,1)S(1)}, bf16[4,296,128]{2,1,0:T(8,128)(2,1)S(1)}, u32[]{:S(2)}, u32[]{:S(2)}) collective-permute-start(bf16[4,296,128]{2,1,0:T(8,128)(2,1)S(1)} %pad_maximum_fusion), channel_id=1, source_target_pairs={{0,1},{1,0},{2,3},{3,2},{4,5},{5,4},{6,7},{7,6},{8,9},{9,8},{10,11... | collective-permute-start | bytes 909320 | tf_op jit(solution)/shard_map/ppermute | solution.py:433

commit v5 on v4

--- a/solution.py
+++ b/solution.py
@@ -29,8 +29,9 @@
     return high, (x - high.astype(F32)).astype(BF16)
 
 
-def position():
-    return lax.axis_index("core"), 2 * lax.axis_index("tm_lo") + lax.axis_index("y")
+def order_of(core):
+    plane = 2 * lax.axis_index("tm_lo") + lax.axis_index("y")
+    return jnp.where(core == 0, plane, lax.axis_index("z_0"))
 
 
 def call(body, outs, ins, scratch=(), flops=0, grant=24, **more):
@@ -172,7 +173,7 @@
 
 
 def pack_kernel(times, own, came, chosen, inner, outer, earlier):
-    core, _ = position()
+    core = lax.axis_index("core")
     used = jnp.where(lax.axis_index(times) == 0, 0.0, 1.0)
     earlier[...] = (came[...].astype(F32) * used).astype(BF16)
     both = mm(chosen[core], jnp.concatenate([earlier[...], own[...]], axis=0)).astype(BF16)
@@ -249,7 +250,7 @@
 def mid_kernel(dims, halo, *refs):
     table, rows_halo, x_early, x_own, pre_own, dact, outside, cotangent = refs[:8]
     acts, slopes, conv, down, total, x = refs[8:]
-    core, _ = position()
+    core = lax.axis_index("core")
     conv[...], down[...], total[...] = one_row(
         dims, 1 - core, halo[...], *refs[:8], acts, slopes, x
     )
@@ -264,7 +265,7 @@
     frames, rows, pair = dims
     _, _, _, _, _, _, _, cotangent = refs[:8]
     acts_in, slopes_in, conv_in, down_in, total_in, mine, keep, give, acts, slopes, x, packed = refs[8:]
-    core, plane = position()
+    core = lax.axis_index("core")
     halo = (halo[...].astype(F32) * jnp.where(at_end(heights), 0.0, 1.0)).astype(BF16)
     acts[1 - core] = acts_in[...]
     slopes[1 - core] = slopes_in[...]
@@ -293,11 +294,12 @@
         if rest:
             packed[h, half + down_rows + 8 :] = jnp.zeros((rest, WIDTH), F32)
     for m in range(4):
-        at = pl.multiple_of(jnp.bitwise_xor(plane, m) * chunk, 8)
+        at = pl.multiple_of(jnp.bitwise_xor(order_of(core), m) * chunk, 8)
         if m:
             keep[m - 1] = packed[core, pl.ds(at, chunk)]
         else:
             mine[...] = packed[core, pl.ds(at, chunk)]
+        at = pl.multiple_of(jnp.bitwise_xor(order_of(1 - core), m) * chunk, 8)
         give[m] = packed[1 - core, pl.ds(at, chunk)].astype(BF16)
 
 
@@ -331,7 +333,7 @@
 
 def edge_kernel(dims, slopes, backward, table, rows_halo, send_inner, send_outer):
     frames, rows, pair = dims
-    core, _ = position()
+    core = lax.axis_index("core")
     total = {}
     spread_slope(total, slopes, backward, frames, [(0, 0, 0), (rows - 1, 2, 1)], pair)
     groups = [
@@ -374,11 +376,11 @@
     pieces, (conv, conv_bias, down, down_bias, flat, sums, sems) = refs[:4], refs[-7:]
     if other:
         pieces = [refs[0].at[m] for m in range(4)]
-    core, plane = position()
+    core = lax.axis_index("core")
     which = 1 - core if other else core
     chunk = pieces[0].shape[0]
     for m in range(4):
-        at = pl.multiple_of(jnp.bitwise_xor(plane, m) * chunk, 8)
+        at = pl.multiple_of(jnp.bitwise_xor(order_of(which), m) * chunk, 8)
         flat[pl.ds(at, chunk)] = pieces[m][...].astype(F32) * scale
     half, down_rows = conv.shape[0] // 2, down.shape[0]
     at = pl.multiple_of(half * which, 8)
@@ -532,17 +534,32 @@
         flops=10**9,
     )(acts, slopes, backward, down_flat, bias2, table, rows_own)
 
+    def cross(value, mask, first):
+        names = times + heights
+        sizes = [lax.axis_size(axis) for axis in names]
+        pairs = []
+        for source in range(math.prod(sizes)):
+            at = dict(zip(names, np.unravel_index(source, sizes)))
+            if (at["core"] == 0) == first:
+                at["tm_lo"], at["y"] = at["tm_lo"] ^ (mask >> 1), at["y"] ^ (mask & 1)
+            else:
+                at["z_0"] ^= mask
+            target = np.ravel_multi_index([at[axis] for axis in names], sizes)
+            pairs.append((source, int(target)))
+        return lax.ppermute(value, names, pairs)
+
     given = swap_inner(give)
     rest = (keep + given[1:].astype(F32)).astype(BF16)
-    planes = ("tm_lo", "y")
-    parts = [exchange(rest[m - 1], planes, m) for m in (1, 2, 3)]
+    steps = (1, 2, 3)
+    parts = [cross(rest[m - 1], m, True) for m in steps]
     mine = mine + given[0].astype(F32) + sum(part.astype(F32) for part in parts)
     mine = mine.astype(BF16)
+    parts = [cross(mine, m, False) for m in steps]
+    mine = (mine.astype(F32) + sum(part.astype(F32) for part in parts)).astype(BF16)
     for axis in axes["rest"]:
         parts = [exchange(mine, axis, m) for m in range(1, lax.axis_size(axis))]
-        mine = mine.astype(F32) + sum(part.astype(F32) for part in parts)
-        mine = mine.astype(BF16)
-    pieces = [mine] + [exchange(mine, planes, m) for m in (1, 2, 3)]
+        mine = (mine.astype(F32) + sum(part.astype(F32) for part in parts)).astype(BF16)
+    pieces = [mine] + [cross(mine, m, True) for m in steps]
     theirs = swap_inner(jnp.stack(pieces))
     count = frames * count_tm * rows * count_height * columns
     scale = 1.0 / math.sqrt(count)
@@ -603,12 +620,13 @@
 def solution(mesh):
     count_tm, count_height = mesh.shape["tm"], mesh.shape["height"]
     tm_parts, height_parts = factors(count_tm // 2), factors(count_height // 4)
+    assert height_parts[0] == 4
     tm_names = tuple(f"tm_{n}" for n in range(len(tm_parts)))
     height_names = tuple(f"z_{n}" for n in range(len(height_parts)))
     axes = {
         "tm": tm_names + ("tm_lo",),
         "height": height_names + ("y", "core"),
-        "rest": tm_names + height_names,
+        "rest": tm_names + height_names[1:],
     }
     fine = Mesh(
         mesh.devices.reshape(tm_parts + [2] + height_parts + [2, 2]), axes["tm"] + axes["height"]

time: 47.9 us -> 47.7 us (level)
  starting transfers between devices: 21 us -> 20.2 us
  waiting for transfers between devices: 13.7 us -> 14.3 us
    ppermute x2, starting transfers between devices: 4.54 us -> 3.74 us  [along_tm(): return lax.ppermute(value, times, pairs)]
where the time goes in v5:
time: 47.7 us; the launch traced here: 47.6 us
  starting transfers between devices  20.2 us (42%)
  waiting for transfers between devices  14.3 us (30%)
  Pallas kernels  11.2 us (23%)
  other arithmetic  1.03 us (2%)
  between operations  0.77 us (2%)
    ppermute x9, waiting for transfers between devices, cross(): return lax.ppermute(value, names, pairs)  12 us
    ppermute x9, starting transfers between devices, cross(): return lax.ppermute(value, names, pairs)  11.6 us
    ppermute x2, starting transfers between devices, swap_outer(): return lax.ppermute(value, times + heights, pairs)  3.76 us
    ppermute x2, starting transfers between devices, along_tm(): return lax.ppermute(value, times, pairs)  3.74 us
    pallas_call x1, Pallas kernels, local(): call(functools.partial(late_kernel, dims), [((frames, rows // 2, pair, wi...  2.16 us
    pallas_call x1, Pallas kernels, local(): call(functools.partial(first_kernel, dims, len(sources)), [(source.shape,...  2.12 us
    ppermute x2, waiting for transfers between devices, along_tm(): return lax.ppermute(value, times, pairs)  1.95 us
    pallas_call x1, Pallas kernels, local(): call(functools.partial(main_kernel, dims, heights), [((chunk, WIDTH), F32...  1.49 us
  transfers between devices with their start and end apart: 17, of which 11 were waited for; matrix products, arithmetic and copies ran while one was open for 2% of the time, Pallas kernels for 18%

profile of v5, /device:TPU:0, one launch (start us, length us, event | category | flops | bytes accessed | tf_op | source)
XLA Modules:
  0.0 47.6 jit_solution(11541432083924721180)
XLA Ops:
  0.6 3.0 %collective-permute-start = (bf16[48,1024]{1,0:T(8,128)(2,1)}, bf16[48,1024]{1,0:T(8,128)(2,1)S(1)}, u32[]{:S(2)}, u32[]{:S(2)}) collective-permute-start(bf16[48,1024]{1,0:T(8,128)(2,1)} %bitcast.40), channel_id=1, source_target_pairs={{0,16},{16,0},{1,17},{17,1},{2,18},{18,2},{3,19},{19,3},{4,20},{20... | collective-permute-start | bytes 294920 | tf_op jit(solution)/shard_map/ppermute | solution.py:432
  3.7 2.1 %shard_map.145 = (bf16[48,1024]{1,0:T(8,128)(2,1)S(1)}, bf16[512,512]{1,0:T(8,128)(2,1)S(1)}, bf16[192,192]{1,0:T(8,128)(2,1)S(1)}, bf16[512,256]{1,0:T(8,128)(2...) custom-call(bf16[27,48,128]{2,1,0:T(8,128)(2,1)} %bitcast.38, ...), custom_call_target="tpu_custom_call" | custom-call | flops 1000000000 | bytes 1048576 | tf_op jit(solution)/shard_map/pallas_call | solution.py:465
  7.0 1.9 %collective-permute-start.1 = (bf16[48,1024]{1,0:T(8,128)(2,1)S(1)}, bf16[48,1024]{1,0:T(8,128)(2,1)S(1)}, u32[]{:S(2)}, u32[]{:S(2)}) collective-permute-start(bf16[48,1024]{1,0:T(8,128)(2,1)S(1)} %get-tuple-element.50), channel_id=1, source_target_pairs={{1,2},{3,4},{5,6},{7,8},{9,10},{11,12},{13,14},{2,1},{4,3},{6,5},{... | collective-permute-start | bytes 294920 | tf_op jit(solution)/shard_map/ppermute | solution.py:443
  8.8 1.1 %shard_map.147 = (bf16[2,2,144,256]{3,2,1,0:T(8,128)(2,1)S(1)}, f32[2,2,128,256]{3,2,1,0:T(8,128)S(1)}) custom-call(bf16[48,1024]{1,0:T(8,128)(2,1)S(1)} %get-tuple-element.53.earlier, bf16[512,512]{1,0:T(8,128)(2,1)S(1)} %get-tuple-element.51.table.refs_0_, bf16[192,192]{1,0:T(8,128)(2,1)S(1)} %get-tuple-element.54.rows_own, ...), custom_call_target="tpu_custom_call" | custom-call | flops 1000000000 | bytes 1048576 | tf_op jit(solution)/shard_map/pallas_call | solution.py:487
  10.0 1.4 %shard_map.148 = (bf16[2,256,128]{2,1,0:T(8,128)(2,1)S(1)}, bf16[256,256]{1,0:T(8,128)(2,1)S(1)}, f32[1296,128]{1,0:T(8,128)S(1)}, f32[256,256]{1,0:T(8,128)S(1)}, f32[8,128]{1,0:T(8,128)S(1)}) custom-call(bf16[48,1024]{1,0:T(8,128)(2,1)S(1)} %collective-permute-done.2.halo, bf16[512,512]{1,0:T(8,128)(2,1)S(1)} %get-tuple-element.51.table.refs_0_, ...), custom_call_target="tpu_custom_call" | custom-call | flops 1000000000 | bytes 1048576 | tf_op jit(solution)/shard_map/pallas_call | solution.py:500
  11.6 1.5 %shard_map.149 = (f32[296,128]{1,0:T(8,128)S(1)}, f32[3,296,128]{2,1,0:T(8,128)S(1)}, bf16[4,296,128]{2,1,0:T(8,128)(2,1)S(1)}, bf16[2,2,256,128]{3,2,1,0:T(8,128)(2,1)S(1)}, bf16[2,256,256]{2,1,0:T(8,128)(2,1)S(1)}) custom-call(bf16[48,1024]{1,0:T(8,128)(2,1)S(1)} %collective-permute-done.1.halo, bf16[512,512]{1,0:T(8,128)(2,1)S(1)} %get-tuple-element.51.table.refs_0_, ...), custom_call_target="tpu_custom_call" | custom-call | flops 1000000000 | bytes 1048576 | tf_op jit(solution)/shard_map/pallas_call | solution.py:513
  14.2 1.9 %collective-permute-start.14 = (bf16[48,1024]{1,0:T(8,128)(2,1)S(1)}, bf16[48,1024]{1,0:T(8,128)(2,1)S(1)}, u32[]{:S(2)}, u32[]{:S(2)}) collective-permute-start(bf16[48,1024]{1,0:T(8,128)(2,1)S(1)} %get-tuple-element.87), channel_id=1, source_target_pairs={{1,2},{3,4},{5,6},{7,8},{9,10},{11,12},{13,14},{2,1},{4,3},{6,5},{... | collective-permute-start | bytes 294920 | tf_op jit(solution)/shard_map/ppermute | solution.py:443
  16.9 2.2 %shard_map.150 = (bf16[2,1,128,256]{3,2,1,0:T(8,128)(2,1)}, f32[48,1024]{1,0:T(8,128)S(1)}, f32[48,1024]{1,0:T(8,128)S(1)}) custom-call(bf16[2,2,256,128]{3,2,1,0:T(8,128)(2,1)S(1)} %get-tuple-element.69.acts, bf16[2,256,256]{2,1,0:T(8,128)(2,1)S(1)} %get-tuple-element.70.slopes, bf16[432,384]{1,0:T(8,128)(2,1)S(1)} %get-tuple-element.71.backward, ...), custom_call_target="tpu_custom_call" | custom-call | flops 1000000000 | bytes 1048576 | tf_op jit(solution)/shard_map/pallas_call | solution.py:530
  19.1 1.7 %collective-permute-start.4 = (bf16[296,128]{1,0:T(8,128)(2,1)S(1)}, bf16[296,128]{1,0:T(8,128)(2,1)S(1)}, u32[]{:S(2)}, u32[]{:S(2)}) collective-permute-start(bf16[296,128]{1,0:T(8,128)(2,1)S(1)} %get-tuple-element.90), channel_id=1, source_target_pairs={{0,2},{1,5},{2,0},{3,7},{4,6},{5,1},{6,4},{7,3},{8,10},{9,13},{10,... | collective-permute-start | bytes 227336 | tf_op jit(solution)/shard_map/ppermute | solution.py:549
  20.8 1.5 %collective-permute-start.5 = (bf16[296,128]{1,0:T(8,128)(2,1)S(1)}, bf16[296,128]{1,0:T(8,128)(2,1)S(1)}, u32[]{:S(2)}, u32[]{:S(2)}) collective-permute-start(bf16[296,128]{1,0:T(8,128)(2,1)S(1)} %get-tuple-element.92), channel_id=1, source_target_pairs={{0,16},{1,9},{2,18},{3,11},{4,20},{5,13},{6,22},{7,15},{8,24},{9,1... | collective-permute-start | bytes 227336 | tf_op jit(solution)/shard_map/ppermute | solution.py:549
  23.6 1.7 %collective-permute-done.5 = bf16[296,128]{1,0:T(8,128)(2,1)S(1)} collective-permute-done((bf16[296,128]{1,0:T(8,128)(2,1)S(1)}, bf16[296,128]{1,0:T(8,128)(2,1)S(1)}, u32[]{:S(2)}, u32[]{:S(2)}) %collective-permute-start.5) | collective-permute-done | bytes 75808 | tf_op jit(solution)/shard_map/ppermute | solution.py:549
  25.2 2.4 %collective-permute-done.6 = bf16[296,128]{1,0:T(8,128)(2,1)S(1)} collective-permute-done((bf16[296,128]{1,0:T(8,128)(2,1)S(1)}, bf16[296,128]{1,0:T(8,128)(2,1)S(1)}, u32[]{:S(2)}, u32[]{:S(2)}) %collective-permute-start.6) | collective-permute-done | bytes 75808 | tf_op jit(solution)/shard_map/ppermute | solution.py:549
  27.7 1.6 %collective-permute-start.7 = (bf16[296,128]{1,0:T(8,128)(2,1)S(1)}, bf16[296,128]{1,0:T(8,128)(2,1)S(1)}, u32[]{:S(2)}, u32[]{:S(2)}) collective-permute-start(bf16[296,128]{1,0:T(8,128)(2,1)S(1)} %fusion.3), channel_id=1, source_target_pairs={{0,4},{1,3},{2,6},{3,1},{4,0},{5,7},{6,2},{7,5},{8,12},{9,11},{10,... | collective-permute-start | bytes 227336 | tf_op jit(solution)/shard_map/ppermute | solution.py:549
  29.3 1.1 %collective-permute-start.8 = (bf16[296,128]{1,0:T(8,128)(2,1)S(1)}, bf16[296,128]{1,0:T(8,128)(2,1)S(1)}, u32[]{:S(2)}, u32[]{:S(2)}) collective-permute-start(bf16[296,128]{1,0:T(8,128)(2,1)S(1)} %fusion.3), channel_id=1, source_target_pairs={{0,8},{1,17},{2,10},{3,19},{4,12},{5,21},{6,14},{7,23},{8,0},{9,25... | collective-permute-start | bytes 227336 | tf_op jit(solution)/shard_map/ppermute | solution.py:549
  30.4 1.7 %collective-permute-start.9 = (bf16[296,128]{1,0:T(8,128)(2,1)S(1)}, bf16[296,128]{1,0:T(8,128)(2,1)S(1)}, u32[]{:S(2)}, u32[]{:S(2)}) collective-permute-start(bf16[296,128]{1,0:T(8,128)(2,1)S(1)} %fusion.3), channel_id=1, source_target_pairs={{0,12},{1,19},{2,14},{3,17},{4,8},{5,23},{6,10},{7,21},{8,4},{9,27... | collective-permute-start | bytes 227336 | tf_op jit(solution)/shard_map/ppermute | solution.py:549
  32.3 3.2 %collective-permute-done.8 = bf16[296,128]{1,0:T(8,128)(2,1)S(1)} collective-permute-done((bf16[296,128]{1,0:T(8,128)(2,1)S(1)}, bf16[296,128]{1,0:T(8,128)(2,1)S(1)}, u32[]{:S(2)}, u32[]{:S(2)}) %collective-permute-start.8) | collective-permute-done | bytes 75808 | tf_op jit(solution)/shard_map/ppermute | solution.py:549
  35.4 1.3 %collective-permute-done.9 = bf16[296,128]{1,0:T(8,128)(2,1)S(1)} collective-permute-done((bf16[296,128]{1,0:T(8,128)(2,1)S(1)}, bf16[296,128]{1,0:T(8,128)(2,1)S(1)}, u32[]{:S(2)}, u32[]{:S(2)}) %collective-permute-start.9) | collective-permute-done | bytes 75808 | tf_op jit(solution)/shard_map/ppermute | solution.py:549
  36.7 1.2 %collective-permute-start.10 = (bf16[296,128]{1,0:T(8,128)(2,1)S(1)}, bf16[296,128]{1,0:T(8,128)(2,1)S(1)}, u32[]{:S(2)}, u32[]{:S(2)}) collective-permute-start(bf16[296,128]{1,0:T(8,128)(2,1)S(1)} %add_convert_fusion.1.refs_0_), channel_id=1, source_target_pairs={{0,2},{1,5},{2,0},{3,7},{4,6},{5,1},{6,4},{7,3},{8,10},{9,13},{10,... | collective-permute-start | bytes 227336 | tf_op jit(solution)/shard_map/ppermute | solution.py:549
  38.5 1.8 %collective-permute-start.12 = (bf16[296,128]{1,0:T(8,128)(2,1)S(1)}, bf16[296,128]{1,0:T(8,128)(2,1)S(1)}, u32[]{:S(2)}, u32[]{:S(2)}) collective-permute-start(bf16[296,128]{1,0:T(8,128)(2,1)S(1)} %add_convert_fusion.1.refs_0_), channel_id=1, source_target_pairs={{0,18},{1,13},{2,16},{3,15},{4,22},{5,9},{6,20},{7,11},{8,26},{9,5... | collective-permute-start | bytes 227336 | tf_op jit(solution)/shard_map/ppermute | solution.py:549
  41.2 1.2 %collective-permute-done.11.refs_2_ = bf16[296,128]{1,0:T(8,128)(2,1)S(1)} collective-permute-done((bf16[296,128]{1,0:T(8,128)(2,1)S(1)}, bf16[296,128]{1,0:T(8,128)(2,1)S(1)}, u32[]{:S(2)}, u32[]{:S(2)}) %collective-permute-start.11) | collective-permute-done | bytes 75808 | tf_op jit(solution)/shard_map/ppermute | solution.py:549
  42.3 1.5 %collective-permute-done.12.refs_3_ = bf16[296,128]{1,0:T(8,128)(2,1)S(1)} collective-permute-done((bf16[296,128]{1,0:T(8,128)(2,1)S(1)}, bf16[296,128]{1,0:T(8,128)(2,1)S(1)}, u32[]{:S(2)}, u32[]{:S(2)}) %collective-permute-start.12) | collective-permute-done | bytes 75808 | tf_op jit(solution)/shard_map/ppermute | solution.py:549
  43.9 1.1 %collective-permute-done.16 = bf16[6,8,1024]{2,1,0:T(8,128)(2,1)S(1)} collective-permute-done((bf16[6,8,1024]{2,1,0:T(8,128)(2,1)S(1)}, bf16[6,8,1024]{2,1,0:T(8,128)(2,1)S(1)}, u32[]{:S(2)}, u32[]{:S(2)}) %collective-permute-start.16) | collective-permute-done | bytes 98336 | tf_op jit(solution)/shard_map/ppermute | solution.py:432
  45.7 0.9 %shard_map.151 = (f32[1296,128]{1,0:T(8,128)}, f32[1,128]{1,0:T(1,128)}, f32[512,256]{1,0:T(8,128)}, f32[1,256]{1,0:T(1,128)}) custom-call(bf16[296,128]{1,0:T(8,128)(2,1)S(1)} %add_convert_fusion.1.refs_0_, bf16[296,128]{1,0:T(8,128)(2,1)S(1)} %collective-permute-done.10.refs_1_, bf16[296,128]{1,0:T(8,128)(2,1)S(1)} %collective-permute-done.11.refs_2_, ...), custom_call_target="tpu_custom_call" | custom-call | bytes 1048576 | tf_op jit(solution)/shard_map/pallas_call | solution.py:577
  46.6 0.9 %shard_map.152 = (f32[1296,128]{1,0:T(8,128)}, f32[1,128]{1,0:T(1,128)}, f32[512,256]{1,0:T(8,128)}, f32[1,256]{1,0:T(1,128)}) custom-call(bf16[4,296,128]{2,1,0:T(8,128)(2,1)S(1)} %collective-permute-done.13.refs_0_, f32[1296,128]{1,0:T(8,128)} %get-tuple-element.78.refs_1_, ...), custom_call_target="tpu_custom_call", output_to_operand_aliasing={{0}: (1, {}), {1}: (2, {}), {2}: (3, {}), {3}: (4, {})} | custom-call | bytes 1048576 | tf_op jit(solution)/shard_map/pallas_call | solution.py:580
  (30 shorter events, 7.0 us)
Async XLA Ops:
  0.6 6.0 %collective-permute-start = (bf16[48,1024]{1,0:T(8,128)(2,1)}, bf16[48,1024]{1,0:T(8,128)(2,1)S(1)}, u32[]{:S(2)}, u32[]{:S(2)}) collective-permute-start(bf16[48,1024]{1,0:T(8,128)(2,1)} %bitcast.40), channel_id=1, source_target_pairs={{0,16},{16,0},{1,17},{17,1},{2,18},{18,2},{3,19},{19,3},{4,20},{20... | collective-permute-start | bytes 294920 | tf_op jit(solution)/shard_map/ppermute | solution.py:432
  6.9 3.1 %collective-permute-start.2 = (bf16[48,1024]{1,0:T(8,128)(2,1)S(1)}, bf16[48,1024]{1,0:T(8,128)(2,1)S(1)}, u32[]{:S(2)}, u32[]{:S(2)}) collective-permute-start(bf16[48,1024]{1,0:T(8,128)(2,1)S(1)} %get-tuple-element.63), channel_id=1, source_target_pairs={{0,1},{1,0},{2,3},{3,2},{4,5},{5,4},{6,7},{7,6},{8,9},{9,8},{10,11... | collective-permute-start | bytes 294920 | tf_op jit(solution)/shard_map/ppermute | solution.py:435
  7.0 4.7 %collective-permute-start.1 = (bf16[48,1024]{1,0:T(8,128)(2,1)S(1)}, bf16[48,1024]{1,0:T(8,128)(2,1)S(1)}, u32[]{:S(2)}, u32[]{:S(2)}) collective-permute-start(bf16[48,1024]{1,0:T(8,128)(2,1)S(1)} %get-tuple-element.50), channel_id=1, source_target_pairs={{1,2},{3,4},{5,6},{7,8},{9,10},{11,12},{13,14},{2,1},{4,3},{6,5},{... | collective-permute-start | bytes 294920 | tf_op jit(solution)/shard_map/ppermute | solution.py:443
  13.1 5.9 %collective-permute-start.3 = (bf16[4,296,128]{2,1,0:T(8,128)(2,1)S(1)}, bf16[4,296,128]{2,1,0:T(8,128)(2,1)S(1)}, u32[]{:S(2)}, u32[]{:S(2)}) collective-permute-start(bf16[4,296,128]{2,1,0:T(8,128)(2,1)S(1)} %get-tuple-element.76), channel_id=1, source_target_pairs={{0,1},{1,0},{2,3},{3,2},{4,5},{5,4},{6,7},{7,6},{8,9},{9,8},{10,11... | collective-permute-start | bytes 909320 | tf_op jit(solution)/shard_map/ppermute | solution.py:435
  14.2 8.5 %collective-permute-start.14 = (bf16[48,1024]{1,0:T(8,128)(2,1)S(1)}, bf16[48,1024]{1,0:T(8,128)(2,1)S(1)}, u32[]{:S(2)}, u32[]{:S(2)}) collective-permute-start(bf16[48,1024]{1,0:T(8,128)(2,1)S(1)} %get-tuple-element.87), channel_id=1, source_target_pairs={{1,2},{3,4},{5,6},{7,8},{9,10},{11,12},{13,14},{2,1},{4,3},{6,5},{... | collective-permute-start | bytes 294920 | tf_op jit(solution)/shard_map/ppermute | solution.py:443
  16.1 6.6 %collective-permute-start.15 = (bf16[48,1024]{1,0:T(8,128)(2,1)S(1)}, bf16[48,1024]{1,0:T(8,128)(2,1)S(1)}, u32[]{:S(2)}, u32[]{:S(2)}) collective-permute-start(bf16[48,1024]{1,0:T(8,128)(2,1)S(1)} %get-tuple-element.88), channel_id=1, source_target_pairs={{0,1},{1,0},{2,3},{3,2},{4,5},{5,4},{6,7},{7,6},{8,9},{9,8},{10,11... | collective-permute-start | bytes 294920 | tf_op jit(solution)/shard_map/ppermute | solution.py:435
  19.1 4.4 %collective-permute-start.4 = (bf16[296,128]{1,0:T(8,128)(2,1)S(1)}, bf16[296,128]{1,0:T(8,128)(2,1)S(1)}, u32[]{:S(2)}, u32[]{:S(2)}) collective-permute-start(bf16[296,128]{1,0:T(8,128)(2,1)S(1)} %get-tuple-element.90), channel_id=1, source_target_pairs={{0,2},{1,5},{2,0},{3,7},{4,6},{5,1},{6,4},{7,3},{8,10},{9,13},{10,... | collective-permute-start | bytes 227336 | tf_op jit(solution)/shard_map/ppermute | solution.py:549
  20.8 4.4 %collective-permute-start.5 = (bf16[296,128]{1,0:T(8,128)(2,1)S(1)}, bf16[296,128]{1,0:T(8,128)(2,1)S(1)}, u32[]{:S(2)}, u32[]{:S(2)}) collective-permute-start(bf16[296,128]{1,0:T(8,128)(2,1)S(1)} %get-tuple-element.92), channel_id=1, source_target_pairs={{0,16},{1,9},{2,18},{3,11},{4,20},{5,13},{6,22},{7,15},{8,24},{9,1... | collective-permute-start | bytes 227336 | tf_op jit(solution)/shard_map/ppermute | solution.py:549
  22.4 5.3 %collective-permute-start.6 = (bf16[296,128]{1,0:T(8,128)(2,1)S(1)}, bf16[296,128]{1,0:T(8,128)(2,1)S(1)}, u32[]{:S(2)}, u32[]{:S(2)}) collective-permute-start(bf16[296,128]{1,0:T(8,128)(2,1)S(1)} %get-tuple-element.91), channel_id=1, source_target_pairs={{0,18},{1,13},{2,16},{3,15},{4,22},{5,9},{6,20},{7,11},{8,26},{9,5... | collective-permute-start | bytes 227336 | tf_op jit(solution)/shard_map/ppermute | solution.py:549
  27.7 4.6 %collective-permute-start.7 = (bf16[296,128]{1,0:T(8,128)(2,1)S(1)}, bf16[296,128]{1,0:T(8,128)(2,1)S(1)}, u32[]{:S(2)}, u32[]{:S(2)}) collective-permute-start(bf16[296,128]{1,0:T(8,128)(2,1)S(1)} %fusion.3), channel_id=1, source_target_pairs={{0,4},{1,3},{2,6},{3,1},{4,0},{5,7},{6,2},{7,5},{8,12},{9,11},{10,... | collective-permute-start | bytes 227336 | tf_op jit(solution)/shard_map/ppermute | solution.py:549
  29.3 6.1 %collective-permute-start.8 = (bf16[296,128]{1,0:T(8,128)(2,1)S(1)}, bf16[296,128]{1,0:T(8,128)(2,1)S(1)}, u32[]{:S(2)}, u32[]{:S(2)}) collective-permute-start(bf16[296,128]{1,0:T(8,128)(2,1)S(1)} %fusion.3), channel_id=1, source_target_pairs={{0,8},{1,17},{2,10},{3,19},{4,12},{5,21},{6,14},{7,23},{8,0},{9,25... | collective-permute-start | bytes 227336 | tf_op jit(solution)/shard_map/ppermute | solution.py:549
  30.4 6.3 %collective-permute-start.9 = (bf16[296,128]{1,0:T(8,128)(2,1)S(1)}, bf16[296,128]{1,0:T(8,128)(2,1)S(1)}, u32[]{:S(2)}, u32[]{:S(2)}) collective-permute-start(bf16[296,128]{1,0:T(8,128)(2,1)S(1)} %fusion.3), channel_id=1, source_target_pairs={{0,12},{1,19},{2,14},{3,17},{4,8},{5,23},{6,10},{7,21},{8,4},{9,27... | collective-permute-start | bytes 227336 | tf_op jit(solution)/shard_map/ppermute | solution.py:549
  36.7 4.4 %collective-permute-start.10 = (bf16[296,128]{1,0:T(8,128)(2,1)S(1)}, bf16[296,128]{1,0:T(8,128)(2,1)S(1)}, u32[]{:S(2)}, u32[]{:S(2)}) collective-permute-start(bf16[296,128]{1,0:T(8,128)(2,1)S(1)} %add_convert_fusion.1.refs_0_), channel_id=1, source_target_pairs={{0,2},{1,5},{2,0},{3,7},{4,6},{5,1},{6,4},{7,3},{8,10},{9,13},{10,... | collective-permute-start | bytes 227336 | tf_op jit(solution)/shard_map/ppermute | solution.py:549
  38.0 4.4 %collective-permute-start.11 = (bf16[296,128]{1,0:T(8,128)(2,1)S(1)}, bf16[296,128]{1,0:T(8,128)(2,1)S(1)}, u32[]{:S(2)}, u32[]{:S(2)}) collective-permute-start(bf16[296,128]{1,0:T(8,128)(2,1)S(1)} %add_convert_fusion.1.refs_0_), channel_id=1, source_target_pairs={{0,16},{1,9},{2,18},{3,11},{4,20},{5,13},{6,22},{7,15},{8,24},{9,1... | collective-permute-start | bytes 227336 | tf_op jit(solution)/shard_map/ppermute | solution.py:549
  38.5 5.3 %collective-permute-start.12 = (bf16[296,128]{1,0:T(8,128)(2,1)S(1)}, bf16[296,128]{1,0:T(8,128)(2,1)S(1)}, u32[]{:S(2)}, u32[]{:S(2)}) collective-permute-start(bf16[296,128]{1,0:T(8,128)(2,1)S(1)} %add_convert_fusion.1.refs_0_), channel_id=1, source_target_pairs={{0,18},{1,13},{2,16},{3,15},{4,22},{5,9},{6,20},{7,11},{8,26},{9,5... | collective-permute-start | bytes 227336 | tf_op jit(solution)/shard_map/ppermute | solution.py:549
  40.3 4.7 %collective-permute-start.16 = (bf16[6,8,1024]{2,1,0:T(8,128)(2,1)S(1)}, bf16[6,8,1024]{2,1,0:T(8,128)(2,1)S(1)}, u32[]{:S(2)}, u32[]{:S(2)}) collective-permute-start(bf16[6,8,1024]{2,1,0:T(8,128)(2,1)S(1)} %fusion), channel_id=1, source_target_pairs={{0,16},{16,0},{1,17},{17,1},{2,18},{18,2},{3,19},{19,3},{4,20},{20... | collective-permute-start | bytes 294920 | tf_op jit(solution)/shard_map/ppermute | solution.py:432
  43.8 2.8 %collective-permute-start.13 = (bf16[4,296,128]{2,1,0:T(8,128)(2,1)S(1)}, bf16[4,296,128]{2,1,0:T(8,128)(2,1)S(1)}, u32[]{:S(2)}, u32[]{:S(2)}) collective-permute-start(bf16[4,296,128]{2,1,0:T(8,128)(2,1)S(1)} %pad_maximum_fusion), channel_id=1, source_target_pairs={{0,1},{1,0},{2,3},{3,2},{4,5},{5,4},{6,7},{7,6},{8,9},{9,8},{10,11... | collective-permute-start | bytes 909320 | tf_op jit(solution)/shard_map/ppermute | solution.py:435

commit v6 on v5

--- a/solution.py
+++ b/solution.py
@@ -264,7 +264,7 @@
 def main_kernel(dims, heights, halo, *refs):
     frames, rows, pair = dims
     _, _, _, _, _, _, _, cotangent = refs[:8]
-    acts_in, slopes_in, conv_in, down_in, total_in, mine, keep, give, acts, slopes, x, packed = refs[8:]
+    acts_in, slopes_in, conv_in, down_in, total_in, mine, keep, give_mine, give, acts, slopes, x, packed = refs[8:]
     core = lax.axis_index("core")
     halo = (halo[...].astype(F32) * jnp.where(at_end(heights), 0.0, 1.0)).astype(BF16)
     acts[1 - core] = acts_in[...]
@@ -300,7 +300,10 @@
         else:
             mine[...] = packed[core, pl.ds(at, chunk)]
         at = pl.multiple_of(jnp.bitwise_xor(order_of(1 - core), m) * chunk, 8)
-        give[m] = packed[1 - core, pl.ds(at, chunk)].astype(BF16)
+        if m:
+            give[m - 1] = packed[1 - core, pl.ds(at, chunk)].astype(BF16)
+        else:
+            give_mine[...] = packed[1 - core, pl.ds(at, chunk)].astype(BF16)
 
 
 def shifted_slope(slopes, f, r, pair):
@@ -510,12 +513,13 @@
         [rows_scratch],
         flops=10**9,
     )(inner, *common)
-    mine, keep, give, acts, slopes = call(
+    mine, keep, give_mine, give, acts, slopes = call(
         functools.partial(main_kernel, dims, heights),
         [
             ((chunk, WIDTH), F32),
             ((3, chunk, WIDTH), F32),
-            ((4, chunk, WIDTH), BF16),
+            ((chunk, WIDTH), BF16),
+            ((3, chunk, WIDTH), BF16),
             ((rows, *acts_shape), BF16),
             ((rows, *slopes_shape), BF16),
         ],
@@ -549,10 +553,11 @@
         return lax.ppermute(value, names, pairs)
 
     given = swap_inner(give)
-    rest = (keep + given[1:].astype(F32)).astype(BF16)
+    given_mine = swap_inner(give_mine)
+    rest = (keep + given.astype(F32)).astype(BF16)
     steps = (1, 2, 3)
     parts = [cross(rest[m - 1], m, True) for m in steps]
-    mine = mine + given[0].astype(F32) + sum(part.astype(F32) for part in parts)
+    mine = mine + given_mine.astype(F32) + sum(part.astype(F32) for part in parts)
     mine = mine.astype(BF16)
     parts = [cross(mine, m, False) for m in steps]
     mine = (mine.astype(F32) + sum(part.astype(F32) for part in parts)).astype(BF16)

time: 47.7 us -> 47.2 us (0.990)
    ppermute x9, waiting for transfers between devices: 12 us -> 11.3 us  [cross(): return lax.ppermute(value, names, pairs)]
    ppermute x4 -> x5, starting transfers between devices: 1.12 us -> 1.11 us  [swap_inner(): return lax.ppermute(value, 'core', [(0, 1), (1, 0)])]
  transfers between devices with their start and end apart: 17 -> 18, of which waited for: 11 -> 12; matrix products, arithmetic and copies ran while one was open for 2% -> 2% of each run, Pallas kernels for 18% -> 18%
where the time goes in v6:
time: 47.2 us; the launch traced here: 47.1 us
  starting transfers between devices  20.1 us (43%)
  waiting for transfers between devices  13.9 us (29%)
  Pallas kernels  11.2 us (24%)
  other arithmetic  1.05 us (2%)
  between operations  0.77 us (2%)
    ppermute x9, starting transfers between devices, cross(): return lax.ppermute(value, names, pairs)  11.6 us
    ppermute x9, waiting for transfers between devices, cross(): return lax.ppermute(value, names, pairs)  11.3 us
    ppermute x2, starting transfers between devices, swap_outer(): return lax.ppermute(value, times + heights, pairs)  3.78 us
    ppermute x2, starting transfers between devices, along_tm(): return lax.ppermute(value, times, pairs)  3.63 us
    ppermute x2, waiting for transfers between devices, along_tm(): return lax.ppermute(value, times, pairs)  2.25 us
    pallas_call x1, Pallas kernels, local(): call(functools.partial(late_kernel, dims), [((frames, rows // 2, pair, wi...  2.16 us
    pallas_call x1, Pallas kernels, local(): call(functools.partial(first_kernel, dims, len(sources)), [(source.shape,...  2.12 us
    pallas_call x1, Pallas kernels, local(): call(functools.partial(main_kernel, dims, heights), [((chunk, WIDTH), F32...  1.49 us
  transfers between devices with their start and end apart: 18, of which 12 were waited for; matrix products, arithmetic and copies ran while one was open for 2% of the time, Pallas kernels for 18%

profile of v6, /device:TPU:0, one launch (start us, length us, event | category | flops | bytes accessed | tf_op | source)
XLA Modules:
  0.0 47.1 jit_solution(6151594881853779544)
XLA Ops:
  0.6 3.0 %collective-permute-start = (bf16[48,1024]{1,0:T(8,128)(2,1)}, bf16[48,1024]{1,0:T(8,128)(2,1)S(1)}, u32[]{:S(2)}, u32[]{:S(2)}) collective-permute-start(bf16[48,1024]{1,0:T(8,128)(2,1)} %bitcast.35), channel_id=1, source_target_pairs={{0,16},{16,0},{1,17},{17,1},{2,18},{18,2},{3,19},{19,3},{4,20},{20... | collective-permute-start | bytes 294920 | tf_op jit(solution)/shard_map/ppermute | solution.py:435
  3.7 2.1 %shard_map.145 = (bf16[48,1024]{1,0:T(8,128)(2,1)S(1)}, bf16[512,512]{1,0:T(8,128)(2,1)S(1)}, bf16[192,192]{1,0:T(8,128)(2,1)S(1)}, bf16[512,256]{1,0:T(8,128)(2...) custom-call(bf16[27,48,128]{2,1,0:T(8,128)(2,1)} %bitcast.33, ...), custom_call_target="tpu_custom_call" | custom-call | flops 1000000000 | bytes 1048576 | tf_op jit(solution)/shard_map/pallas_call | solution.py:468
  5.8 0.9 %collective-permute-done.came = bf16[48,1024]{1,0:T(8,128)(2,1)S(1)} collective-permute-done((bf16[48,1024]{1,0:T(8,128)(2,1)}, bf16[48,1024]{1,0:T(8,128)(2,1)S(1)}, u32[]{:S(2)}, u32[]{:S(2)}) %collective-permute-start) | collective-permute-done | bytes 98336 | tf_op jit(solution)/shard_map/ppermute | solution.py:435
  7.0 1.9 %collective-permute-start.1 = (bf16[48,1024]{1,0:T(8,128)(2,1)S(1)}, bf16[48,1024]{1,0:T(8,128)(2,1)S(1)}, u32[]{:S(2)}, u32[]{:S(2)}) collective-permute-start(bf16[48,1024]{1,0:T(8,128)(2,1)S(1)} %get-tuple-element.51), channel_id=1, source_target_pairs={{1,2},{3,4},{5,6},{7,8},{9,10},{11,12},{13,14},{2,1},{4,3},{6,5},{... | collective-permute-start | bytes 294920 | tf_op jit(solution)/shard_map/ppermute | solution.py:446
  8.8 1.1 %shard_map.147 = (bf16[2,2,144,256]{3,2,1,0:T(8,128)(2,1)S(1)}, f32[2,2,128,256]{3,2,1,0:T(8,128)S(1)}) custom-call(bf16[48,1024]{1,0:T(8,128)(2,1)S(1)} %get-tuple-element.54.earlier, bf16[512,512]{1,0:T(8,128)(2,1)S(1)} %get-tuple-element.52.table.refs_0_, bf16[192,192]{1,0:T(8,128)(2,1)S(1)} %get-tuple-element.55.rows_own, ...), custom_call_target="tpu_custom_call" | custom-call | flops 1000000000 | bytes 1048576 | tf_op jit(solution)/shard_map/pallas_call | solution.py:490
  10.0 1.4 %shard_map.148 = (bf16[2,256,128]{2,1,0:T(8,128)(2,1)S(1)}, bf16[256,256]{1,0:T(8,128)(2,1)S(1)}, f32[1296,128]{1,0:T(8,128)S(1)}, f32[256,256]{1,0:T(8,128)S(1)}, f32[8,128]{1,0:T(8,128)S(1)}) custom-call(bf16[48,1024]{1,0:T(8,128)(2,1)S(1)} %collective-permute-done.2.halo, bf16[512,512]{1,0:T(8,128)(2,1)S(1)} %get-tuple-element.52.table.refs_0_, ...), custom_call_target="tpu_custom_call" | custom-call | flops 1000000000 | bytes 1048576 | tf_op jit(solution)/shard_map/pallas_call | solution.py:503
  11.6 1.5 %shard_map.149 = (f32[296,128]{1,0:T(8,128)S(1)}, f32[3,296,128]{2,1,0:T(8,128)S(1)}, bf16[296,128]{1,0:T(8,128)(2,1)S(1)}, bf16[3,296,128]{2,1,0:T(8,128)(2,1)S...) custom-call(bf16[48,1024]{1,0:T(8,128)(2,1)S(1)} %collective-permute-done.1.halo, ...), custom_call_target="tpu_custom_call" | custom-call | flops 1000000000 | bytes 1048576 | tf_op jit(solution)/shard_map/pallas_call | solution.py:516
  13.3 0.9 %shard_map.153 = (bf16[48,1024]{1,0:T(8,128)(2,1)S(1)}, bf16[48,1024]{1,0:T(8,128)(2,1)S(1)}) custom-call(bf16[2,256,256]{2,1,0:T(8,128)(2,1)S(1)} %get-tuple-element.71.slopes, bf16[432,384]{1,0:T(8,128)(2,1)S(1)} %get-tuple-element.72.backward, bf16[512,512]{1,0:T(8,128)(2,1)S(1)} %get-tuple-element.52.table.refs_0_, ...), custom_call_target="tpu_custom_call" | custom-call | flops 1000000000 | bytes 1048576 | tf_op jit(solution)/shard_map/pallas_call | solution.py:531
  14.2 1.9 %collective-permute-start.15 = (bf16[48,1024]{1,0:T(8,128)(2,1)S(1)}, bf16[48,1024]{1,0:T(8,128)(2,1)S(1)}, u32[]{:S(2)}, u32[]{:S(2)}) collective-permute-start(bf16[48,1024]{1,0:T(8,128)(2,1)S(1)} %get-tuple-element.89), channel_id=1, source_target_pairs={{1,2},{3,4},{5,6},{7,8},{9,10},{11,12},{13,14},{2,1},{4,3},{6,5},{... | collective-permute-start | bytes 294920 | tf_op jit(solution)/shard_map/ppermute | solution.py:446
  16.9 2.2 %shard_map.150 = (bf16[2,1,128,256]{3,2,1,0:T(8,128)(2,1)}, f32[48,1024]{1,0:T(8,128)S(1)}, f32[48,1024]{1,0:T(8,128)S(1)}) custom-call(bf16[2,2,256,128]{3,2,1,0:T(8,128)(2,1)S(1)} %get-tuple-element.70.acts, bf16[2,256,256]{2,1,0:T(8,128)(2,1)S(1)} %get-tuple-element.71.slopes, bf16[432,384]{1,0:T(8,128)(2,1)S(1)} %get-tuple-element.72.backward, ...), custom_call_target="tpu_custom_call" | custom-call | flops 1000000000 | bytes 1048576 | tf_op jit(solution)/shard_map/pallas_call | solution.py:534
  19.1 1.7 %collective-permute-start.5 = (bf16[296,128]{1,0:T(8,128)(2,1)S(1)}, bf16[296,128]{1,0:T(8,128)(2,1)S(1)}, u32[]{:S(2)}, u32[]{:S(2)}) collective-permute-start(bf16[296,128]{1,0:T(8,128)(2,1)S(1)} %get-tuple-element.92), channel_id=1, source_target_pairs={{0,2},{1,5},{2,0},{3,7},{4,6},{5,1},{6,4},{7,3},{8,10},{9,13},{10,... | collective-permute-start | bytes 227336 | tf_op jit(solution)/shard_map/ppermute | solution.py:553
  20.9 1.5 %collective-permute-start.6 = (bf16[296,128]{1,0:T(8,128)(2,1)S(1)}, bf16[296,128]{1,0:T(8,128)(2,1)S(1)}, u32[]{:S(2)}, u32[]{:S(2)}) collective-permute-start(bf16[296,128]{1,0:T(8,128)(2,1)S(1)} %get-tuple-element.94), channel_id=1, source_target_pairs={{0,16},{1,9},{2,18},{3,11},{4,20},{5,13},{6,22},{7,15},{8,24},{9,1... | collective-permute-start | bytes 227336 | tf_op jit(solution)/shard_map/ppermute | solution.py:553
  23.6 1.7 %collective-permute-done.6 = bf16[296,128]{1,0:T(8,128)(2,1)S(1)} collective-permute-done((bf16[296,128]{1,0:T(8,128)(2,1)S(1)}, bf16[296,128]{1,0:T(8,128)(2,1)S(1)}, u32[]{:S(2)}, u32[]{:S(2)}) %collective-permute-start.6) | collective-permute-done | bytes 75808 | tf_op jit(solution)/shard_map/ppermute | solution.py:553
  25.2 2.4 %collective-permute-done.7 = bf16[296,128]{1,0:T(8,128)(2,1)S(1)} collective-permute-done((bf16[296,128]{1,0:T(8,128)(2,1)S(1)}, bf16[296,128]{1,0:T(8,128)(2,1)S(1)}, u32[]{:S(2)}, u32[]{:S(2)}) %collective-permute-start.7) | collective-permute-done | bytes 75808 | tf_op jit(solution)/shard_map/ppermute | solution.py:553
  27.7 2.7 %collective-permute-start.10 = (bf16[296,128]{1,0:T(8,128)(2,1)S(1)}, bf16[296,128]{1,0:T(8,128)(2,1)S(1)}, u32[]{:S(2)}, u32[]{:S(2)}) collective-permute-start(bf16[296,128]{1,0:T(8,128)(2,1)S(1)} %add_convert_fusion.2), channel_id=1, source_target_pairs={{0,12},{1,19},{2,14},{3,17},{4,8},{5,23},{6,10},{7,21},{8,4},{9,27... | collective-permute-start | bytes 227336 | tf_op jit(solution)/shard_map/ppermute | solution.py:553
  30.9 1.2 %collective-permute-start.9 = (bf16[296,128]{1,0:T(8,128)(2,1)S(1)}, bf16[296,128]{1,0:T(8,128)(2,1)S(1)}, u32[]{:S(2)}, u32[]{:S(2)}) collective-permute-start(bf16[296,128]{1,0:T(8,128)(2,1)S(1)} %add_convert_fusion.2), channel_id=1, source_target_pairs={{0,8},{1,17},{2,10},{3,19},{4,12},{5,21},{6,14},{7,23},{8,0},{9,25... | collective-permute-start | bytes 227336 | tf_op jit(solution)/shard_map/ppermute | solution.py:553
  32.3 1.7 %collective-permute-done.10 = bf16[296,128]{1,0:T(8,128)(2,1)S(1)} collective-permute-done((bf16[296,128]{1,0:T(8,128)(2,1)S(1)}, bf16[296,128]{1,0:T(8,128)(2,1)S(1)}, u32[]{:S(2)}, u32[]{:S(2)}) %collective-permute-start.10) | collective-permute-done | bytes 75808 | tf_op jit(solution)/shard_map/ppermute | solution.py:553
  34.8 1.4 %collective-permute-done.9 = bf16[296,128]{1,0:T(8,128)(2,1)S(1)} collective-permute-done((bf16[296,128]{1,0:T(8,128)(2,1)S(1)}, bf16[296,128]{1,0:T(8,128)(2,1)S(1)}, u32[]{:S(2)}, u32[]{:S(2)}) %collective-permute-start.9) | collective-permute-done | bytes 75808 | tf_op jit(solution)/shard_map/ppermute | solution.py:553
  37.7 2.1 %collective-permute-start.13 = (bf16[296,128]{1,0:T(8,128)(2,1)S(1)}, bf16[296,128]{1,0:T(8,128)(2,1)S(1)}, u32[]{:S(2)}, u32[]{:S(2)}) collective-permute-start(bf16[296,128]{1,0:T(8,128)(2,1)S(1)} %add_convert_fusion.1.refs_0_), channel_id=1, source_target_pairs={{0,18},{1,13},{2,16},{3,15},{4,22},{5,9},{6,20},{7,11},{8,26},{9,5... | collective-permute-start | bytes 227336 | tf_op jit(solution)/shard_map/ppermute | solution.py:553
  40.7 1.3 %collective-permute-done.12.refs_2_ = bf16[296,128]{1,0:T(8,128)(2,1)S(1)} collective-permute-done((bf16[296,128]{1,0:T(8,128)(2,1)S(1)}, bf16[296,128]{1,0:T(8,128)(2,1)S(1)}, u32[]{:S(2)}, u32[]{:S(2)}) %collective-permute-start.12) | collective-permute-done | bytes 75808 | tf_op jit(solution)/shard_map/ppermute | solution.py:553
  42.0 1.0 %collective-permute-done.13.refs_3_ = bf16[296,128]{1,0:T(8,128)(2,1)S(1)} collective-permute-done((bf16[296,128]{1,0:T(8,128)(2,1)S(1)}, bf16[296,128]{1,0:T(8,128)(2,1)S(1)}, u32[]{:S(2)}, u32[]{:S(2)}) %collective-permute-start.13) | collective-permute-done | bytes 75808 | tf_op jit(solution)/shard_map/ppermute | solution.py:553
  43.1 1.4 %collective-permute-done.17 = bf16[6,8,1024]{2,1,0:T(8,128)(2,1)S(1)} collective-permute-done((bf16[6,8,1024]{2,1,0:T(8,128)(2,1)S(1)}, bf16[6,8,1024]{2,1,0:T(8,128)(2,1)S(1)}, u32[]{:S(2)}, u32[]{:S(2)}) %collective-permute-start.17) | collective-permute-done | bytes 98336 | tf_op jit(solution)/shard_map/ppermute | solution.py:435
  45.2 0.9 %shard_map.151 = (f32[1296,128]{1,0:T(8,128)}, f32[1,128]{1,0:T(1,128)}, f32[512,256]{1,0:T(8,128)}, f32[1,256]{1,0:T(1,128)}) custom-call(bf16[296,128]{1,0:T(8,128)(2,1)S(1)} %add_convert_fusion.1.refs_0_, bf16[296,128]{1,0:T(8,128)(2,1)S(1)} %collective-permute-done.11.refs_1_, bf16[296,128]{1,0:T(8,128)(2,1)S(1)} %collective-permute-done.12.refs_2_, ...), custom_call_target="tpu_custom_call" | custom-call | bytes 1048576 | tf_op jit(solution)/shard_map/pallas_call | solution.py:582
  46.1 0.9 %shard_map.152 = (f32[1296,128]{1,0:T(8,128)}, f32[1,128]{1,0:T(1,128)}, f32[512,256]{1,0:T(8,128)}, f32[1,256]{1,0:T(1,128)}) custom-call(bf16[4,296,128]{2,1,0:T(8,128)(2,1)S(1)} %collective-permute-done.14.refs_0_, f32[1296,128]{1,0:T(8,128)} %get-tuple-element.80.refs_1_, ...), custom_call_target="tpu_custom_call", output_to_operand_aliasing={{0}: (1, {}), {1}: (2, {}), {2}: (3, {}), {3}: (4, {})} | custom-call | bytes 1048576 | tf_op jit(solution)/shard_map/pallas_call | solution.py:585
  (32 shorter events, 7.5 us)
Async XLA Ops:
  0.6 6.0 %collective-permute-start = (bf16[48,1024]{1,0:T(8,128)(2,1)}, bf16[48,1024]{1,0:T(8,128)(2,1)S(1)}, u32[]{:S(2)}, u32[]{:S(2)}) collective-permute-start(bf16[48,1024]{1,0:T(8,128)(2,1)} %bitcast.35), channel_id=1, source_target_pairs={{0,16},{16,0},{1,17},{17,1},{2,18},{18,2},{3,19},{19,3},{4,20},{20... | collective-permute-start | bytes 294920 | tf_op jit(solution)/shard_map/ppermute | solution.py:435
  6.9 3.1 %collective-permute-start.2 = (bf16[48,1024]{1,0:T(8,128)(2,1)S(1)}, bf16[48,1024]{1,0:T(8,128)(2,1)S(1)}, u32[]{:S(2)}, u32[]{:S(2)}) collective-permute-start(bf16[48,1024]{1,0:T(8,128)(2,1)S(1)} %get-tuple-element.64), channel_id=1, source_target_pairs={{0,1},{1,0},{2,3},{3,2},{4,5},{5,4},{6,7},{7,6},{8,9},{9,8},{10,11... | collective-permute-start | bytes 294920 | tf_op jit(solution)/shard_map/ppermute | solution.py:438
  7.0 4.7 %collective-permute-start.1 = (bf16[48,1024]{1,0:T(8,128)(2,1)S(1)}, bf16[48,1024]{1,0:T(8,128)(2,1)S(1)}, u32[]{:S(2)}, u32[]{:S(2)}) collective-permute-start(bf16[48,1024]{1,0:T(8,128)(2,1)S(1)} %get-tuple-element.51), channel_id=1, source_target_pairs={{1,2},{3,4},{5,6},{7,8},{9,10},{11,12},{13,14},{2,1},{4,3},{6,5},{... | collective-permute-start | bytes 294920 | tf_op jit(solution)/shard_map/ppermute | solution.py:446
  13.1 5.9 %collective-permute-start.4 = (bf16[3,296,128]{2,1,0:T(8,128)(2,1)S(1)}, bf16[3,296,128]{2,1,0:T(8,128)(2,1)S(1)}, u32[]{:S(2)}, u32[]{:S(2)}) collective-permute-start(bf16[3,296,128]{2,1,0:T(8,128)(2,1)S(1)} %get-tuple-element.79), channel_id=1, source_target_pairs={{0,1},{1,0},{2,3},{3,2},{4,5},{5,4},{6,7},{7,6},{8,9},{9,8},{10,11... | collective-permute-start | bytes 681992 | tf_op jit(solution)/shard_map/ppermute | solution.py:438
  14.2 8.2 %collective-permute-start.15 = (bf16[48,1024]{1,0:T(8,128)(2,1)S(1)}, bf16[48,1024]{1,0:T(8,128)(2,1)S(1)}, u32[]{:S(2)}, u32[]{:S(2)}) collective-permute-start(bf16[48,1024]{1,0:T(8,128)(2,1)S(1)} %get-tuple-element.89), channel_id=1, source_target_pairs={{1,2},{3,4},{5,6},{7,8},{9,10},{11,12},{13,14},{2,1},{4,3},{6,5},{... | collective-permute-start | bytes 294920 | tf_op jit(solution)/shard_map/ppermute | solution.py:446
  16.1 6.6 %collective-permute-start.16 = (bf16[48,1024]{1,0:T(8,128)(2,1)S(1)}, bf16[48,1024]{1,0:T(8,128)(2,1)S(1)}, u32[]{:S(2)}, u32[]{:S(2)}) collective-permute-start(bf16[48,1024]{1,0:T(8,128)(2,1)S(1)} %get-tuple-element.90), channel_id=1, source_target_pairs={{0,1},{1,0},{2,3},{3,2},{4,5},{5,4},{6,7},{7,6},{8,9},{9,8},{10,11... | collective-permute-start | bytes 294920 | tf_op jit(solution)/shard_map/ppermute | solution.py:438
  16.9 5.9 %collective-permute-start.3 = (bf16[296,128]{1,0:T(8,128)(2,1)S(1)}, bf16[296,128]{1,0:T(8,128)(2,1)S(1)}, u32[]{:S(2)}, u32[]{:S(2)}) collective-permute-start(bf16[296,128]{1,0:T(8,128)(2,1)S(1)} %get-tuple-element.77), channel_id=1, source_target_pairs={{0,1},{1,0},{2,3},{3,2},{4,5},{5,4},{6,7},{7,6},{8,9},{9,8},{10,11... | collective-permute-start | bytes 227336 | tf_op jit(solution)/shard_map/ppermute | solution.py:438
  19.1 4.4 %collective-permute-start.5 = (bf16[296,128]{1,0:T(8,128)(2,1)S(1)}, bf16[296,128]{1,0:T(8,128)(2,1)S(1)}, u32[]{:S(2)}, u32[]{:S(2)}) collective-permute-start(bf16[296,128]{1,0:T(8,128)(2,1)S(1)} %get-tuple-element.92), channel_id=1, source_target_pairs={{0,2},{1,5},{2,0},{3,7},{4,6},{5,1},{6,4},{7,3},{8,10},{9,13},{10,... | collective-permute-start | bytes 227336 | tf_op jit(solution)/shard_map/ppermute | solution.py:553
  20.9 4.4 %collective-permute-start.6 = (bf16[296,128]{1,0:T(8,128)(2,1)S(1)}, bf16[296,128]{1,0:T(8,128)(2,1)S(1)}, u32[]{:S(2)}, u32[]{:S(2)}) collective-permute-start(bf16[296,128]{1,0:T(8,128)(2,1)S(1)} %get-tuple-element.94), channel_id=1, source_target_pairs={{0,16},{1,9},{2,18},{3,11},{4,20},{5,13},{6,22},{7,15},{8,24},{9,1... | collective-permute-start | bytes 227336 | tf_op jit(solution)/shard_map/ppermute | solution.py:553
  22.4 5.3 %collective-permute-start.7 = (bf16[296,128]{1,0:T(8,128)(2,1)S(1)}, bf16[296,128]{1,0:T(8,128)(2,1)S(1)}, u32[]{:S(2)}, u32[]{:S(2)}) collective-permute-start(bf16[296,128]{1,0:T(8,128)(2,1)S(1)} %get-tuple-element.93), channel_id=1, source_target_pairs={{0,18},{1,13},{2,16},{3,15},{4,22},{5,9},{6,20},{7,11},{8,26},{9,5... | collective-permute-start | bytes 227336 | tf_op jit(solution)/shard_map/ppermute | solution.py:553
  27.7 6.3 %collective-permute-start.10 = (bf16[296,128]{1,0:T(8,128)(2,1)S(1)}, bf16[296,128]{1,0:T(8,128)(2,1)S(1)}, u32[]{:S(2)}, u32[]{:S(2)}) collective-permute-start(bf16[296,128]{1,0:T(8,128)(2,1)S(1)} %add_convert_fusion.2), channel_id=1, source_target_pairs={{0,12},{1,19},{2,14},{3,17},{4,8},{5,23},{6,10},{7,21},{8,4},{9,27... | collective-permute-start | bytes 227336 | tf_op jit(solution)/shard_map/ppermute | solution.py:553
  30.4 4.4 %collective-permute-start.8 = (bf16[296,128]{1,0:T(8,128)(2,1)S(1)}, bf16[296,128]{1,0:T(8,128)(2,1)S(1)}, u32[]{:S(2)}, u32[]{:S(2)}) collective-permute-start(bf16[296,128]{1,0:T(8,128)(2,1)S(1)} %add_convert_fusion.2), channel_id=1, source_target_pairs={{0,4},{1,3},{2,6},{3,1},{4,0},{5,7},{6,2},{7,5},{8,12},{9,11},{10,... | collective-permute-start | bytes 227336 | tf_op jit(solution)/shard_map/ppermute | solution.py:553
  30.9 5.3 %collective-permute-start.9 = (bf16[296,128]{1,0:T(8,128)(2,1)S(1)}, bf16[296,128]{1,0:T(8,128)(2,1)S(1)}, u32[]{:S(2)}, u32[]{:S(2)}) collective-permute-start(bf16[296,128]{1,0:T(8,128)(2,1)S(1)} %add_convert_fusion.2), channel_id=1, source_target_pairs={{0,8},{1,17},{2,10},{3,19},{4,12},{5,21},{6,14},{7,23},{8,0},{9,25... | collective-permute-start | bytes 227336 | tf_op jit(solution)/shard_map/ppermute | solution.py:553
  36.2 4.4 %collective-permute-start.11 = (bf16[296,128]{1,0:T(8,128)(2,1)S(1)}, bf16[296,128]{1,0:T(8,128)(2,1)S(1)}, u32[]{:S(2)}, u32[]{:S(2)}) collective-permute-start(bf16[296,128]{1,0:T(8,128)(2,1)S(1)} %add_convert_fusion.1.refs_0_), channel_id=1, source_target_pairs={{0,2},{1,5},{2,0},{3,7},{4,6},{5,1},{6,4},{7,3},{8,10},{9,13},{10,... | collective-permute-start | bytes 227336 | tf_op jit(solution)/shard_map/ppermute | solution.py:553
  37.0 5.0 %collective-permute-start.12 = (bf16[296,128]{1,0:T(8,128)(2,1)S(1)}, bf16[296,128]{1,0:T(8,128)(2,1)S(1)}, u32[]{:S(2)}, u32[]{:S(2)}) collective-permute-start(bf16[296,128]{1,0:T(8,128)(2,1)S(1)} %add_convert_fusion.1.refs_0_), channel_id=1, source_target_pairs={{0,16},{1,9},{2,18},{3,11},{4,20},{5,13},{6,22},{7,15},{8,24},{9,1... | collective-permute-start | bytes 227336 | tf_op jit(solution)/shard_map/ppermute | solution.py:553
  37.7 5.3 %collective-permute-start.13 = (bf16[296,128]{1,0:T(8,128)(2,1)S(1)}, bf16[296,128]{1,0:T(8,128)(2,1)S(1)}, u32[]{:S(2)}, u32[]{:S(2)}) collective-permute-start(bf16[296,128]{1,0:T(8,128)(2,1)S(1)} %add_convert_fusion.1.refs_0_), channel_id=1, source_target_pairs={{0,18},{1,13},{2,16},{3,15},{4,22},{5,9},{6,20},{7,11},{8,26},{9,5... | collective-permute-start | bytes 227336 | tf_op jit(solution)/shard_map/ppermute | solution.py:553
  39.8 4.7 %collective-permute-start.17 = (bf16[6,8,1024]{2,1,0:T(8,128)(2,1)S(1)}, bf16[6,8,1024]{2,1,0:T(8,128)(2,1)S(1)}, u32[]{:S(2)}, u32[]{:S(2)}) collective-permute-start(bf16[6,8,1024]{2,1,0:T(8,128)(2,1)S(1)} %fusion), channel_id=1, source_target_pairs={{0,16},{16,0},{1,17},{17,1},{2,18},{18,2},{3,19},{19,3},{4,20},{20... | collective-permute-start | bytes 294920 | tf_op jit(solution)/shard_map/ppermute | solution.py:435
  43.0 3.1 %collective-permute-start.14 = (bf16[4,296,128]{2,1,0:T(8,128)(2,1)S(1)}, bf16[4,296,128]{2,1,0:T(8,128)(2,1)S(1)}, u32[]{:S(2)}, u32[]{:S(2)}) collective-permute-start(bf16[4,296,128]{2,1,0:T(8,128)(2,1)S(1)} %pad_maximum_fusion), channel_id=1, source_target_pairs={{0,1},{1,0},{2,3},{3,2},{4,5},{5,4},{6,7},{7,6},{8,9},{9,8},{10,11... | collective-permute-start | bytes 909320 | tf_op jit(solution)/shard_map/ppermute | solution.py:438

commit v7 on v5

--- a/solution.py
+++ b/solution.py
@@ -375,7 +375,7 @@
 def finish_kernel(scale, other, *refs):
     pieces, (conv, conv_bias, down, down_bias, flat, sums, sems) = refs[:4], refs[-7:]
     if other:
-        pieces = [refs[0].at[m] for m in range(4)]
+        pieces = [refs[0], *(refs[1].at[m] for m in range(3))]
     core = lax.axis_index("core")
     which = 1 - core if other else core
     chunk = pieces[0].shape[0]
@@ -560,7 +560,8 @@
         parts = [exchange(mine, axis, m) for m in range(1, lax.axis_size(axis))]
         mine = (mine.astype(F32) + sum(part.astype(F32) for part in parts)).astype(BF16)
     pieces = [mine] + [cross(mine, m, True) for m in steps]
-    theirs = swap_inner(jnp.stack(pieces))
+    theirs_mine = swap_inner(mine)
+    theirs = swap_inner(jnp.stack(pieces[1:]))
     count = frames * count_tm * rows * count_height * columns
     scale = 1.0 / math.sqrt(count)
     outs = [
@@ -580,11 +581,11 @@
     grad_conv, grad_conv_bias, grad_down, grad_down_bias = call(
         functools.partial(finish_kernel, scale, True),
         outs,
-        [VMEM] + [HBM] * 4,
+        [VMEM] * 2 + [HBM] * 4,
         scratch,
         out_specs=[HBM] * 4,
-        input_output_aliases={1: 0, 2: 1, 3: 2, 4: 3},
-    )(theirs, *grads)
+        input_output_aliases={2: 0, 3: 1, 4: 2, 5: 3},
+    )(theirs_mine, theirs, *grads)
 
     from_inner = swap_inner(send_inner).reshape((frames + 2) * colors, 4, pixel_columns)
     from_outer = swap_outer(send_outer).reshape((frames + 2) * colors, 4, pixel_columns)

time: 47.7 us -> 47.7 us (level)
    ppermute x4 -> x5, starting transfers between devices: 1.12 us -> 1.12 us  [swap_inner(): return lax.ppermute(value, 'core', [(0, 1), (1, 0)])]
  transfers between devices with their start and end apart: 17 -> 18, of which waited for: 11 -> 11; matrix products, arithmetic and copies ran while one was open for 2% -> 2% of each run, Pallas kernels for 18% -> 18%
where the time goes in v7:
time: 47.7 us; the launch traced here: 47.6 us
  starting transfers between devices  20.2 us (42%)
  waiting for transfers between devices  14.3 us (30%)
  Pallas kernels  11.2 us (23%)
  other arithmetic  1.02 us (2%)
  between operations  0.78 us (2%)
    ppermute x9, waiting for transfers between devices, cross(): return lax.ppermute(value, names, pairs)  12 us
    ppermute x9, starting transfers between devices, cross(): return lax.ppermute(value, names, pairs)  11.6 us
    ppermute x2, starting transfers between devices, swap_outer(): return lax.ppermute(value, times + heights, pairs)  3.76 us
    ppermute x2, starting transfers between devices, along_tm(): return lax.ppermute(value, times, pairs)  3.74 us
    pallas_call x1, Pallas kernels, local(): call(functools.partial(late_kernel, dims), [((frames, rows // 2, pair, wi...  2.16 us
    pallas_call x1, Pallas kernels, local(): call(functools.partial(first_kernel, dims, len(sources)), [(source.shape,...  2.12 us
    ppermute x2, waiting for transfers between devices, along_tm(): return lax.ppermute(value, times, pairs)  1.98 us
    pallas_call x1, Pallas kernels, local(): call(functools.partial(main_kernel, dims, heights), [((chunk, WIDTH), F32...  1.49 us
  transfers between devices with their start and end apart: 18, of which 11 were waited for; matrix products, arithmetic and copies ran while one was open for 2% of the time, Pallas kernels for 18%

profile of v7, /device:TPU:0, one launch (start us, length us, event | category | flops | bytes accessed | tf_op | source)
XLA Modules:
  0.0 47.6 jit_solution(16170966138768750796)
XLA Ops:
  0.6 3.0 %collective-permute-start = (bf16[48,1024]{1,0:T(8,128)(2,1)}, bf16[48,1024]{1,0:T(8,128)(2,1)S(1)}, u32[]{:S(2)}, u32[]{:S(2)}) collective-permute-start(bf16[48,1024]{1,0:T(8,128)(2,1)} %bitcast.38), channel_id=1, source_target_pairs={{0,16},{16,0},{1,17},{17,1},{2,18},{18,2},{3,19},{19,3},{4,20},{20... | collective-permute-start | bytes 294920 | tf_op jit(solution)/shard_map/ppermute | solution.py:432
  3.7 2.1 %shard_map.145 = (bf16[48,1024]{1,0:T(8,128)(2,1)S(1)}, bf16[512,512]{1,0:T(8,128)(2,1)S(1)}, bf16[192,192]{1,0:T(8,128)(2,1)S(1)}, bf16[512,256]{1,0:T(8,128)(2...) custom-call(bf16[27,48,128]{2,1,0:T(8,128)(2,1)} %bitcast.36, ...), custom_call_target="tpu_custom_call" | custom-call | flops 1000000000 | bytes 1048576 | tf_op jit(solution)/shard_map/pallas_call | solution.py:465
  7.0 1.9 %collective-permute-start.1 = (bf16[48,1024]{1,0:T(8,128)(2,1)S(1)}, bf16[48,1024]{1,0:T(8,128)(2,1)S(1)}, u32[]{:S(2)}, u32[]{:S(2)}) collective-permute-start(bf16[48,1024]{1,0:T(8,128)(2,1)S(1)} %get-tuple-element.50), channel_id=1, source_target_pairs={{1,2},{3,4},{5,6},{7,8},{9,10},{11,12},{13,14},{2,1},{4,3},{6,5},{... | collective-permute-start | bytes 294920 | tf_op jit(solution)/shard_map/ppermute | solution.py:443
  8.8 1.1 %shard_map.147 = (bf16[2,2,144,256]{3,2,1,0:T(8,128)(2,1)S(1)}, f32[2,2,128,256]{3,2,1,0:T(8,128)S(1)}) custom-call(bf16[48,1024]{1,0:T(8,128)(2,1)S(1)} %get-tuple-element.53.earlier, bf16[512,512]{1,0:T(8,128)(2,1)S(1)} %get-tuple-element.51.table.refs_0_, bf16[192,192]{1,0:T(8,128)(2,1)S(1)} %get-tuple-element.54.rows_own, ...), custom_call_target="tpu_custom_call" | custom-call | flops 1000000000 | bytes 1048576 | tf_op jit(solution)/shard_map/pallas_call | solution.py:487
  10.0 1.4 %shard_map.148 = (bf16[2,256,128]{2,1,0:T(8,128)(2,1)S(1)}, bf16[256,256]{1,0:T(8,128)(2,1)S(1)}, f32[1296,128]{1,0:T(8,128)S(1)}, f32[256,256]{1,0:T(8,128)S(1)}, f32[8,128]{1,0:T(8,128)S(1)}) custom-call(bf16[48,1024]{1,0:T(8,128)(2,1)S(1)} %collective-permute-done.2.halo, bf16[512,512]{1,0:T(8,128)(2,1)S(1)} %get-tuple-element.51.table.refs_0_, ...), custom_call_target="tpu_custom_call" | custom-call | flops 1000000000 | bytes 1048576 | tf_op jit(solution)/shard_map/pallas_call | solution.py:500
  11.6 1.5 %shard_map.149 = (f32[296,128]{1,0:T(8,128)S(1)}, f32[3,296,128]{2,1,0:T(8,128)S(1)}, bf16[4,296,128]{2,1,0:T(8,128)(2,1)S(1)}, bf16[2,2,256,128]{3,2,1,0:T(8,128)(2,1)S(1)}, bf16[2,256,256]{2,1,0:T(8,128)(2,1)S(1)}) custom-call(bf16[48,1024]{1,0:T(8,128)(2,1)S(1)} %collective-permute-done.1.halo, bf16[512,512]{1,0:T(8,128)(2,1)S(1)} %get-tuple-element.51.table.refs_0_, ...), custom_call_target="tpu_custom_call" | custom-call | flops 1000000000 | bytes 1048576 | tf_op jit(solution)/shard_map/pallas_call | solution.py:513
  14.2 1.9 %collective-permute-start.15 = (bf16[48,1024]{1,0:T(8,128)(2,1)S(1)}, bf16[48,1024]{1,0:T(8,128)(2,1)S(1)}, u32[]{:S(2)}, u32[]{:S(2)}) collective-permute-start(bf16[48,1024]{1,0:T(8,128)(2,1)S(1)} %get-tuple-element.87), channel_id=1, source_target_pairs={{1,2},{3,4},{5,6},{7,8},{9,10},{11,12},{13,14},{2,1},{4,3},{6,5},{... | collective-permute-start | bytes 294920 | tf_op jit(solution)/shard_map/ppermute | solution.py:443
  16.9 2.2 %shard_map.150 = (bf16[2,1,128,256]{3,2,1,0:T(8,128)(2,1)}, f32[48,1024]{1,0:T(8,128)S(1)}, f32[48,1024]{1,0:T(8,128)S(1)}) custom-call(bf16[2,2,256,128]{3,2,1,0:T(8,128)(2,1)S(1)} %get-tuple-element.69.acts, bf16[2,256,256]{2,1,0:T(8,128)(2,1)S(1)} %get-tuple-element.70.slopes, bf16[432,384]{1,0:T(8,128)(2,1)S(1)} %get-tuple-element.71.backward, ...), custom_call_target="tpu_custom_call" | custom-call | flops 1000000000 | bytes 1048576 | tf_op jit(solution)/shard_map/pallas_call | solution.py:530
  19.1 1.7 %collective-permute-start.4 = (bf16[296,128]{1,0:T(8,128)(2,1)S(1)}, bf16[296,128]{1,0:T(8,128)(2,1)S(1)}, u32[]{:S(2)}, u32[]{:S(2)}) collective-permute-start(bf16[296,128]{1,0:T(8,128)(2,1)S(1)} %get-tuple-element.90), channel_id=1, source_target_pairs={{0,2},{1,5},{2,0},{3,7},{4,6},{5,1},{6,4},{7,3},{8,10},{9,13},{10,... | collective-permute-start | bytes 227336 | tf_op jit(solution)/shard_map/ppermute | solution.py:549
  20.8 1.5 %collective-permute-start.5 = (bf16[296,128]{1,0:T(8,128)(2,1)S(1)}, bf16[296,128]{1,0:T(8,128)(2,1)S(1)}, u32[]{:S(2)}, u32[]{:S(2)}) collective-permute-start(bf16[296,128]{1,0:T(8,128)(2,1)S(1)} %get-tuple-element.92), channel_id=1, source_target_pairs={{0,16},{1,9},{2,18},{3,11},{4,20},{5,13},{6,22},{7,15},{8,24},{9,1... | collective-permute-start | bytes 227336 | tf_op jit(solution)/shard_map/ppermute | solution.py:549
  23.6 1.7 %collective-permute-done.5 = bf16[296,128]{1,0:T(8,128)(2,1)S(1)} collective-permute-done((bf16[296,128]{1,0:T(8,128)(2,1)S(1)}, bf16[296,128]{1,0:T(8,128)(2,1)S(1)}, u32[]{:S(2)}, u32[]{:S(2)}) %collective-permute-start.5) | collective-permute-done | bytes 75808 | tf_op jit(solution)/shard_map/ppermute | solution.py:549
  25.2 2.4 %collective-permute-done.6 = bf16[296,128]{1,0:T(8,128)(2,1)S(1)} collective-permute-done((bf16[296,128]{1,0:T(8,128)(2,1)S(1)}, bf16[296,128]{1,0:T(8,128)(2,1)S(1)}, u32[]{:S(2)}, u32[]{:S(2)}) %collective-permute-start.6) | collective-permute-done | bytes 75808 | tf_op jit(solution)/shard_map/ppermute | solution.py:549
  27.7 1.6 %collective-permute-start.7 = (bf16[296,128]{1,0:T(8,128)(2,1)S(1)}, bf16[296,128]{1,0:T(8,128)(2,1)S(1)}, u32[]{:S(2)}, u32[]{:S(2)}) collective-permute-start(bf16[296,128]{1,0:T(8,128)(2,1)S(1)} %fusion.3), channel_id=1, source_target_pairs={{0,4},{1,3},{2,6},{3,1},{4,0},{5,7},{6,2},{7,5},{8,12},{9,11},{10,... | collective-permute-start | bytes 227336 | tf_op jit(solution)/shard_map/ppermute | solution.py:549
  29.3 1.1 %collective-permute-start.8 = (bf16[296,128]{1,0:T(8,128)(2,1)S(1)}, bf16[296,128]{1,0:T(8,128)(2,1)S(1)}, u32[]{:S(2)}, u32[]{:S(2)}) collective-permute-start(bf16[296,128]{1,0:T(8,128)(2,1)S(1)} %fusion.3), channel_id=1, source_target_pairs={{0,8},{1,17},{2,10},{3,19},{4,12},{5,21},{6,14},{7,23},{8,0},{9,25... | collective-permute-start | bytes 227336 | tf_op jit(solution)/shard_map/ppermute | solution.py:549
  30.4 1.7 %collective-permute-start.9 = (bf16[296,128]{1,0:T(8,128)(2,1)S(1)}, bf16[296,128]{1,0:T(8,128)(2,1)S(1)}, u32[]{:S(2)}, u32[]{:S(2)}) collective-permute-start(bf16[296,128]{1,0:T(8,128)(2,1)S(1)} %fusion.3), channel_id=1, source_target_pairs={{0,12},{1,19},{2,14},{3,17},{4,8},{5,23},{6,10},{7,21},{8,4},{9,27... | collective-permute-start | bytes 227336 | tf_op jit(solution)/shard_map/ppermute | solution.py:549
  32.3 3.2 %collective-permute-done.8 = bf16[296,128]{1,0:T(8,128)(2,1)S(1)} collective-permute-done((bf16[296,128]{1,0:T(8,128)(2,1)S(1)}, bf16[296,128]{1,0:T(8,128)(2,1)S(1)}, u32[]{:S(2)}, u32[]{:S(2)}) %collective-permute-start.8) | collective-permute-done | bytes 75808 | tf_op jit(solution)/shard_map/ppermute | solution.py:549
  35.4 1.3 %collective-permute-done.9 = bf16[296,128]{1,0:T(8,128)(2,1)S(1)} collective-permute-done((bf16[296,128]{1,0:T(8,128)(2,1)S(1)}, bf16[296,128]{1,0:T(8,128)(2,1)S(1)}, u32[]{:S(2)}, u32[]{:S(2)}) %collective-permute-start.9) | collective-permute-done | bytes 75808 | tf_op jit(solution)/shard_map/ppermute | solution.py:549
  36.7 1.2 %collective-permute-start.11 = (bf16[296,128]{1,0:T(8,128)(2,1)S(1)}, bf16[296,128]{1,0:T(8,128)(2,1)S(1)}, u32[]{:S(2)}, u32[]{:S(2)}) collective-permute-start(bf16[296,128]{1,0:T(8,128)(2,1)S(1)} %add_convert_fusion.1.refs_0_), channel_id=1, source_target_pairs={{0,2},{1,5},{2,0},{3,7},{4,6},{5,1},{6,4},{7,3},{8,10},{9,13},{10,... | collective-permute-start | bytes 227336 | tf_op jit(solution)/shard_map/ppermute | solution.py:549
  38.5 1.8 %collective-permute-start.13 = (bf16[296,128]{1,0:T(8,128)(2,1)S(1)}, bf16[296,128]{1,0:T(8,128)(2,1)S(1)}, u32[]{:S(2)}, u32[]{:S(2)}) collective-permute-start(bf16[296,128]{1,0:T(8,128)(2,1)S(1)} %add_convert_fusion.1.refs_0_), channel_id=1, source_target_pairs={{0,18},{1,13},{2,16},{3,15},{4,22},{5,9},{6,20},{7,11},{8,26},{9,5... | collective-permute-start | bytes 227336 | tf_op jit(solution)/shard_map/ppermute | solution.py:549
  41.2 1.2 %collective-permute-done.12.refs_2_ = bf16[296,128]{1,0:T(8,128)(2,1)S(1)} collective-permute-done((bf16[296,128]{1,0:T(8,128)(2,1)S(1)}, bf16[296,128]{1,0:T(8,128)(2,1)S(1)}, u32[]{:S(2)}, u32[]{:S(2)}) %collective-permute-start.12) | collective-permute-done | bytes 75808 | tf_op jit(solution)/shard_map/ppermute | solution.py:549
  42.3 1.5 %collective-permute-done.13.refs_3_ = bf16[296,128]{1,0:T(8,128)(2,1)S(1)} collective-permute-done((bf16[296,128]{1,0:T(8,128)(2,1)S(1)}, bf16[296,128]{1,0:T(8,128)(2,1)S(1)}, u32[]{:S(2)}, u32[]{:S(2)}) %collective-permute-start.13) | collective-permute-done | bytes 75808 | tf_op jit(solution)/shard_map/ppermute | solution.py:549
  43.9 1.1 %collective-permute-done.17 = bf16[6,8,1024]{2,1,0:T(8,128)(2,1)S(1)} collective-permute-done((bf16[6,8,1024]{2,1,0:T(8,128)(2,1)S(1)}, bf16[6,8,1024]{2,1,0:T(8,128)(2,1)S(1)}, u32[]{:S(2)}, u32[]{:S(2)}) %collective-permute-start.17) | collective-permute-done | bytes 98336 | tf_op jit(solution)/shard_map/ppermute | solution.py:432
  45.7 0.9 %shard_map.151 = (f32[1296,128]{1,0:T(8,128)}, f32[1,128]{1,0:T(1,128)}, f32[512,256]{1,0:T(8,128)}, f32[1,256]{1,0:T(1,128)}) custom-call(bf16[296,128]{1,0:T(8,128)(2,1)S(1)} %add_convert_fusion.1.refs_0_, bf16[296,128]{1,0:T(8,128)(2,1)S(1)} %collective-permute-done.11.refs_1_, bf16[296,128]{1,0:T(8,128)(2,1)S(1)} %collective-permute-done.12.refs_2_, ...), custom_call_target="tpu_custom_call" | custom-call | bytes 1048576 | tf_op jit(solution)/shard_map/pallas_call | solution.py:578
  46.7 0.9 %shard_map.152 = (f32[1296,128]{1,0:T(8,128)}, f32[1,128]{1,0:T(1,128)}, f32[512,256]{1,0:T(8,128)}, f32[1,256]{1,0:T(1,128)}) custom-call(bf16[296,128]{1,0:T(8,128)(2,1)S(1)} %collective-permute-done.10.refs_0_, bf16[3,296,128]{2,1,0:T(8,128)(2,1)S(1)} %collective-permute-done.14.refs_1_, ...), custom_call_target="tpu_custom_call", output_to_operand_aliasing={{0}: (2, {}), {1}: (3, {}), {2}: (4, {}), {3}: (5, {})} | custom-call | bytes 1048576 | tf_op jit(solution)/shard_map/pallas_call | solution.py:581
  (32 shorter events, 7.0 us)
Async XLA Ops:
  0.6 6.0 %collective-permute-start = (bf16[48,1024]{1,0:T(8,128)(2,1)}, bf16[48,1024]{1,0:T(8,128)(2,1)S(1)}, u32[]{:S(2)}, u32[]{:S(2)}) collective-permute-start(bf16[48,1024]{1,0:T(8,128)(2,1)} %bitcast.38), channel_id=1, source_target_pairs={{0,16},{16,0},{1,17},{17,1},{2,18},{18,2},{3,19},{19,3},{4,20},{20... | collective-permute-start | bytes 294920 | tf_op jit(solution)/shard_map/ppermute | solution.py:432
  6.9 3.1 %collective-permute-start.2 = (bf16[48,1024]{1,0:T(8,128)(2,1)S(1)}, bf16[48,1024]{1,0:T(8,128)(2,1)S(1)}, u32[]{:S(2)}, u32[]{:S(2)}) collective-permute-start(bf16[48,1024]{1,0:T(8,128)(2,1)S(1)} %get-tuple-element.63), channel_id=1, source_target_pairs={{0,1},{1,0},{2,3},{3,2},{4,5},{5,4},{6,7},{7,6},{8,9},{9,8},{10,11... | collective-permute-start | bytes 294920 | tf_op jit(solution)/shard_map/ppermute | solution.py:435
  7.0 4.7 %collective-permute-start.1 = (bf16[48,1024]{1,0:T(8,128)(2,1)S(1)}, bf16[48,1024]{1,0:T(8,128)(2,1)S(1)}, u32[]{:S(2)}, u32[]{:S(2)}) collective-permute-start(bf16[48,1024]{1,0:T(8,128)(2,1)S(1)} %get-tuple-element.50), channel_id=1, source_target_pairs={{1,2},{3,4},{5,6},{7,8},{9,10},{11,12},{13,14},{2,1},{4,3},{6,5},{... | collective-permute-start | bytes 294920 | tf_op jit(solution)/shard_map/ppermute | solution.py:443
  13.1 5.9 %collective-permute-start.3 = (bf16[4,296,128]{2,1,0:T(8,128)(2,1)S(1)}, bf16[4,296,128]{2,1,0:T(8,128)(2,1)S(1)}, u32[]{:S(2)}, u32[]{:S(2)}) collective-permute-start(bf16[4,296,128]{2,1,0:T(8,128)(2,1)S(1)} %get-tuple-element.76), channel_id=1, source_target_pairs={{0,1},{1,0},{2,3},{3,2},{4,5},{5,4},{6,7},{7,6},{8,9},{9,8},{10,11... | collective-permute-start | bytes 909320 | tf_op jit(solution)/shard_map/ppermute | solution.py:435
  14.2 8.5 %collective-permute-start.15 = (bf16[48,1024]{1,0:T(8,128)(2,1)S(1)}, bf16[48,1024]{1,0:T(8,128)(2,1)S(1)}, u32[]{:S(2)}, u32[]{:S(2)}) collective-permute-start(bf16[48,1024]{1,0:T(8,128)(2,1)S(1)} %get-tuple-element.87), channel_id=1, source_target_pairs={{1,2},{3,4},{5,6},{7,8},{9,10},{11,12},{13,14},{2,1},{4,3},{6,5},{... | collective-permute-start | bytes 294920 | tf_op jit(solution)/shard_map/ppermute | solution.py:443
  16.1 6.6 %collective-permute-start.16 = (bf16[48,1024]{1,0:T(8,128)(2,1)S(1)}, bf16[48,1024]{1,0:T(8,128)(2,1)S(1)}, u32[]{:S(2)}, u32[]{:S(2)}) collective-permute-start(bf16[48,1024]{1,0:T(8,128)(2,1)S(1)} %get-tuple-element.88), channel_id=1, source_target_pairs={{0,1},{1,0},{2,3},{3,2},{4,5},{5,4},{6,7},{7,6},{8,9},{9,8},{10,11... | collective-permute-start | bytes 294920 | tf_op jit(solution)/shard_map/ppermute | solution.py:435
  19.1 4.4 %collective-permute-start.4 = (bf16[296,128]{1,0:T(8,128)(2,1)S(1)}, bf16[296,128]{1,0:T(8,128)(2,1)S(1)}, u32[]{:S(2)}, u32[]{:S(2)}) collective-permute-start(bf16[296,128]{1,0:T(8,128)(2,1)S(1)} %get-tuple-element.90), channel_id=1, source_target_pairs={{0,2},{1,5},{2,0},{3,7},{4,6},{5,1},{6,4},{7,3},{8,10},{9,13},{10,... | collective-permute-start | bytes 227336 | tf_op jit(solution)/shard_map/ppermute | solution.py:549
  20.8 4.4 %collective-permute-start.5 = (bf16[296,128]{1,0:T(8,128)(2,1)S(1)}, bf16[296,128]{1,0:T(8,128)(2,1)S(1)}, u32[]{:S(2)}, u32[]{:S(2)}) collective-permute-start(bf16[296,128]{1,0:T(8,128)(2,1)S(1)} %get-tuple-element.92), channel_id=1, source_target_pairs={{0,16},{1,9},{2,18},{3,11},{4,20},{5,13},{6,22},{7,15},{8,24},{9,1... | collective-permute-start | bytes 227336 | tf_op jit(solution)/shard_map/ppermute | solution.py:549
  22.4 5.3 %collective-permute-start.6 = (bf16[296,128]{1,0:T(8,128)(2,1)S(1)}, bf16[296,128]{1,0:T(8,128)(2,1)S(1)}, u32[]{:S(2)}, u32[]{:S(2)}) collective-permute-start(bf16[296,128]{1,0:T(8,128)(2,1)S(1)} %get-tuple-element.91), channel_id=1, source_target_pairs={{0,18},{1,13},{2,16},{3,15},{4,22},{5,9},{6,20},{7,11},{8,26},{9,5... | collective-permute-start | bytes 227336 | tf_op jit(solution)/shard_map/ppermute | solution.py:549
  27.7 4.6 %collective-permute-start.7 = (bf16[296,128]{1,0:T(8,128)(2,1)S(1)}, bf16[296,128]{1,0:T(8,128)(2,1)S(1)}, u32[]{:S(2)}, u32[]{:S(2)}) collective-permute-start(bf16[296,128]{1,0:T(8,128)(2,1)S(1)} %fusion.3), channel_id=1, source_target_pairs={{0,4},{1,3},{2,6},{3,1},{4,0},{5,7},{6,2},{7,5},{8,12},{9,11},{10,... | collective-permute-start | bytes 227336 | tf_op jit(solution)/shard_map/ppermute | solution.py:549
  29.3 6.1 %collective-permute-start.8 = (bf16[296,128]{1,0:T(8,128)(2,1)S(1)}, bf16[296,128]{1,0:T(8,128)(2,1)S(1)}, u32[]{:S(2)}, u32[]{:S(2)}) collective-permute-start(bf16[296,128]{1,0:T(8,128)(2,1)S(1)} %fusion.3), channel_id=1, source_target_pairs={{0,8},{1,17},{2,10},{3,19},{4,12},{5,21},{6,14},{7,23},{8,0},{9,25... | collective-permute-start | bytes 227336 | tf_op jit(solution)/shard_map/ppermute | solution.py:549
  30.4 6.3 %collective-permute-start.9 = (bf16[296,128]{1,0:T(8,128)(2,1)S(1)}, bf16[296,128]{1,0:T(8,128)(2,1)S(1)}, u32[]{:S(2)}, u32[]{:S(2)}) collective-permute-start(bf16[296,128]{1,0:T(8,128)(2,1)S(1)} %fusion.3), channel_id=1, source_target_pairs={{0,12},{1,19},{2,14},{3,17},{4,8},{5,23},{6,10},{7,21},{8,4},{9,27... | collective-permute-start | bytes 227336 | tf_op jit(solution)/shard_map/ppermute | solution.py:549
  36.7 4.4 %collective-permute-start.11 = (bf16[296,128]{1,0:T(8,128)(2,1)S(1)}, bf16[296,128]{1,0:T(8,128)(2,1)S(1)}, u32[]{:S(2)}, u32[]{:S(2)}) collective-permute-start(bf16[296,128]{1,0:T(8,128)(2,1)S(1)} %add_convert_fusion.1.refs_0_), channel_id=1, source_target_pairs={{0,2},{1,5},{2,0},{3,7},{4,6},{5,1},{6,4},{7,3},{8,10},{9,13},{10,... | collective-permute-start | bytes 227336 | tf_op jit(solution)/shard_map/ppermute | solution.py:549
  38.0 4.4 %collective-permute-start.12 = (bf16[296,128]{1,0:T(8,128)(2,1)S(1)}, bf16[296,128]{1,0:T(8,128)(2,1)S(1)}, u32[]{:S(2)}, u32[]{:S(2)}) collective-permute-start(bf16[296,128]{1,0:T(8,128)(2,1)S(1)} %add_convert_fusion.1.refs_0_), channel_id=1, source_target_pairs={{0,16},{1,9},{2,18},{3,11},{4,20},{5,13},{6,22},{7,15},{8,24},{9,1... | collective-permute-start | bytes 227336 | tf_op jit(solution)/shard_map/ppermute | solution.py:549
  38.5 5.3 %collective-permute-start.13 = (bf16[296,128]{1,0:T(8,128)(2,1)S(1)}, bf16[296,128]{1,0:T(8,128)(2,1)S(1)}, u32[]{:S(2)}, u32[]{:S(2)}) collective-permute-start(bf16[296,128]{1,0:T(8,128)(2,1)S(1)} %add_convert_fusion.1.refs_0_), channel_id=1, source_target_pairs={{0,18},{1,13},{2,16},{3,15},{4,22},{5,9},{6,20},{7,11},{8,26},{9,5... | collective-permute-start | bytes 227336 | tf_op jit(solution)/shard_map/ppermute | solution.py:549
  40.3 4.7 %collective-permute-start.17 = (bf16[6,8,1024]{2,1,0:T(8,128)(2,1)S(1)}, bf16[6,8,1024]{2,1,0:T(8,128)(2,1)S(1)}, u32[]{:S(2)}, u32[]{:S(2)}) collective-permute-start(bf16[6,8,1024]{2,1,0:T(8,128)(2,1)S(1)} %fusion), channel_id=1, source_target_pairs={{0,16},{16,0},{1,17},{17,1},{2,18},{18,2},{3,19},{19,3},{4,20},{20... | collective-permute-start | bytes 294920 | tf_op jit(solution)/shard_map/ppermute | solution.py:432
  41.0 5.6 %collective-permute-start.10 = (bf16[296,128]{1,0:T(8,128)(2,1)S(1)}, bf16[296,128]{1,0:T(8,128)(2,1)S(1)}, u32[]{:S(2)}, u32[]{:S(2)}) collective-permute-start(bf16[296,128]{1,0:T(8,128)(2,1)S(1)} %add_convert_fusion.1.refs_0_), channel_id=1, source_target_pairs={{0,1},{1,0},{2,3},{3,2},{4,5},{5,4},{6,7},{7,6},{8,9},{9,8},{10,11... | collective-permute-start | bytes 227336 | tf_op jit(solution)/shard_map/ppermute | solution.py:435
  43.8 2.8 %collective-permute-start.14 = (bf16[3,296,128]{2,1,0:T(8,128)(2,1)S(1)}, bf16[3,296,128]{2,1,0:T(8,128)(2,1)S(1)}, u32[]{:S(2)}, u32[]{:S(2)}) collective-permute-start(bf16[3,296,128]{2,1,0:T(8,128)(2,1)S(1)} %pad_maximum_fusion), channel_id=1, source_target_pairs={{0,1},{1,0},{2,3},{3,2},{4,5},{5,4},{6,7},{7,6},{8,9},{9,8},{10,11... | collective-permute-start | bytes 681992 | tf_op jit(solution)/shard_map/ppermute | solution.py:435

commit v8 on v7

--- a/solution.py
+++ b/solution.py
@@ -144,7 +144,7 @@
 def first_kernel(dims, count, *refs):
     frames, rows, pair = dims
     sources, targets = refs[:count], refs[count : 2 * count - 1]
-    inside, outside, backward, x, dact, raw, sems = refs[2 * count - 1 :]
+    inside, outside, backward, x, dact, cot_sum, raw, sems = refs[2 * count - 1 :]
     copies = [
         pltpu.make_async_copy(source, target, sems.at[n])
         for n, (source, target) in enumerate(zip(sources, (raw, *targets)))
@@ -170,6 +170,8 @@
     analyse([own[...]], table, [rows_own], x, [where], pair)
     for f in range(frames):
         dact[f] = mm(down_weight[...], cotangent[f, 0], NT)
+    ones = jnp.ones((8, pair), BF16)
+    cot_sum[...] = sum(mm(ones, cotangent[f, 0]) for f in range(frames))
 
 
 def pack_kernel(times, own, came, chosen, inner, outer, earlier):
@@ -262,9 +264,9 @@
 
 
 def main_kernel(dims, heights, halo, *refs):
-    frames, rows, pair = dims
-    _, _, _, _, _, _, _, cotangent = refs[:8]
-    acts_in, slopes_in, conv_in, down_in, total_in, mine, keep, give, acts, slopes, x, packed = refs[8:]
+    _, rows, _ = dims
+    table, rows_halo, x_early, x_own, pre_own, dact, outside, cotangent = refs[:8]
+    cot_sum, acts_in, slopes_in, conv_in, down_in, total_in, mine, keep, give, acts, slopes, x, packed = refs[8:]
     core = lax.axis_index("core")
     halo = (halo[...].astype(F32) * jnp.where(at_end(heights), 0.0, 1.0)).astype(BF16)
     acts[1 - core] = acts_in[...]
@@ -274,8 +276,7 @@
     )
     conv = conv + conv_in[...]
     slope_total = (total + total_in[...])[0:1]
-    ones = jnp.ones((8, pair), BF16)
-    cot_total = sum(mm(ones, cotangent[f, 0]) for f in range(frames))
+    cot_total = cot_sum[...]
 
     chunk = keep.shape[1]
     half = 27 * CH // 2
@@ -471,13 +472,14 @@
             ((9 * CH, 3 * WIDTH), BF16),
             ((frames, rows, TAPS, columns), BF16),
             ((frames, 4 * WIDTH, pair), F32),
+            ((8, width2), F32),
         ],
         [HBM] * len(sources),
         [pltpu.VMEM((27, CH, WIDTH), BF16), pltpu.SemaphoreType.DMA((len(sources),))],
         flops=10**9,
     )(*(pltpu.with_memory_space_constraint(source, pltpu.HBM) for source in sources))
     own, table, rows_own, down_flat, cot, rows_halo, chosen, bias, bias2 = outs[:9]
-    inside, outside, backward, x_own, dact = outs[9:]
+    inside, outside, backward, x_own, dact, cot_sum = outs[9:]
     send_inner, send_outer, earlier = call(
         functools.partial(pack_kernel, times), [(flat_halo, BF16), (flat_halo, BF16), (own.shape, BF16)], [VMEM] * 3
     )(own, came, chosen)
@@ -519,10 +521,10 @@
             ((rows, *acts_shape), BF16),
             ((rows, *slopes_shape), BF16),
         ],
-        [VMEM] * 14,
+        [VMEM] * 15,
         [rows_scratch, pltpu.VMEM((2, 4 * chunk, WIDTH), F32)],
         flops=10**9,
-    )(outer, *common, *inside_parts)
+    )(outer, *common, cot_sum, *inside_parts)
 
     send_inner, send_outer = call(
         functools.partial(edge_kernel, dims), [(flat_halo, BF16), (flat_halo, BF16)], [VMEM] * 4, flops=10**9

time: 47.7 us -> 47.7 us (level)
  no operation moved by 1% of the time
where the time goes in v8:
time: 47.7 us; the launch traced here: 47.6 us
  starting transfers between devices  20.2 us (42%)
  waiting for transfers between devices  14.2 us (30%)
  Pallas kernels  11.2 us (23%)
  other arithmetic  1.02 us (2%)
  between operations  0.78 us (2%)
    ppermute x9, waiting for transfers between devices, cross(): return lax.ppermute(value, names, pairs)  12 us
    ppermute x9, starting transfers between devices, cross(): return lax.ppermute(value, names, pairs)  11.6 us
    ppermute x2, starting transfers between devices, swap_outer(): return lax.ppermute(value, times + heights, pairs)  3.78 us
    ppermute x2, starting transfers between devices, along_tm(): return lax.ppermute(value, times, pairs)  3.75 us
    pallas_call x1, Pallas kernels, local(): call(functools.partial(first_kernel, dims, len(sources)), [(source.shape,...  2.17 us
    pallas_call x1, Pallas kernels, local(): call(functools.partial(late_kernel, dims), [((frames, rows // 2, pair, wi...  2.16 us
    ppermute x2, waiting for transfers between devices, along_tm(): return lax.ppermute(value, times, pairs)  1.92 us
    pallas_call x1, Pallas kernels, local(): call(functools.partial(main_kernel, dims, heights), [((chunk, WIDTH), F32...  1.46 us
  transfers between devices with their start and end apart: 18, of which 11 were waited for; matrix products, arithmetic and copies ran while one was open for 2% of the time, Pallas kernels for 18%

profile of v8, /device:TPU:0, one launch (start us, length us, event | category | flops | bytes accessed | tf_op | source)
XLA Modules:
  0.0 47.6 jit_solution(12381684645787947629)
XLA Ops:
  0.6 3.0 %collective-permute-start = (bf16[48,1024]{1,0:T(8,128)(2,1)}, bf16[48,1024]{1,0:T(8,128)(2,1)S(1)}, u32[]{:S(2)}, u32[]{:S(2)}) collective-permute-start(bf16[48,1024]{1,0:T(8,128)(2,1)} %bitcast.38), channel_id=1, source_target_pairs={{0,16},{16,0},{1,17},{17,1},{2,18},{18,2},{3,19},{19,3},{4,20},{20... | collective-permute-start | bytes 294920 | tf_op jit(solution)/shard_map/ppermute | solution.py:433
  3.7 2.2 %shard_map.145 = (bf16[48,1024]{1,0:T(8,128)(2,1)S(1)}, bf16[512,512]{1,0:T(8,128)(2,1)S(1)}, bf16[192,192]{1,0:T(8,128)(2,1)S(1)}, bf16[512,256]{1,0:T(8,128)(2...) custom-call(bf16[27,48,128]{2,1,0:T(8,128)(2,1)} %bitcast.36, ...), custom_call_target="tpu_custom_call" | custom-call | flops 1000000000 | bytes 1048576 | tf_op jit(solution)/shard_map/pallas_call | solution.py:466
  7.0 1.9 %collective-permute-start.1 = (bf16[48,1024]{1,0:T(8,128)(2,1)S(1)}, bf16[48,1024]{1,0:T(8,128)(2,1)S(1)}, u32[]{:S(2)}, u32[]{:S(2)}) collective-permute-start(bf16[48,1024]{1,0:T(8,128)(2,1)S(1)} %get-tuple-element.51), channel_id=1, source_target_pairs={{1,2},{3,4},{5,6},{7,8},{9,10},{11,12},{13,14},{2,1},{4,3},{6,5},{... | collective-permute-start | bytes 294920 | tf_op jit(solution)/shard_map/ppermute | solution.py:444
  8.8 1.1 %shard_map.147 = (bf16[2,2,144,256]{3,2,1,0:T(8,128)(2,1)S(1)}, f32[2,2,128,256]{3,2,1,0:T(8,128)S(1)}) custom-call(bf16[48,1024]{1,0:T(8,128)(2,1)S(1)} %get-tuple-element.54.earlier, bf16[512,512]{1,0:T(8,128)(2,1)S(1)} %get-tuple-element.52.table.refs_0_, bf16[192,192]{1,0:T(8,128)(2,1)S(1)} %get-tuple-element.55.rows_own, ...), custom_call_target="tpu_custom_call" | custom-call | flops 1000000000 | bytes 1048576 | tf_op jit(solution)/shard_map/pallas_call | solution.py:489
  10.0 1.4 %shard_map.148 = (bf16[2,256,128]{2,1,0:T(8,128)(2,1)S(1)}, bf16[256,256]{1,0:T(8,128)(2,1)S(1)}, f32[1296,128]{1,0:T(8,128)S(1)}, f32[256,256]{1,0:T(8,128)S(1)}, f32[8,128]{1,0:T(8,128)S(1)}) custom-call(bf16[48,1024]{1,0:T(8,128)(2,1)S(1)} %collective-permute-done.2.halo, bf16[512,512]{1,0:T(8,128)(2,1)S(1)} %get-tuple-element.52.table.refs_0_, ...), custom_call_target="tpu_custom_call" | custom-call | flops 1000000000 | bytes 1048576 | tf_op jit(solution)/shard_map/pallas_call | solution.py:502
  11.6 1.5 %shard_map.149 = (f32[296,128]{1,0:T(8,128)S(1)}, f32[3,296,128]{2,1,0:T(8,128)S(1)}, bf16[4,296,128]{2,1,0:T(8,128)(2,1)S(1)}, bf16[2,2,256,128]{3,2,1,0:T(8,128)(2,1)S(1)}, bf16[2,256,256]{2,1,0:T(8,128)(2,1)S(1)}) custom-call(bf16[48,1024]{1,0:T(8,128)(2,1)S(1)} %collective-permute-done.1.halo, bf16[512,512]{1,0:T(8,128)(2,1)S(1)} %get-tuple-element.52.table.refs_0_, ...), custom_call_target="tpu_custom_call" | custom-call | flops 1000000000 | bytes 1048576 | tf_op jit(solution)/shard_map/pallas_call | solution.py:515
  14.2 1.9 %collective-permute-start.15 = (bf16[48,1024]{1,0:T(8,128)(2,1)S(1)}, bf16[48,1024]{1,0:T(8,128)(2,1)S(1)}, u32[]{:S(2)}, u32[]{:S(2)}) collective-permute-start(bf16[48,1024]{1,0:T(8,128)(2,1)S(1)} %get-tuple-element.89), channel_id=1, source_target_pairs={{1,2},{3,4},{5,6},{7,8},{9,10},{11,12},{13,14},{2,1},{4,3},{6,5},{... | collective-permute-start | bytes 294920 | tf_op jit(solution)/shard_map/ppermute | solution.py:444
  16.8 2.2 %shard_map.150 = (bf16[2,1,128,256]{3,2,1,0:T(8,128)(2,1)}, f32[48,1024]{1,0:T(8,128)S(1)}, f32[48,1024]{1,0:T(8,128)S(1)}) custom-call(bf16[2,2,256,128]{3,2,1,0:T(8,128)(2,1)S(1)} %get-tuple-element.71.acts, bf16[2,256,256]{2,1,0:T(8,128)(2,1)S(1)} %get-tuple-element.72.slopes, bf16[432,384]{1,0:T(8,128)(2,1)S(1)} %get-tuple-element.73.backward, ...), custom_call_target="tpu_custom_call" | custom-call | flops 1000000000 | bytes 1048576 | tf_op jit(solution)/shard_map/pallas_call | solution.py:532
  19.1 1.7 %collective-permute-start.4 = (bf16[296,128]{1,0:T(8,128)(2,1)S(1)}, bf16[296,128]{1,0:T(8,128)(2,1)S(1)}, u32[]{:S(2)}, u32[]{:S(2)}) collective-permute-start(bf16[296,128]{1,0:T(8,128)(2,1)S(1)} %get-tuple-element.92), channel_id=1, source_target_pairs={{0,2},{1,5},{2,0},{3,7},{4,6},{5,1},{6,4},{7,3},{8,10},{9,13},{10,... | collective-permute-start | bytes 227336 | tf_op jit(solution)/shard_map/ppermute | solution.py:551
  20.8 1.5 %collective-permute-start.5 = (bf16[296,128]{1,0:T(8,128)(2,1)S(1)}, bf16[296,128]{1,0:T(8,128)(2,1)S(1)}, u32[]{:S(2)}, u32[]{:S(2)}) collective-permute-start(bf16[296,128]{1,0:T(8,128)(2,1)S(1)} %get-tuple-element.94), channel_id=1, source_target_pairs={{0,16},{1,9},{2,18},{3,11},{4,20},{5,13},{6,22},{7,15},{8,24},{9,1... | collective-permute-start | bytes 227336 | tf_op jit(solution)/shard_map/ppermute | solution.py:551
  23.5 1.7 %collective-permute-done.5 = bf16[296,128]{1,0:T(8,128)(2,1)S(1)} collective-permute-done((bf16[296,128]{1,0:T(8,128)(2,1)S(1)}, bf16[296,128]{1,0:T(8,128)(2,1)S(1)}, u32[]{:S(2)}, u32[]{:S(2)}) %collective-permute-start.5) | collective-permute-done | bytes 75808 | tf_op jit(solution)/shard_map/ppermute | solution.py:551
  25.2 2.4 %collective-permute-done.6 = bf16[296,128]{1,0:T(8,128)(2,1)S(1)} collective-permute-done((bf16[296,128]{1,0:T(8,128)(2,1)S(1)}, bf16[296,128]{1,0:T(8,128)(2,1)S(1)}, u32[]{:S(2)}, u32[]{:S(2)}) %collective-permute-start.6) | collective-permute-done | bytes 75808 | tf_op jit(solution)/shard_map/ppermute | solution.py:551
  27.7 1.6 %collective-permute-start.7 = (bf16[296,128]{1,0:T(8,128)(2,1)S(1)}, bf16[296,128]{1,0:T(8,128)(2,1)S(1)}, u32[]{:S(2)}, u32[]{:S(2)}) collective-permute-start(bf16[296,128]{1,0:T(8,128)(2,1)S(1)} %fusion.3), channel_id=1, source_target_pairs={{0,4},{1,3},{2,6},{3,1},{4,0},{5,7},{6,2},{7,5},{8,12},{9,11},{10,... | collective-permute-start | bytes 227336 | tf_op jit(solution)/shard_map/ppermute | solution.py:551
  29.3 1.1 %collective-permute-start.8 = (bf16[296,128]{1,0:T(8,128)(2,1)S(1)}, bf16[296,128]{1,0:T(8,128)(2,1)S(1)}, u32[]{:S(2)}, u32[]{:S(2)}) collective-permute-start(bf16[296,128]{1,0:T(8,128)(2,1)S(1)} %fusion.3), channel_id=1, source_target_pairs={{0,8},{1,17},{2,10},{3,19},{4,12},{5,21},{6,14},{7,23},{8,0},{9,25... | collective-permute-start | bytes 227336 | tf_op jit(solution)/shard_map/ppermute | solution.py:551
  30.4 1.7 %collective-permute-start.9 = (bf16[296,128]{1,0:T(8,128)(2,1)S(1)}, bf16[296,128]{1,0:T(8,128)(2,1)S(1)}, u32[]{:S(2)}, u32[]{:S(2)}) collective-permute-start(bf16[296,128]{1,0:T(8,128)(2,1)S(1)} %fusion.3), channel_id=1, source_target_pairs={{0,12},{1,19},{2,14},{3,17},{4,8},{5,23},{6,10},{7,21},{8,4},{9,27... | collective-permute-start | bytes 227336 | tf_op jit(solution)/shard_map/ppermute | solution.py:551
  32.2 3.2 %collective-permute-done.8 = bf16[296,128]{1,0:T(8,128)(2,1)S(1)} collective-permute-done((bf16[296,128]{1,0:T(8,128)(2,1)S(1)}, bf16[296,128]{1,0:T(8,128)(2,1)S(1)}, u32[]{:S(2)}, u32[]{:S(2)}) %collective-permute-start.8) | collective-permute-done | bytes 75808 | tf_op jit(solution)/shard_map/ppermute | solution.py:551
  35.4 1.3 %collective-permute-done.9 = bf16[296,128]{1,0:T(8,128)(2,1)S(1)} collective-permute-done((bf16[296,128]{1,0:T(8,128)(2,1)S(1)}, bf16[296,128]{1,0:T(8,128)(2,1)S(1)}, u32[]{:S(2)}, u32[]{:S(2)}) %collective-permute-start.9) | collective-permute-done | bytes 75808 | tf_op jit(solution)/shard_map/ppermute | solution.py:551
  36.7 1.2 %collective-permute-start.11 = (bf16[296,128]{1,0:T(8,128)(2,1)S(1)}, bf16[296,128]{1,0:T(8,128)(2,1)S(1)}, u32[]{:S(2)}, u32[]{:S(2)}) collective-permute-start(bf16[296,128]{1,0:T(8,128)(2,1)S(1)} %add_convert_fusion.1.refs_0_), channel_id=1, source_target_pairs={{0,2},{1,5},{2,0},{3,7},{4,6},{5,1},{6,4},{7,3},{8,10},{9,13},{10,... | collective-permute-start | bytes 227336 | tf_op jit(solution)/shard_map/ppermute | solution.py:551
  38.5 1.8 %collective-permute-start.13 = (bf16[296,128]{1,0:T(8,128)(2,1)S(1)}, bf16[296,128]{1,0:T(8,128)(2,1)S(1)}, u32[]{:S(2)}, u32[]{:S(2)}) collective-permute-start(bf16[296,128]{1,0:T(8,128)(2,1)S(1)} %add_convert_fusion.1.refs_0_), channel_id=1, source_target_pairs={{0,18},{1,13},{2,16},{3,15},{4,22},{5,9},{6,20},{7,11},{8,26},{9,5... | collective-permute-start | bytes 227336 | tf_op jit(solution)/shard_map/ppermute | solution.py:551
  41.2 1.2 %collective-permute-done.12.refs_2_ = bf16[296,128]{1,0:T(8,128)(2,1)S(1)} collective-permute-done((bf16[296,128]{1,0:T(8,128)(2,1)S(1)}, bf16[296,128]{1,0:T(8,128)(2,1)S(1)}, u32[]{:S(2)}, u32[]{:S(2)}) %collective-permute-start.12) | collective-permute-done | bytes 75808 | tf_op jit(solution)/shard_map/ppermute | solution.py:551
  42.3 1.5 %collective-permute-done.13.refs_3_ = bf16[296,128]{1,0:T(8,128)(2,1)S(1)} collective-permute-done((bf16[296,128]{1,0:T(8,128)(2,1)S(1)}, bf16[296,128]{1,0:T(8,128)(2,1)S(1)}, u32[]{:S(2)}, u32[]{:S(2)}) %collective-permute-start.13) | collective-permute-done | bytes 75808 | tf_op jit(solution)/shard_map/ppermute | solution.py:551
  43.9 1.1 %collective-permute-done.17 = bf16[6,8,1024]{2,1,0:T(8,128)(2,1)S(1)} collective-permute-done((bf16[6,8,1024]{2,1,0:T(8,128)(2,1)S(1)}, bf16[6,8,1024]{2,1,0:T(8,128)(2,1)S(1)}, u32[]{:S(2)}, u32[]{:S(2)}) %collective-permute-start.17) | collective-permute-done | bytes 98336 | tf_op jit(solution)/shard_map/ppermute | solution.py:433
  45.7 0.9 %shard_map.151 = (f32[1296,128]{1,0:T(8,128)}, f32[1,128]{1,0:T(1,128)}, f32[512,256]{1,0:T(8,128)}, f32[1,256]{1,0:T(1,128)}) custom-call(bf16[296,128]{1,0:T(8,128)(2,1)S(1)} %add_convert_fusion.1.refs_0_, bf16[296,128]{1,0:T(8,128)(2,1)S(1)} %collective-permute-done.11.refs_1_, bf16[296,128]{1,0:T(8,128)(2,1)S(1)} %collective-permute-done.12.refs_2_, ...), custom_call_target="tpu_custom_call" | custom-call | bytes 1048576 | tf_op jit(solution)/shard_map/pallas_call | solution.py:580
  46.6 0.9 %shard_map.152 = (f32[1296,128]{1,0:T(8,128)}, f32[1,128]{1,0:T(1,128)}, f32[512,256]{1,0:T(8,128)}, f32[1,256]{1,0:T(1,128)}) custom-call(bf16[296,128]{1,0:T(8,128)(2,1)S(1)} %collective-permute-done.10.refs_0_, bf16[3,296,128]{2,1,0:T(8,128)(2,1)S(1)} %collective-permute-done.14.refs_1_, ...), custom_call_target="tpu_custom_call", output_to_operand_aliasing={{0}: (2, {}), {1}: (3, {}), {2}: (4, {}), {3}: (5, {})} | custom-call | bytes 1048576 | tf_op jit(solution)/shard_map/pallas_call | solution.py:583
  (32 shorter events, 6.9 us)
Async XLA Ops:
  0.6 6.0 %collective-permute-start = (bf16[48,1024]{1,0:T(8,128)(2,1)}, bf16[48,1024]{1,0:T(8,128)(2,1)S(1)}, u32[]{:S(2)}, u32[]{:S(2)}) collective-permute-start(bf16[48,1024]{1,0:T(8,128)(2,1)} %bitcast.38), channel_id=1, source_target_pairs={{0,16},{16,0},{1,17},{17,1},{2,18},{18,2},{3,19},{19,3},{4,20},{20... | collective-permute-start | bytes 294920 | tf_op jit(solution)/shard_map/ppermute | solution.py:433
  6.9 3.1 %collective-permute-start.2 = (bf16[48,1024]{1,0:T(8,128)(2,1)S(1)}, bf16[48,1024]{1,0:T(8,128)(2,1)S(1)}, u32[]{:S(2)}, u32[]{:S(2)}) collective-permute-start(bf16[48,1024]{1,0:T(8,128)(2,1)S(1)} %get-tuple-element.65), channel_id=1, source_target_pairs={{0,1},{1,0},{2,3},{3,2},{4,5},{5,4},{6,7},{7,6},{8,9},{9,8},{10,11... | collective-permute-start | bytes 294920 | tf_op jit(solution)/shard_map/ppermute | solution.py:436
  7.0 4.7 %collective-permute-start.1 = (bf16[48,1024]{1,0:T(8,128)(2,1)S(1)}, bf16[48,1024]{1,0:T(8,128)(2,1)S(1)}, u32[]{:S(2)}, u32[]{:S(2)}) collective-permute-start(bf16[48,1024]{1,0:T(8,128)(2,1)S(1)} %get-tuple-element.51), channel_id=1, source_target_pairs={{1,2},{3,4},{5,6},{7,8},{9,10},{11,12},{13,14},{2,1},{4,3},{6,5},{... | collective-permute-start | bytes 294920 | tf_op jit(solution)/shard_map/ppermute | solution.py:444
  13.1 5.9 %collective-permute-start.3 = (bf16[4,296,128]{2,1,0:T(8,128)(2,1)S(1)}, bf16[4,296,128]{2,1,0:T(8,128)(2,1)S(1)}, u32[]{:S(2)}, u32[]{:S(2)}) collective-permute-start(bf16[4,296,128]{2,1,0:T(8,128)(2,1)S(1)} %get-tuple-element.78), channel_id=1, source_target_pairs={{0,1},{1,0},{2,3},{3,2},{4,5},{5,4},{6,7},{7,6},{8,9},{9,8},{10,11... | collective-permute-start | bytes 909320 | tf_op jit(solution)/shard_map/ppermute | solution.py:436
  14.2 8.5 %collective-permute-start.15 = (bf16[48,1024]{1,0:T(8,128)(2,1)S(1)}, bf16[48,1024]{1,0:T(8,128)(2,1)S(1)}, u32[]{:S(2)}, u32[]{:S(2)}) collective-permute-start(bf16[48,1024]{1,0:T(8,128)(2,1)S(1)} %get-tuple-element.89), channel_id=1, source_target_pairs={{1,2},{3,4},{5,6},{7,8},{9,10},{11,12},{13,14},{2,1},{4,3},{6,5},{... | collective-permute-start | bytes 294920 | tf_op jit(solution)/shard_map/ppermute | solution.py:444
  16.1 6.6 %collective-permute-start.16 = (bf16[48,1024]{1,0:T(8,128)(2,1)S(1)}, bf16[48,1024]{1,0:T(8,128)(2,1)S(1)}, u32[]{:S(2)}, u32[]{:S(2)}) collective-permute-start(bf16[48,1024]{1,0:T(8,128)(2,1)S(1)} %get-tuple-element.90), channel_id=1, source_target_pairs={{0,1},{1,0},{2,3},{3,2},{4,5},{5,4},{6,7},{7,6},{8,9},{9,8},{10,11... | collective-permute-start | bytes 294920 | tf_op jit(solution)/shard_map/ppermute | solution.py:436
  19.1 4.4 %collective-permute-start.4 = (bf16[296,128]{1,0:T(8,128)(2,1)S(1)}, bf16[296,128]{1,0:T(8,128)(2,1)S(1)}, u32[]{:S(2)}, u32[]{:S(2)}) collective-permute-start(bf16[296,128]{1,0:T(8,128)(2,1)S(1)} %get-tuple-element.92), channel_id=1, source_target_pairs={{0,2},{1,5},{2,0},{3,7},{4,6},{5,1},{6,4},{7,3},{8,10},{9,13},{10,... | collective-permute-start | bytes 227336 | tf_op jit(solution)/shard_map/ppermute | solution.py:551
  20.8 4.4 %collective-permute-start.5 = (bf16[296,128]{1,0:T(8,128)(2,1)S(1)}, bf16[296,128]{1,0:T(8,128)(2,1)S(1)}, u32[]{:S(2)}, u32[]{:S(2)}) collective-permute-start(bf16[296,128]{1,0:T(8,128)(2,1)S(1)} %get-tuple-element.94), channel_id=1, source_target_pairs={{0,16},{1,9},{2,18},{3,11},{4,20},{5,13},{6,22},{7,15},{8,24},{9,1... | collective-permute-start | bytes 227336 | tf_op jit(solution)/shard_map/ppermute | solution.py:551
  22.3 5.3 %collective-permute-start.6 = (bf16[296,128]{1,0:T(8,128)(2,1)S(1)}, bf16[296,128]{1,0:T(8,128)(2,1)S(1)}, u32[]{:S(2)}, u32[]{:S(2)}) collective-permute-start(bf16[296,128]{1,0:T(8,128)(2,1)S(1)} %get-tuple-element.93), channel_id=1, source_target_pairs={{0,18},{1,13},{2,16},{3,15},{4,22},{5,9},{6,20},{7,11},{8,26},{9,5... | collective-permute-start | bytes 227336 | tf_op jit(solution)/shard_map/ppermute | solution.py:551
  27.7 4.6 %collective-permute-start.7 = (bf16[296,128]{1,0:T(8,128)(2,1)S(1)}, bf16[296,128]{1,0:T(8,128)(2,1)S(1)}, u32[]{:S(2)}, u32[]{:S(2)}) collective-permute-start(bf16[296,128]{1,0:T(8,128)(2,1)S(1)} %fusion.3), channel_id=1, source_target_pairs={{0,4},{1,3},{2,6},{3,1},{4,0},{5,7},{6,2},{7,5},{8,12},{9,11},{10,... | collective-permute-start | bytes 227336 | tf_op jit(solution)/shard_map/ppermute | solution.py:551
  29.3 6.1 %collective-permute-start.8 = (bf16[296,128]{1,0:T(8,128)(2,1)S(1)}, bf16[296,128]{1,0:T(8,128)(2,1)S(1)}, u32[]{:S(2)}, u32[]{:S(2)}) collective-permute-start(bf16[296,128]{1,0:T(8,128)(2,1)S(1)} %fusion.3), channel_id=1, source_target_pairs={{0,8},{1,17},{2,10},{3,19},{4,12},{5,21},{6,14},{7,23},{8,0},{9,25... | collective-permute-start | bytes 227336 | tf_op jit(solution)/shard_map/ppermute | solution.py:551
  30.4 6.3 %collective-permute-start.9 = (bf16[296,128]{1,0:T(8,128)(2,1)S(1)}, bf16[296,128]{1,0:T(8,128)(2,1)S(1)}, u32[]{:S(2)}, u32[]{:S(2)}) collective-permute-start(bf16[296,128]{1,0:T(8,128)(2,1)S(1)} %fusion.3), channel_id=1, source_target_pairs={{0,12},{1,19},{2,14},{3,17},{4,8},{5,23},{6,10},{7,21},{8,4},{9,27... | collective-permute-start | bytes 227336 | tf_op jit(solution)/shard_map/ppermute | solution.py:551
  36.7 4.4 %collective-permute-start.11 = (bf16[296,128]{1,0:T(8,128)(2,1)S(1)}, bf16[296,128]{1,0:T(8,128)(2,1)S(1)}, u32[]{:S(2)}, u32[]{:S(2)}) collective-permute-start(bf16[296,128]{1,0:T(8,128)(2,1)S(1)} %add_convert_fusion.1.refs_0_), channel_id=1, source_target_pairs={{0,2},{1,5},{2,0},{3,7},{4,6},{5,1},{6,4},{7,3},{8,10},{9,13},{10,... | collective-permute-start | bytes 227336 | tf_op jit(solution)/shard_map/ppermute | solution.py:551
  37.9 4.4 %collective-permute-start.12 = (bf16[296,128]{1,0:T(8,128)(2,1)S(1)}, bf16[296,128]{1,0:T(8,128)(2,1)S(1)}, u32[]{:S(2)}, u32[]{:S(2)}) collective-permute-start(bf16[296,128]{1,0:T(8,128)(2,1)S(1)} %add_convert_fusion.1.refs_0_), channel_id=1, source_target_pairs={{0,16},{1,9},{2,18},{3,11},{4,20},{5,13},{6,22},{7,15},{8,24},{9,1... | collective-permute-start | bytes 227336 | tf_op jit(solution)/shard_map/ppermute | solution.py:551
  38.5 5.3 %collective-permute-start.13 = (bf16[296,128]{1,0:T(8,128)(2,1)S(1)}, bf16[296,128]{1,0:T(8,128)(2,1)S(1)}, u32[]{:S(2)}, u32[]{:S(2)}) collective-permute-start(bf16[296,128]{1,0:T(8,128)(2,1)S(1)} %add_convert_fusion.1.refs_0_), channel_id=1, source_target_pairs={{0,18},{1,13},{2,16},{3,15},{4,22},{5,9},{6,20},{7,11},{8,26},{9,5... | collective-permute-start | bytes 227336 | tf_op jit(solution)/shard_map/ppermute | solution.py:551
  40.3 4.7 %collective-permute-start.17 = (bf16[6,8,1024]{2,1,0:T(8,128)(2,1)S(1)}, bf16[6,8,1024]{2,1,0:T(8,128)(2,1)S(1)}, u32[]{:S(2)}, u32[]{:S(2)}) collective-permute-start(bf16[6,8,1024]{2,1,0:T(8,128)(2,1)S(1)} %fusion), channel_id=1, source_target_pairs={{0,16},{16,0},{1,17},{17,1},{2,18},{18,2},{3,19},{19,3},{4,20},{20... | collective-permute-start | bytes 294920 | tf_op jit(solution)/shard_map/ppermute | solution.py:433
  41.0 5.6 %collective-permute-start.10 = (bf16[296,128]{1,0:T(8,128)(2,1)S(1)}, bf16[296,128]{1,0:T(8,128)(2,1)S(1)}, u32[]{:S(2)}, u32[]{:S(2)}) collective-permute-start(bf16[296,128]{1,0:T(8,128)(2,1)S(1)} %add_convert_fusion.1.refs_0_), channel_id=1, source_target_pairs={{0,1},{1,0},{2,3},{3,2},{4,5},{5,4},{6,7},{7,6},{8,9},{9,8},{10,11... | collective-permute-start | bytes 227336 | tf_op jit(solution)/shard_map/ppermute | solution.py:436
  43.8 2.8 %collective-permute-start.14 = (bf16[3,296,128]{2,1,0:T(8,128)(2,1)S(1)}, bf16[3,296,128]{2,1,0:T(8,128)(2,1)S(1)}, u32[]{:S(2)}, u32[]{:S(2)}) collective-permute-start(bf16[3,296,128]{2,1,0:T(8,128)(2,1)S(1)} %pad_maximum_fusion), channel_id=1, source_target_pairs={{0,1},{1,0},{2,3},{3,2},{4,5},{5,4},{6,7},{7,6},{8,9},{9,8},{10,11... | collective-permute-start | bytes 681992 | tf_op jit(solution)/shard_map/ppermute | solution.py:436
